TPU v7x, 256 devices: a whole 4x4x8 slice. The times are simulated.
256 devices in a mesh: gx: 8 (over y, core), gy: 4 (over x), gz: 8 (over z).
Axes of the slice: x: 4, y: 4, z: 8, core: 2. Of those that a mesh axis runs over, the one named last changes fastest.
Arguments:
- block_state: bfloat16 [8, 128, 10, 32, 1024], P('gx', ('gy', 'gz')), may hold values from -6 to 6
- block_level: int32 [8, 128], P('gx'), may hold values from 0 to 2, as said below
- block_velocity: bfloat16 [8, 128, 3], P('gx', ('gy', 'gz')), may hold values from -1 to 1
- diffusivity: float32 [10], replicated, may hold values from 0.05 to 0.6
- reaction_matrix: float32 [10, 10], replicated, may hold values from -3 to 3
- ghost_source: int32 [8, 128, 6], P('gx'), may hold values from 0 to 127, as said below
- swap_bit: int32 [8, 4, 8], P('gx', 'gy', 'gz'), may hold values from -1 to 2, as said below
- swap_slot: int32 [8, 4, 8], P('gx', 'gy', 'gz'), may hold values from 0 to 3, as said below
Outputs:
- new_state: bfloat16 [8, 128, 10, 32, 1024], P('gx', ('gy', 'gz'))
Inputs may be any that keep to these rules, and one draw needn't show every extreme that they name: `block_level`: levels are 0, 1 or 2; all blocks of some devices have level 2. `ghost_source`: ghost sources lie in the same gx slab; blocks of a slab are numbered device by device in gy+gz order, 4 a device. Among the 24 ghost faces of the blocks of one device, at most 2 come from the blocks of any one device, and exactly 2 from some device. `swap_bit`: all devices of one (gy, gz) column share the value, so trade partners are paired; -1 means that the column trades no block. `swap_slot`: of two partners, the one whose sum of 2 ** level over its blocks is larger (ties: the lower gx index) names its first block of highest level, the other its first block of lowest level.
All inputs are finite; a program needn't handle non-finite values.
Results may differ from a plain program's by a relative error of at most 0.001.
Values may be sent and summed in bfloat16 or wider, within the bound.
No kernel may reach another device: no remote copies, remote signals or barrier semaphores. Data moves between devices by JAX's collectives and lax.ppermute only.
A program may use at most 128 MiB of HBM per device.

v0:
```python
import jax
import jax.numpy as jnp
from jax import lax
from jax.sharding import PartitionSpec as P

dt_base = 0.05


def swapped(x, axis, bit):
    return lax.ppermute(x, axis, [(i, i ^ 1 << bit) for i in range(lax.axis_size(axis))])


def coarsen_face(layer, cells):
    fields = layer.shape[0]
    square = layer.reshape(fields, cells // 2, 2, cells // 2, 2)
    means = jnp.mean(square, axis=(2, 4))
    return jnp.repeat(jnp.repeat(means, 2, axis=1), 2, axis=2).reshape(fields, cells * cells)


def collect_faces(blocks):
    per_dev, fields, cells, plane = blocks.shape
    pieces = [
        blocks[:, :, 0, :],
        blocks[:, :, -1, :],
        blocks[:, :, :, :cells],
        blocks[:, :, :, plane - cells :],
        blocks[:, :, :, 0::cells],
        blocks[:, :, :, cells - 1 :: cells],
    ]
    return jnp.stack([piece.reshape(per_dev, fields, plane) for piece in pieces], axis=1)


def upwind_term(values, minus, plus, speed):
    return jnp.maximum(speed, 0.0) * (values - minus) + jnp.minimum(speed, 0.0) * (plus - values)


def advance_block(packet, diffusivity, reaction_matrix):
    values, raw_ghosts, coarse_flags, level_here, speeds = packet
    fields, cells, plane = values.shape
    layers = []
    for face_no in range(6):
        layer = raw_ghosts[face_no].astype(jnp.float32)
        layers.append(jnp.where(coarse_flags[face_no] > 0, coarsen_face(layer, cells), layer))
    velocity = speeds.astype(jnp.float32)
    substeps = jnp.left_shift(jnp.int32(1), level_here)
    scale = substeps.astype(jnp.float32)
    step_size = dt_base / scale
    position = lax.broadcasted_iota(jnp.int32, (1, 1, plane), 2) % cells
    low_x = layers[0][:, None, :]
    high_x = layers[1][:, None, :]
    low_y = layers[2].reshape(fields, cells, cells)
    high_y = layers[3].reshape(fields, cells, cells)
    low_z = jnp.repeat(layers[4].reshape(fields, cells, cells), cells, axis=2)
    high_z = jnp.repeat(layers[5].reshape(fields, cells, cells), cells, axis=2)
    rates = diffusivity[:, None, None]

    def substep(index, species_field):
        minus_x = jnp.concatenate([low_x, species_field[:, :-1, :]], axis=1)
        plus_x = jnp.concatenate([species_field[:, 1:, :], high_x], axis=1)
        minus_y = jnp.concatenate([low_y, species_field[:, :, : plane - cells]], axis=2)
        plus_y = jnp.concatenate([species_field[:, :, cells:], high_y], axis=2)
        negative_depth_face = jnp.where(
            position == 0,
            low_z,
            jnp.concatenate([species_field[:, :, :1], species_field[:, :, :-1]], axis=2),
        )
        plus_z = jnp.where(
            position == cells - 1,
            high_z,
            jnp.concatenate([species_field[:, :, 1:], species_field[:, :, -1:]], axis=2),
        )
        diffused_field = (
            minus_x
            + plus_x
            + (minus_y + plus_y)
            + (negative_depth_face + plus_z)
            - 6.0 * species_field
        )
        upwind = (
            upwind_term(species_field, minus_x, plus_x, velocity[0])
            + upwind_term(species_field, minus_y, plus_y, velocity[1])
            + upwind_term(species_field, negative_depth_face, plus_z, velocity[2])
        )
        sender_rank = jnp.einsum(
            "uj,jqi->uqi", reaction_matrix, species_field, precision=lax.Precision.HIGHEST
        )
        change = rates * diffused_field * (scale * scale) - upwind * scale + sender_rank
        return species_field + step_size * change

    result = lax.fori_loop(jnp.int32(0), substeps, substep, values.astype(jnp.float32))
    return result.astype(jnp.bfloat16)


def plan_sends(faces, wanted, my_index, per_dev, peers):
    requests = per_dev * 6
    fields, plane = (faces.shape[2], faces.shape[3])
    capacity = 2 * max(1, requests // peers)
    opposite = jnp.bitwise_xor(jnp.arange(requests, dtype=jnp.int32) % 6, 1)
    source_dev = wanted // per_dev
    source_face = wanted % per_dev * 6 + opposite[None, :]
    earlier = jnp.arange(requests)[None, :] < jnp.arange(requests)[:, None]
    same_source = source_dev[:, :, None] == source_dev[:, None, :]
    ranking = jnp.sum(same_source & earlier[None], axis=2)
    slot_ids = jnp.arange(capacity, dtype=jnp.int32)
    matches = (source_dev == my_index)[:, None, :] & (
        ranking[:, None, :] == slot_ids[None, :, None]
    )
    selected_blocks = jnp.sum(jnp.where(matches, source_face[:, None, :], 0), axis=2)
    filled = jnp.any(matches, axis=2)
    flat_faces = faces.reshape(requests, fields, plane)
    outgoing = jnp.where(
        filled[:, :, None, None],
        jnp.take(flat_faces, selected_blocks, axis=0),
        jnp.zeros((), jnp.bfloat16),
    )
    my_sources = lax.dynamic_slice_in_dim(source_dev, my_index, 1, 0)[0]
    my_ranks = lax.dynamic_slice_in_dim(ranking, my_index, 1, 0)[0]
    lookup = my_sources * capacity + my_ranks
    return (outgoing, lookup, capacity)


def local(
    block_state,
    block_level,
    block_velocity,
    diffusivity,
    reaction_matrix,
    ghost_source,
    swap_bit,
    swap_slot,
):
    blocks = block_state[0]
    per_dev, fields, cells, plane = blocks.shape
    peers = lax.axis_size(("gy", "gz"))
    my_index = lax.axis_index(("gy", "gz"))
    levels = block_level[0]
    requests = per_dev * 6
    wanted = ghost_source[0].reshape(peers, requests)
    mine = lax.dynamic_slice_in_dim(wanted, my_index, 1, 0)[0]
    faces = collect_faces(blocks)
    outgoing, lookup, capacity = plan_sends(faces, wanted, my_index, per_dev, peers)
    arrived = lax.all_to_all(outgoing, ("gy", "gz"), split_axis=0, concat_axis=0, tiled=True)
    raw_ghosts = jnp.take(arrived.reshape(peers * capacity, fields, plane), lookup, axis=0)
    raw_ghosts = raw_ghosts.reshape(per_dev, 6, fields, plane)
    own_levels = lax.dynamic_slice_in_dim(levels, my_index * per_dev, per_dev, 0)
    coarse_flags = (jnp.take(levels, mine).reshape(per_dev, 6) != own_levels[:, None]).astype(
        jnp.int32
    )
    speeds = block_velocity[0]
    bit_here = swap_bit[0, 0, 0]
    slot_here = swap_slot[0, 0, 0]
    bit_count = lax.axis_size("gx").bit_length() - 1
    fresh = lax.map(
        lambda packet: advance_block(packet, diffusivity, reaction_matrix),
        (blocks, raw_ghosts, coarse_flags, own_levels, speeds),
    )
    departing_blocks = lax.dynamic_index_in_dim(fresh, slot_here, 0, keepdims=False)
    coming = departing_blocks
    for bit_no in range(bit_count):
        partner_block = swapped(departing_blocks, "gx", bit_no)
        coming = jnp.where(bit_here == bit_no, partner_block, coming)
    result = lax.dynamic_update_index_in_dim(fresh, coming, slot_here, 0)
    return result[None]


def solution(mesh):
    in_specs = (
        P("gx", ("gy", "gz"), None, None, None),
        P("gx", None),
        P("gx", ("gy", "gz"), None),
        P(),
        P(),
        P("gx", None, None),
        P("gx", "gy", "gz"),
        P("gx", "gy", "gz"),
    )
    out_specs = P("gx", ("gy", "gz"), None, None, None)
    return jax.shard_map(local, mesh=mesh, in_specs=in_specs, out_specs=out_specs, check_vma=False)
```

profile of v0, /device:TPU:32, one launch (start us, length us, event | category | flops | bytes accessed | tf_op | source)
XLA Modules:
  0.0 828.6 jit_solution(16291415789504661971)
XLA Ops:
  4.8 12.9 %slice.173 = bf16[4,10,32,32]{3,0,1,2:T(4,128)(2,1)} slice(bf16[4,10,32,1024]{3,0,1,2:T(4,128)(2,1)S(1)} %bitcast.219), slice={[0:4:1], [0:10:1], [0:32:1], [0:1024:32]} | slice | bytes 163840 | tf_op jit(solution)/shard_map/slice | solution.py:27
  17.7 12.9 %slice.174 = bf16[4,10,32,32]{3,0,1,2:T(4,128)(2,1)} slice(bf16[4,10,32,1024]{3,0,1,2:T(4,128)(2,1)S(1)} %bitcast.220), slice={[0:4:1], [0:10:1], [0:32:1], [31:1024:32]} | slice | bytes 163840 | tf_op jit(solution)/shard_map/slice | solution.py:28
  50.6 11.2 %all-to-all-start = ((bf16[32,2,10,1024]{3,1,2,0:T(2,128)(2,1)}), bf16[32,2,10,1024]{3,1,2,0:T(2,128)(2,1)}, u32[]{:S(2)}, u32[]{:S(2)}) async-start(bf16[32,2,10,1024]{3,1,2,0:T(2,128)(2,1)} %broadcast_select_fusion.6), calls=%async_computation | async-start | bytes 2621440 | tf_op jit(solution)/shard_map/all_to_all | solution.py:142
  68.4 27.4 %all-to-all-done = bf16[32,2,10,1024]{3,1,2,0:T(2,128)(2,1)} async-done(((bf16[32,2,10,1024]{3,1,2,0:T(2,128)(2,1)}), bf16[32,2,10,1024]{3,1,2,0:T(2,128)(2,1)}, u32[]{:S(2)}, u32[]{:S(2)}) %all-to-all-start) | async-done | bytes 1310752 | tf_op jit(solution)/shard_map/all_to_all | solution.py:142
  109.1 685.1 %while.34 = (s32[]{:T(128)}, bf16[4,10,32,1024]{3,1,2,0:T(8,128)(2,1)}, bf16[4,10,32,1024]{3,1,2,0:T(8,128)(2,1)}, s32[4]{0:T(128)S(1)}, s32[4,6]{1,0:T(4,128)S(...) while((s32[]{:T(128)}, ...), condition=%wide.region_12.13_spmd, body=%wide.region_3.12_spmd.sunk | while | flops 52975640 | bytes 63364548 | solution.py:153
  138.3 139.3 %while.35 = (s32[]{:T(128)}, f32[10,32,1024]{2,0,1:T(8,128)}, s32[]{:T(128)}, f32[]{:T(128)}, f32[10,1,1]{0,2,1:T(1,128)S(1)}, /*index=5*/f32[10,1,1024]{2,0,1:T...) while((s32[]{:T(128)}, f32[10,32,1024]{2,0,1:T(8,128)}, ...), condition=%wide.region_11.11_spmd.clone.clone, body=%wide.region_10.10_spmd.clone.clone.sunk | while | flops 52115456 | bytes 55138744 | solution.py:90
  166.1 7.0 multiply_add_fusion.2
  200.9 7.0 multiply_add_fusion.2
  235.8 7.0 multiply_add_fusion.2
  270.6 7.0 multiply_add_fusion.2
  309.6 139.3 %while.35 = (s32[]{:T(128)}, f32[10,32,1024]{2,0,1:T(8,128)}, s32[]{:T(128)}, f32[]{:T(128)}, f32[10,1,1]{0,2,1:T(1,128)S(1)}, /*index=5*/f32[10,1,1024]{2,0,1:T...) while((s32[]{:T(128)}, f32[10,32,1024]{2,0,1:T(8,128)}, ...), condition=%wide.region_11.11_spmd.clone.clone, body=%wide.region_10.10_spmd.clone.clone.sunk | while | flops 52115456 | bytes 55138744 | solution.py:90
  372.2 7.0 multiply_add_fusion.2
  407.0 7.0 multiply_add_fusion.2
  441.8 7.0 multiply_add_fusion.2
  480.9 139.3 %while.35 = (s32[]{:T(128)}, f32[10,32,1024]{2,0,1:T(8,128)}, s32[]{:T(128)}, f32[]{:T(128)}, f32[10,1,1]{0,2,1:T(1,128)S(1)}, /*index=5*/f32[10,1,1024]{2,0,1:T...) while((s32[]{:T(128)}, f32[10,32,1024]{2,0,1:T(8,128)}, ...), condition=%wide.region_11.11_spmd.clone.clone, body=%wide.region_10.10_spmd.clone.clone.sunk | while | flops 52115456 | bytes 55138744 | solution.py:90
  508.7 7.0 multiply_add_fusion.2
  543.5 7.0 multiply_add_fusion.2
  578.3 7.0 multiply_add_fusion.2
  613.1 7.0 multiply_add_fusion.2
  652.2 139.3 %while.35 = (s32[]{:T(128)}, f32[10,32,1024]{2,0,1:T(8,128)}, s32[]{:T(128)}, f32[]{:T(128)}, f32[10,1,1]{0,2,1:T(1,128)S(1)}, /*index=5*/f32[10,1,1024]{2,0,1:T...) while((s32[]{:T(128)}, f32[10,32,1024]{2,0,1:T(8,128)}, ...), condition=%wide.region_11.11_spmd.clone.clone, body=%wide.region_10.10_spmd.clone.clone.sunk | while | flops 52115456 | bytes 55138744 | solution.py:90
  680.0 7.0 multiply_add_fusion.2
  749.6 7.0 multiply_add_fusion.2
  805.7 9.5 %collective-permute-done = bf16[10,32,1024]{2,1,0:T(8,128)(2,1)S(1)} collective-permute-done((bf16[10,32,1024]{2,1,0:T(8,128)(2,1)S(1)}, bf16[10,32,1024]{2,1,0:T(8,128)(2,1)S(1)}, u32[]{:S(2)}, u32[]{:S(2)}) %collective-permute-start) | collective-permute-done | bytes 655392 | tf_op jit(solution)/shard_map/ppermute | solution.py:10
  815.2 11.8 %collective-permute-done.1 = bf16[10,32,1024]{2,1,0:T(8,128)(2,1)S(1)} collective-permute-done((bf16[10,32,1024]{2,1,0:T(8,128)(2,1)S(1)}, bf16[10,32,1024]{2,1,0:T(8,128)(2,1)S(1)}, u32[]{:S(2)}, u32[]{:S(2)}) %collective-permute-start.1) | collective-permute-done | bytes 655392 | tf_op jit(solution)/shard_map/ppermute | solution.py:10
  (741 shorter events, 614.6 us)
Async XLA Ops:
  0.0 66.4 %copy-start = (s32[1,128]{1,0:T(1,128)S(1)}, s32[1,128]{1,0:T(1,128)}, u32[]{:S(2)}) copy-start(s32[1,128]{1,0:T(1,128)} %param.13) | copy-start | bytes 1540
  3.8 26.9 %copy-start.12 = (s32[1,128,6]{1,0,2:T(1,128)S(1)}, s32[1,128,6]{1,0,2:T(1,128)}, u32[]{:S(2)}) copy-start(s32[1,128,6]{1,0,2:T(1,128)} %param.17) | copy-start | bytes 9220
  34.1 4.9 copy-start.9
  50.6 45.2 %all-to-all-start = ((bf16[32,2,10,1024]{3,1,2,0:T(2,128)(2,1)}), bf16[32,2,10,1024]{3,1,2,0:T(2,128)(2,1)}, u32[]{:S(2)}, u32[]{:S(2)}) async-start(bf16[32,2,10,1024]{3,1,2,0:T(2,128)(2,1)} %broadcast_select_fusion.6), calls=%async_computation | async-start | bytes 2621440 | tf_op jit(solution)/shard_map/all_to_all | solution.py:142
  102.9 6.1 copy-start.14
  102.9 6.1 copy-start.15
  134.7 3.6 copy-start.16
  163.4 2.8 copy-start.8
  198.2 2.8 copy-start.8
  233.0 2.8 copy-start.8
  267.8 2.8 copy-start.8
  306.0 3.6 copy-start.16
  334.6 2.8 copy-start.8
  369.4 2.8 copy-start.8
  404.3 2.8 copy-start.8
  439.1 2.8 copy-start.8
  477.3 3.6 copy-start.16
  505.9 2.8 copy-start.8
  540.7 2.8 copy-start.8
  648.6 3.6 copy-start.16
  795.9 19.3 %collective-permute-start = (bf16[10,32,1024]{2,1,0:T(8,128)(2,1)S(1)}, bf16[10,32,1024]{2,1,0:T(8,128)(2,1)S(1)}, u32[]{:S(2)}, u32[]{:S(2)}) collective-permute-start(bf16[10,32,1024]{2,1,0:T(8,128)(2,1)S(1)} %bitcast.236), channel_id=1, source_target_pairs={{0,128},{32,160},{64,192},{96,224},{128,0},{160,32},{192,64},{224,... | collective-permute-start | bytes 1966088 | tf_op jit(solution)/shard_map/ppermute | solution.py:10
  799.2 27.8 %collective-permute-start.1 = (bf16[10,32,1024]{2,1,0:T(8,128)(2,1)S(1)}, bf16[10,32,1024]{2,1,0:T(8,128)(2,1)S(1)}, u32[]{:S(2)}, u32[]{:S(2)}) collective-permute-start(bf16[10,32,1024]{2,1,0:T(8,128)(2,1)S(1)} %bitcast.237), channel_id=1, source_target_pairs={{0,64},{32,96},{64,0},{96,32},{128,192},{160,224},{192,128},{224,1... | collective-permute-start | bytes 1966088 | tf_op jit(solution)/shard_map/ppermute | solution.py:10
  799.9 27.1 %collective-permute-start.2 = (bf16[10,32,1024]{2,1,0:T(8,128)(2,1)S(1)}, bf16[10,32,1024]{2,1,0:T(8,128)(2,1)S(1)}, u32[]{:S(2)}, u32[]{:S(2)}) collective-permute-start(bf16[10,32,1024]{2,1,0:T(8,128)(2,1)S(1)} %bitcast.238), channel_id=1, source_target_pairs={{0,32},{32,0},{64,96},{96,64},{128,160},{160,128},{192,224},{224,1... | collective-permute-start | bytes 1966088 | tf_op jit(solution)/shard_map/ppermute | solution.py:10
  800.6 28.1 %copy-start.1 = (s32[1,128]{1,0:T(1,128)S(1)}, s32[1,128]{1,0:T(1,128)}, u32[]{:S(2)}) copy-start(s32[1,128]{1,0:T(1,128)} %param.13) | copy-start | bytes 1540
  (120 other events, 293.9 us)
where the time goes:
time: 833 us; the launch traced here: 829 us
  local copies, waits for them, and re-layouts  552 us (66%)
  matrix products  113 us (14%)
  other arithmetic  63.2 us (8%)
  waiting for transfers between devices  48.6 us (6%)
  loops' own time  35.3 us (4%)
  starting transfers between devices  15.2 us (2%)
    dot_general x16, matrix products, substep(): jnp.einsum('uj,jqi->uqi', reaction_matrix, species_field, precision=lax.P...  113 us
    reshape x16, local copies, waits for them, and re-layouts, advance_block(): low_z = jnp.repeat(layers[4].reshape(fields, cells, cells), cells, axis=2)  86.5 us
    while x304, local copies, waits for them, and re-layouts  83.3 us
    reshape x16, local copies, waits for them, and re-layouts, advance_block(): high_z = jnp.repeat(layers[5].reshape(fields, cells, cells), cells, axis=2)  73.4 us
    broadcast_in_dim x16, local copies, waits for them, and re-layouts, advance_block(): low_z = jnp.repeat(layers[4].reshape(fields, cells, cells), cells, axis=2)  71.7 us
    broadcast_in_dim x16, local copies, waits for them, and re-layouts, advance_block(): high_z = jnp.repeat(layers[5].reshape(fields, cells, cells), cells, axis=2)  71.4 us
    slice x16, local copies, waits for them, and re-layouts, substep(): species_field[:, :, :-1]  44.4 us
    another operation x1, loops' own time, local(): lax.map(lambda packet: advance_block(packet, diffusivity, reaction_matrix...  33.7 us
  transfers between devices with their start and end apart: 4, of which 3 were waited for; matrix products, arithmetic and copies ran while one was open for 1% of the time, Pallas kernels for 0%

commit v1 on v0

v1 whole, which is shorter than its diff:
```python
import functools

import jax
import jax.numpy as jnp
from jax import lax
from jax.experimental import pallas as pl
from jax.experimental.pallas import tpu as pltpu
from jax.sharding import PartitionSpec as P

f32 = jnp.float32
bf16 = jnp.bfloat16
dt_base = 0.05
LANES = 128
ROWS = 8
PAD = 8


def swapped(x, axis, bit):
    return lax.ppermute(x, axis, [(i, i ^ 1 << bit) for i in range(lax.axis_size(axis))])


def lane_roll(x, shift):
    shift = shift % LANES
    return x if shift == 0 else pltpu.roll(x, shift, x.ndim - 1)


def pack_kernel(send_ref, u_ref, o_ref, sel_ref, face_ref):
    blk = pl.program_id(0)
    _, fields, cells, plane = u_ref.shape
    groups = LANES // cells
    tiles = plane // LANES

    @pl.when(blk == 0)
    def _():
        row = lax.broadcasted_iota(jnp.int32, sel_ref.shape, 0)
        col = lax.broadcasted_iota(jnp.int32, sel_ref.shape, 1)
        high = col // LANES
        within = col % LANES
        t = within % cells
        jj = within // cells
        source = (groups * t + jj) * cells + high * (cells - 1)
        sel_ref[...] = jnp.where((t < tiles) & (row == source), 1.0, 0.0).astype(bf16)

    lane = lax.broadcasted_iota(jnp.int32, (1, ROWS, LANES), 2)

    def put(face_no, value):
        face_ref[blk * 6 + face_no] = value.reshape(fields * ROWS, LANES).astype(bf16)

    for face_no, edge in ((0, 0), (1, cells - 1)):
        pieces = [
            u_ref[0, :, edge : edge + 1, pl.ds(LANES * t, LANES)].astype(f32)
            for t in range(tiles)
        ]
        put(face_no, jnp.concatenate(pieces, axis=1))
    for face_no, tile, group in ((2, 0, 0), (3, tiles - 1, groups - 1)):
        strip = u_ref[0, :, :, pl.ds(LANES * tile, LANES)].astype(f32)
        total = jnp.zeros((fields, ROWS, LANES), f32)
        for b in range(groups):
            moved = lane_roll(strip[:, ROWS * b : ROWS * b + ROWS], cells * (b - group))
            total = jnp.where(lane // cells == b, moved, total)
        put(face_no, total)
    picked = jnp.dot(
        u_ref[0].reshape(fields * cells, plane), sel_ref[...], preferred_element_type=f32
    ).reshape(fields, cells, 2 * LANES)
    for face_no, high in ((4, 0), (5, 1)):
        total = jnp.zeros((fields, ROWS, LANES), f32)
        for b in range(groups):
            part = picked[:, ROWS * b : ROWS * b + ROWS, LANES * high : LANES * high + LANES]
            total = total + lane_roll(part, tiles * b)
        put(face_no, total)

    @pl.when(blk == pl.num_programs(0) - 1)
    def _():
        def copy(slot, carry):
            o_ref[slot] = face_ref[send_ref[slot]]
            return carry

        lax.fori_loop(0, o_ref.shape[0], copy, 0)


def pack_faces(blocks, send, slots):
    per_dev, fields, cells, plane = blocks.shape
    return pl.pallas_call(
        pack_kernel,
        grid_spec=pltpu.PrefetchScalarGridSpec(
            num_scalar_prefetch=1,
            grid=(per_dev,),
            in_specs=[pl.BlockSpec((1, fields, cells, plane), lambda b, s: (b, 0, 0, 0))],
            out_specs=pl.BlockSpec((slots, fields * ROWS, LANES), lambda b, s: (0, 0, 0)),
            scratch_shapes=[
                pltpu.VMEM((plane, 2 * LANES), bf16),
                pltpu.VMEM((per_dev * 6, fields * ROWS, LANES), bf16),
            ],
        ),
        out_shape=jax.ShapeDtypeStruct((slots, fields * ROWS, LANES), bf16),
        compiler_params=pltpu.CompilerParams(vmem_limit_bytes=32 << 20),
        name="pack_faces",
    )(send, blocks)


def advance_kernel(first, per_dev, ints_ref, vals_ref, u_ref, arr_ref, o_ref, sa_ref, sb_ref, e_ref, rk_ref):
    _, fields, cells, plane = u_ref.shape
    groups = LANES // cells
    tiles = plane // LANES
    blk = ints_ref[pl.program_id(0) + first]
    level = ints_ref[per_dev + blk]
    lookup = lambda q: ints_ref[2 * per_dev + q]
    coarse = lambda q: ints_ref[2 * per_dev + 6 * per_dev + q]
    velocity = [vals_ref[blk * 3 + d] for d in range(3)]
    diffusivity = lambda f: vals_ref[3 * per_dev + f]
    reaction = lambda f, e: vals_ref[3 * per_dev + fields + f * fields + e]

    n = jnp.left_shift(jnp.int32(1), level)
    scale = n.astype(f32)
    dt = dt_base / scale
    lane = lax.broadcasted_iota(jnp.int32, (ROWS, LANES), 1)
    sub = lax.broadcasted_iota(jnp.int32, (ROWS, LANES), 0)
    k_first = lane % cells == 0
    k_last = lane % cells == cells - 1

    for t in range(tiles):
        for half in range(cells // 16):
            sa_ref[:, t + 1, pl.ds(PAD + 16 * half, 16), :] = u_ref[
                0, :, pl.ds(16 * half, 16), pl.ds(LANES * t, LANES)
            ].astype(f32)

    def pair_lanes(x, step):
        even = ((lane // step) % 2 == 0)[None]
        return x + jnp.where(even, lane_roll(x, -step), lane_roll(x, step))

    def pair_rows(x):
        even = (sub % 2 == 0)[None]
        return x + jnp.where(even, pltpu.roll(x, ROWS - 1, 1), pltpu.roll(x, 1, 1))

    def face(face_no, pair_a, pair_b):
        q = blk * 6 + face_no
        layer = arr_ref[lookup(q)].astype(f32).reshape(fields, ROWS, LANES)
        return jnp.where(coarse(q) > 0, pair_b(pair_a(layer)) * 0.25, layer)

    by_cells = lambda x: pair_lanes(x, cells)
    by_one = lambda x: pair_lanes(x, 1)
    states = (sa_ref, sb_ref)
    low, high = face(0, by_cells, by_one), face(1, by_cells, by_one)
    for state in states:
        for t in range(tiles):
            state[:, t + 1, PAD - 1 : PAD, :] = low[:, t : t + 1, :]
            state[:, t + 1, PAD + cells : PAD + cells + 1, :] = high[:, t : t + 1, :]
    low, high = face(2, by_one, pair_rows), face(3, by_one, pair_rows)
    for b in range(groups):
        low_b = lane_roll(low, cells * (groups - 1 - b))
        high_b = lane_roll(high, -cells * b)
        for state in states:
            state[:, 0, pl.ds(PAD + ROWS * b, ROWS), :] = low_b
            state[:, tiles + 1, pl.ds(PAD + ROWS * b, ROWS), :] = high_b
    low, high = face(4, by_cells, pair_rows), face(5, by_cells, pair_rows)
    for b in range(groups):
        for t in range(tiles):
            at = tiles * b + t
            e_ref[:, t, pl.ds(ROWS * b, ROWS), :] = jnp.where(
                k_first[None], lane_roll(low, -at), lane_roll(high, cells - 1 - at)
            )

    adv = dt * scale
    dif = dt * scale * scale
    minus = [adv * jnp.maximum(v, 0.0) for v in velocity]
    plus = [-(adv * jnp.minimum(v, 0.0)) for v in velocity]
    outflow = sum(minus) + sum(plus)
    rates = [dif * diffusivity(f) for f in range(fields)]

    size = fields * ROWS
    ri = lax.broadcasted_iota(jnp.int32, (size, size), 0)
    ci = lax.broadcasted_iota(jnp.int32, (size, size), 1)
    matrix = jnp.zeros((size, size), f32)
    for f in range(fields):
        line = jnp.zeros((size, size), f32)
        for e in range(fields):
            term = dt * reaction(f, e)
            if e == f:
                term = term - (6.0 * rates[f] + outflow)
            line = jnp.where(ci // ROWS == e, term, line)
        matrix = jnp.where(ri // ROWS == f, line, matrix)
    matrix = jnp.where(ri % ROWS == ci % ROWS, matrix, 0.0)
    matrix_high = matrix.astype(bf16)
    rk_ref[:, 0:size] = matrix_high
    rk_ref[:, size : 2 * size] = (matrix - matrix_high.astype(f32)).astype(bf16)
    rk_ref[:, 2 * size : 3 * size] = matrix_high

    def substep(src, dst):
        own = rk_ref[...]

        def two_tiles(pair, carry):
            for it in range(cells // ROWS):
                row = PAD + ROWS * it
                centre = [
                    [src[f, 2 * pair + 1 + q, pl.ds(row, ROWS), :] for f in range(fields)]
                    for q in range(2)
                ]
                both = jnp.concatenate([jnp.concatenate(c, axis=0) for c in centre], axis=1)
                both_high = both.astype(bf16)
                both_low = (both - both_high.astype(f32)).astype(bf16)
                stacked = jnp.concatenate([both_high, both_high, both_low], axis=0)
                mixed = jnp.dot(own, stacked, preferred_element_type=f32)
                for q in range(2):
                    t = 2 * pair + q
                    for f in range(fields):
                        c = centre[q][f]
                        minus_x = src[f, t + 1, pl.ds(row - 1, ROWS), :]
                        plus_x = src[f, t + 1, pl.ds(row + 1, ROWS), :]
                        left = src[f, t, pl.ds(row, ROWS), :]
                        right = src[f, t + 2, pl.ds(row, ROWS), :]
                        edge = e_ref[f, t, pl.ds(ROWS * it, ROWS), :]
                        minus_y = lane_roll(jnp.where(lane >= LANES - cells, left, c), cells)
                        plus_y = lane_roll(jnp.where(lane < cells, right, c), -cells)
                        minus_z = jnp.where(k_first, edge, lane_roll(c, 1))
                        plus_z = jnp.where(k_last, edge, lane_roll(c, -1))
                        near = (rates[f] + minus[0]) * minus_x + (rates[f] + plus[0]) * plus_x
                        near += (rates[f] + minus[1]) * minus_y + (rates[f] + plus[1]) * plus_y
                        near += (rates[f] + minus[2]) * minus_z + (rates[f] + plus[2]) * plus_z
                        own_terms = mixed[ROWS * f : ROWS * f + ROWS, LANES * q : LANES * q + LANES]
                        dst[f, t + 1, pl.ds(row, ROWS), :] = near + (c + own_terms)
            return carry

        lax.fori_loop(0, tiles // 2, two_tiles, 0)

    def finish(src):
        for t in range(tiles):
            for half in range(cells // 16):
                o_ref[0, :, pl.ds(16 * half, 16), pl.ds(LANES * t, LANES)] = src[
                    :, t + 1, pl.ds(PAD + 16 * half, 16), :
                ].astype(bf16)

    @pl.when(n == 1)
    def _():
        substep(sa_ref, sb_ref)
        finish(sb_ref)

    @pl.when(n > 1)
    def _():
        def two(i, carry):
            substep(sa_ref, sb_ref)
            substep(sb_ref, sa_ref)
            return carry

        lax.fori_loop(0, n // 2, two, 0)
        finish(sa_ref)


def advance(ints, vals, blocks, arrived, first, count, slots_out):
    per_dev, fields, cells, plane = blocks.shape
    tiles = plane // LANES
    shape = (1, fields, cells, plane)
    if slots_out == 1:
        out_map = lambda b, i, v: (0, 0, 0, 0)
    else:
        out_map = lambda b, i, v: (i[b + first], 0, 0, 0)
    return pl.pallas_call(
        functools.partial(advance_kernel, first, per_dev),
        grid_spec=pltpu.PrefetchScalarGridSpec(
            num_scalar_prefetch=2,
            grid=(count,),
            in_specs=[
                pl.BlockSpec(shape, lambda b, i, v: (i[b + first], 0, 0, 0)),
                pl.BlockSpec(arrived.shape, lambda b, i, v: (0, 0, 0)),
            ],
            out_specs=pl.BlockSpec(shape, out_map),
            scratch_shapes=[
                pltpu.VMEM((fields, tiles + 2, cells + 2 * PAD, LANES), f32),
                pltpu.VMEM((fields, tiles + 2, cells + 2 * PAD, LANES), f32),
                pltpu.VMEM((fields, tiles, cells, LANES), f32),
                pltpu.VMEM((fields * ROWS, 3 * fields * ROWS), bf16),
            ],
        ),
        out_shape=jax.ShapeDtypeStruct((slots_out, fields, cells, plane), bf16),
        compiler_params=pltpu.CompilerParams(vmem_limit_bytes=40 << 20),
        name="advance",
    )(ints, vals, blocks, arrived)


def plan(wanted, my_index, per_dev):
    peers, requests = wanted.shape
    at = lax.broadcasted_iota(jnp.int32, wanted.shape, 1)
    source_dev = wanted // per_dev
    code = wanted % per_dev * 6 + jnp.bitwise_xor(at % 6, 1)
    key = at * 64 + code
    match = source_dev == my_index
    first = jnp.min(jnp.where(match, key, 64 * requests), axis=1) % 64
    second = jnp.maximum(jnp.max(jnp.where(match, key, 0), axis=1), 0) % 64
    send = jnp.stack([first, second], axis=1).reshape(2 * peers)
    mine = lax.dynamic_slice_in_dim(wanted, my_index, 1, 0)[0]
    my_source = mine // per_dev
    order = jnp.arange(requests, dtype=jnp.int32)
    repeated = (my_source[:, None] == my_source[None, :]) & (order[None, :] < order[:, None])
    lookup = my_source * 2 + jnp.any(repeated, axis=1).astype(jnp.int32)
    return send, mine, lookup


def local(
    block_state,
    block_level,
    block_velocity,
    diffusivity,
    reaction_matrix,
    ghost_source,
    swap_bit,
    swap_slot,
):
    blocks = block_state[0]
    per_dev, fields, cells, plane = blocks.shape
    peers = lax.axis_size(("gy", "gz"))
    my_index = lax.axis_index(("gy", "gz"))
    levels = block_level[0]
    wanted = ghost_source[0].reshape(peers, per_dev * 6)
    send, mine, lookup = plan(wanted, my_index, per_dev)
    outgoing = pack_faces(blocks, send, 2 * peers)
    arrived = lax.all_to_all(outgoing, ("gy", "gz"), split_axis=0, concat_axis=0, tiled=True)

    own_levels = lax.dynamic_slice_in_dim(levels, my_index * per_dev, per_dev, 0)
    known = mine[:, None] == jnp.arange(levels.shape[0], dtype=jnp.int32)[None, :]
    source_levels = jnp.sum(jnp.where(known, levels[None, :], 0), axis=1)
    coarse = (source_levels.reshape(per_dev, 6) != own_levels[:, None]).astype(jnp.int32)
    bit_here = swap_bit[0, 0, 0]
    slot_here = swap_slot[0, 0, 0]
    rest = jnp.arange(per_dev, dtype=jnp.int32)
    rest = jnp.where(rest == 0, slot_here, rest - (rest <= slot_here))
    ints = jnp.concatenate([rest, own_levels, lookup, coarse.reshape(-1)])
    vals = jnp.concatenate(
        [block_velocity[0].astype(f32).reshape(-1), diffusivity, reaction_matrix.reshape(-1)]
    )
    departing = advance(ints, vals, blocks, arrived, 0, 1, 1)
    coming = departing
    for bit_no in range(lax.axis_size("gx").bit_length() - 1):
        coming = jnp.where(bit_here == bit_no, swapped(departing, "gx", bit_no), coming)
    stay = advance(ints, vals, blocks, arrived, 1, per_dev - 1, per_dev)
    result = lax.dynamic_update_slice_in_dim(stay, coming, slot_here, 0)
    return result[None]


def solution(mesh):
    in_specs = (
        P("gx", ("gy", "gz"), None, None, None),
        P("gx", None),
        P("gx", ("gy", "gz"), None),
        P(),
        P(),
        P("gx", None, None),
        P("gx", "gy", "gz"),
        P("gx", "gy", "gz"),
    )
    out_specs = P("gx", ("gy", "gz"), None, None, None)
    return jax.shard_map(local, mesh=mesh, in_specs=in_specs, out_specs=out_specs, check_vma=False)
```

time: 833 us -> 98.5 us (0.12)
  local copies, waits for them, and re-layouts: 552 us -> 4.01 us
  matrix products: 113 us -> 0 us
  other arithmetic: 63.2 us -> 2.91 us
  Pallas kernels: 0 us -> 41.5 us
  loops' own time: 35.3 us -> 0 us
  waiting for transfers between devices: 48.6 us -> 32.3 us
    reshape x49 -> x2, local copies, waits for them, and re-layouts: 163 us -> 0.18 us  [the longest x1 0.1 us: plan(): send = jnp.stack([first, second], axis=1).reshape(2 * peers)]
    broadcast_in_dim x80 -> x0, local copies, waits for them, and re-layouts: 148 us -> none  [the longest x16 71.7 us: advance_block(): low_z = jnp.repeat(layers[4].reshape(fields, cells, cells), cells, axis=2)]
    dot_general x16 -> x0, matrix products: 113 us -> none  [substep(): jnp.einsum('uj,jqi->uqi', reaction_matrix, species_field, precision=lax.P...]
    slice x79 -> x0, local copies, waits for them, and re-layouts: 112 us -> none  [the longest x16 44.4 us: substep(): species_field[:, :, :-1]]
    while x306 -> x0, local copies, waits for them, and re-layouts: 91.6 us -> none
    pallas_call x0 -> x3, Pallas kernels: none -> 41.5 us  [the longest x2 38.6 us: advance(): pl.pallas_call(functools.partial(advance_kernel, first, per_dev), grid_sp...]
    another operation x5 -> x0, loops' own time: 35.3 us -> none  [the longest x1 33.7 us: local(): lax.map(lambda packet: advance_block(packet, diffusivity, reaction_matrix...]
    ppermute x3, waiting for transfers between devices: 21.3 us -> 0.26 us  [swapped(): lax.ppermute(x, axis, [(i, i ^ 1 << bit) for i in range(lax.axis_size(axi...]
  transfers between devices with their start and end apart: 4 -> 4, of which waited for: 3 -> 2; matrix products, arithmetic and copies ran while one was open for 1% -> 1% of each run, Pallas kernels for 0% -> 29%
where the time goes in v1:
time: 98.5 us; the launch traced here: 98.2 us
  Pallas kernels  41.5 us (42%)
  waiting for transfers between devices  32.3 us (33%)
  starting transfers between devices  15.9 us (16%)
  local copies, waits for them, and re-layouts  4.01 us (4%)
  other arithmetic  2.91 us (3%)
  between operations  1.53 us (2%)
    pallas_call x2, Pallas kernels, advance(): pl.pallas_call(functools.partial(advance_kernel, first, per_dev), grid_sp...  38.6 us
    all_to_all x1, waiting for transfers between devices, local(): lax.all_to_all(outgoing, ('gy', 'gz'), split_axis=0, concat_axis=0, tiled...  32.1 us
    all_to_all x1, starting transfers between devices, local(): lax.all_to_all(outgoing, ('gy', 'gz'), split_axis=0, concat_axis=0, tiled...  11.2 us
    ppermute x3, starting transfers between devices, swapped(): lax.ppermute(x, axis, [(i, i ^ 1 << bit) for i in range(lax.axis_size(axi...  4.66 us
    unnamed x17, local copies, waits for them, and re-layouts  2.93 us
    pallas_call x1, Pallas kernels, pack_faces(): pl.pallas_call(pack_kernel, grid_spec=pltpu.PrefetchScalarGridSpec(num_sc...  2.92 us
  transfers between devices with their start and end apart: 4, of which 2 were waited for; matrix products, arithmetic and copies ran while one was open for 1% of the time, Pallas kernels for 29%

profile of v1, /device:TPU:32, one launch (start us, length us, event | category | flops | bytes accessed | tf_op | source)
XLA Modules:
  0.0 98.2 jit_solution(9918669893605991563)
XLA Ops:
  0.1 0.1 xor.16
  0.2 0.1 iota.72
  0.3 0.7 select_reduce_fusion.2
  1.0 0.1 reduce_min.15
  1.1 0.1 reduce_max.14
  1.3 0.1 reduce_min.20
  1.4 0.1 reduce_max.18
  1.5 0.1 copy.21
  1.6 0.1 reshape.204.send_ref
  1.7 1.7 %copy-done = bf16[1,4,10,32,1024]{4,3,2,1,0:T(8,128)(2,1)S(1)} copy-done((bf16[1,4,10,32,1024]{4,3,2,1,0:T(8,128)(2,1)S(1)}, bf16[1,4,10,32,1024]{4,3,2,1,0:T(8,128)(2,1)}, u32[]{:S(2)}) %copy-start) | copy-done | bytes 2621464
  3.5 2.9 %pack_faces.1 = bf16[64,80,128]{2,1,0:T(8,128)(2,1)S(1)} custom-call(s32[64]{0:T(128)S(1)} %reshape.204.send_ref, bf16[4,10,32,1024]{3,2,1,0:T(8,128)(2,1)S(1)} %bitcast.28), custom_call_target="tpu_custom_call" | custom-call | tf_op jit(solution)/shard_map/pack_faces/pallas_call | solution.py:83
  6.4 1.0 %copy-done.2 = bf16[64,80,128]{2,1,0:T(8,128)(2,1)} copy-done((bf16[64,80,128]{2,1,0:T(8,128)(2,1)}, bf16[64,80,128]{2,1,0:T(8,128)(2,1)S(1)}, u32[]{:S(2)}) %copy-start.2) | copy-done | bytes 1310744
  7.5 11.2 %all-to-all-start = ((bf16[64,80,128]{2,1,0:T(8,128)(2,1)}), bf16[64,80,128]{2,1,0:T(8,128)(2,1)}, u32[]{:S(2)}, u32[]{:S(2)}) async-start(bf16[64,80,128]{2,1,0:T(8,128)(2,1)} %copy-done.2), calls=%async_computation | async-start | bytes 2621440 | tf_op jit(solution)/shard_map/all_to_all | solution.py:315
  18.7 0.1 copy.16
  20.1 0.2 select_reduce_fusion
  20.3 0.2 fusion.1
  20.6 32.1 %all-to-all-done.arr_ref = bf16[64,80,128]{2,1,0:T(8,128)(2,1)} async-done(((bf16[64,80,128]{2,1,0:T(8,128)(2,1)}), bf16[64,80,128]{2,1,0:T(8,128)(2,1)}, u32[]{:S(2)}, u32[]{:S(2)}) %all-to-all-start) | async-done | bytes 1310752 | tf_op jit(solution)/shard_map/all_to_all | solution.py:315
  52.7 10.3 %advance.3 = bf16[1,10,32,1024]{3,2,1,0:T(8,128)(2,1)S(1)} custom-call(s32[56]{0:T(128)S(1)} %pad_add_fusion.1.ints_ref, f32[122]{0:T(128)S(1)} %pad_maximum_fusion.vals_ref, bf16[4,10,32,1024]{3,2,1,0:T(8,128)(2,1)S(1)} %bitcast.29, bf16[64,80,128]{2,1,0:T(8,128)(2,1)} %all-to-all-done.arr_ref), custom_call_target="tpu_custom_call" | custom-call | tf_op jit(solution)/shard_map/advance/pallas_call | solution.py:256
  63.0 0.1 collective-permute-start.2
  63.1 1.7 %collective-permute-start.1 = (bf16[1,10,32,1024]{3,2,1,0:T(8,128)(2,1)S(1)}, bf16[1,10,32,1024]{3,2,1,0:T(8,128)(2,1)}, u32[]{:S(2)}, u32[]{:S(2)}) collective-permute-start(bf16[1,10,32,1024]{3,2,1,0:T(8,128)(2,1)S(1)} %advance.3), channel_id=1, source_target_pairs={{0,64},{32,96},{64,0},{96,32},{128,192},{160,224},{192,128},{224,1... | collective-permute-start | bytes 1966088 | tf_op jit(solution)/shard_map/ppermute | solution.py:19
  64.8 2.9 %collective-permute-start = (bf16[1,10,32,1024]{3,2,1,0:T(8,128)(2,1)S(1)}, bf16[1,10,32,1024]{3,2,1,0:T(8,128)(2,1)}, u32[]{:S(2)}, u32[]{:S(2)}) collective-permute-start(bf16[1,10,32,1024]{3,2,1,0:T(8,128)(2,1)S(1)} %advance.3), channel_id=1, source_target_pairs={{0,128},{32,160},{64,192},{96,224},{128,0},{160,32},{192,64},{224,... | collective-permute-start | bytes 1966088 | tf_op jit(solution)/shard_map/ppermute | solution.py:19
  68.3 28.3 %advance.2 = bf16[4,10,32,1024]{3,2,1,0:T(8,128)(2,1)} custom-call(s32[56]{0:T(128)S(1)} %pad_add_fusion.1.ints_ref, f32[122]{0:T(128)S(1)} %pad_maximum_fusion.vals_ref, bf16[4,10,32,1024]{3,2,1,0:T(8,128)(2,1)S(1)} %bitcast.30, bf16[64,80,128]{2,1,0:T(8,128)(2,1)} %all-to-all-done.arr_ref), custom_call_target="tpu_custom_call" | custom-call | tf_op jit(solution)/shard_map/advance/pallas_call | solution.py:256
  96.6 0.3 collective-permute-done
  96.9 1.3 %bitcast_dynamic-update-slice_fusion = bf16[1,4,10,32,1024]{4,3,2,1,0:T(8,128)(2,1)} fusion(bf16[1,4,10,32,1024]{4,3,2,1,0:T(8,128)(2,1)} %bitcast.31, s32[]{:T(128)S(6)} %select_n.130, bf16[1,10,32,1024]{3,2,1,0:T(8,128)(2,1)} %collective-permute-done, bf16[1,10,32,1024]{3,2,1,0:T(8,128)(2,1)} %collective-permute-done.1, ...), kind=kLoop, calls=%fused_computation | loop fusion | flops 983040 | bytes 3278340 | tf_op jit(solution)/shard_map/dynamic_update_slice | solution.py:334
  (37 shorter events, 0.8 us)
Async XLA Ops:
  1.7 1.7 %copy-start = (bf16[1,4,10,32,1024]{4,3,2,1,0:T(8,128)(2,1)S(1)}, bf16[1,4,10,32,1024]{4,3,2,1,0:T(8,128)(2,1)}, u32[]{:S(2)}) copy-start(bf16[1,4,10,32,1024]{4,3,2,1,0:T(8,128)(2,1)} %param.8) | copy-start | bytes 7864324
  3.5 15.3 %copy-start.3 = (s32[1,128,6]{1,0,2:T(1,128)S(1)}, s32[1,128,6]{1,0,2:T(1,128)}, u32[]{:S(2)}) copy-start(s32[1,128,6]{1,0,2:T(1,128)} %param.13) | copy-start | bytes 9220
  3.5 16.0 %copy-start.6 = (bf16[1,4,3]{2,1,0:T(4,128)(2,1)S(1)}, bf16[1,4,3]{2,1,0:T(4,128)(2,1)}, u32[]{:S(2)}) copy-start(bf16[1,4,3]{2,1,0:T(4,128)(2,1)} %param.10) | copy-start | bytes 76
  3.5 16.1 %copy-start.4 = (f32[10,10]{1,0:T(8,128)S(1)}, f32[10,10]{1,0:T(8,128)}, u32[]{:S(2)}) copy-start(f32[10,10]{1,0:T(8,128)} %param.12) | copy-start | bytes 1204
  3.5 16.2 %copy-start.7 = (s32[1,128]{1,0:T(1,128)S(1)}, s32[1,128]{1,0:T(1,128)}, u32[]{:S(2)}) copy-start(s32[1,128]{1,0:T(1,128)} %param.9) | copy-start | bytes 1540
  3.5 16.6 %copy-start.5 = (f32[10]{0:T(128)S(1)}, f32[10]{0:T(128)}, u32[]{:S(2)}) copy-start(f32[10]{0:T(128)} %param.11) | copy-start | bytes 124
  3.5 49.2 %copy-start.1 = (bf16[1,4,10,32,1024]{4,3,2,1,0:T(8,128)(2,1)S(1)}, bf16[1,4,10,32,1024]{4,3,2,1,0:T(8,128)(2,1)}, u32[]{:S(2)}) copy-start(bf16[1,4,10,32,1024]{4,3,2,1,0:T(8,128)(2,1)} %param.8) | copy-start | bytes 7864324
  6.4 1.1 %copy-start.2 = (bf16[64,80,128]{2,1,0:T(8,128)(2,1)}, bf16[64,80,128]{2,1,0:T(8,128)(2,1)S(1)}, u32[]{:S(2)}) copy-start(bf16[64,80,128]{2,1,0:T(8,128)(2,1)S(1)} %pack_faces.1) | copy-start | bytes 3932164
  7.5 45.2 %all-to-all-start = ((bf16[64,80,128]{2,1,0:T(8,128)(2,1)}), bf16[64,80,128]{2,1,0:T(8,128)(2,1)}, u32[]{:S(2)}, u32[]{:S(2)}) async-start(bf16[64,80,128]{2,1,0:T(8,128)(2,1)} %copy-done.2), calls=%async_computation | async-start | bytes 2621440 | tf_op jit(solution)/shard_map/all_to_all | solution.py:315
  63.0 33.6 %collective-permute-start.2 = (bf16[1,10,32,1024]{3,2,1,0:T(8,128)(2,1)S(1)}, bf16[1,10,32,1024]{3,2,1,0:T(8,128)(2,1)}, u32[]{:S(2)}, u32[]{:S(2)}) collective-permute-start(bf16[1,10,32,1024]{3,2,1,0:T(8,128)(2,1)S(1)} %advance.3), channel_id=1, source_target_pairs={{0,32},{32,0},{64,96},{96,64},{128,160},{160,128},{192,224},{224,1... | collective-permute-start | bytes 1966088 | tf_op jit(solution)/shard_map/ppermute | solution.py:19
  63.1 33.5 %collective-permute-start.1 = (bf16[1,10,32,1024]{3,2,1,0:T(8,128)(2,1)S(1)}, bf16[1,10,32,1024]{3,2,1,0:T(8,128)(2,1)}, u32[]{:S(2)}, u32[]{:S(2)}) collective-permute-start(bf16[1,10,32,1024]{3,2,1,0:T(8,128)(2,1)S(1)} %advance.3), channel_id=1, source_target_pairs={{0,64},{32,96},{64,0},{96,32},{128,192},{160,224},{192,128},{224,1... | collective-permute-start | bytes 1966088 | tf_op jit(solution)/shard_map/ppermute | solution.py:19
  64.8 32.1 %collective-permute-start = (bf16[1,10,32,1024]{3,2,1,0:T(8,128)(2,1)S(1)}, bf16[1,10,32,1024]{3,2,1,0:T(8,128)(2,1)}, u32[]{:S(2)}, u32[]{:S(2)}) collective-permute-start(bf16[1,10,32,1024]{3,2,1,0:T(8,128)(2,1)S(1)} %advance.3), channel_id=1, source_target_pairs={{0,128},{32,160},{64,192},{96,224},{128,0},{160,32},{192,64},{224,... | collective-permute-start | bytes 1966088 | tf_op jit(solution)/shard_map/ppermute | solution.py:19

commit v2 on v1

--- a/solution.py
+++ b/solution.py
@@ -98,25 +98,73 @@
     )(send, blocks)
 
 
-def advance_kernel(first, per_dev, ints_ref, vals_ref, u_ref, arr_ref, o_ref, sa_ref, sb_ref, e_ref, rk_ref):
-    _, fields, cells, plane = u_ref.shape
-    groups = LANES // cells
-    tiles = plane // LANES
-    blk = ints_ref[pl.program_id(0) + first]
-    level = ints_ref[per_dev + blk]
-    lookup = lambda q: ints_ref[2 * per_dev + q]
-    coarse = lambda q: ints_ref[2 * per_dev + 6 * per_dev + q]
-    velocity = [vals_ref[blk * 3 + d] for d in range(3)]
-    diffusivity = lambda f: vals_ref[3 * per_dev + f]
-    reaction = lambda f, e: vals_ref[3 * per_dev + fields + f * fields + e]
-
-    n = jnp.left_shift(jnp.int32(1), level)
+def coefficients(ints_ref, vals_ref, blk, per_dev, fields):
+    n = jnp.left_shift(jnp.int32(1), ints_ref[per_dev + blk])
     scale = n.astype(f32)
     dt = dt_base / scale
+    adv = dt * scale
+    dif = dt * scale * scale
+    velocity = [vals_ref[blk * 3 + d] for d in range(3)]
+    minus = [adv * jnp.maximum(v, 0.0) for v in velocity]
+    plus = [-(adv * jnp.minimum(v, 0.0)) for v in velocity]
+    rates = [dif * vals_ref[3 * per_dev + f] for f in range(fields)]
+    return n, dt, minus, plus, rates
+
+
+def substep(src, put, edge_ref, own, minus, plus, rates, fields, cells, tiles):
     lane = lax.broadcasted_iota(jnp.int32, (ROWS, LANES), 1)
-    sub = lax.broadcasted_iota(jnp.int32, (ROWS, LANES), 0)
     k_first = lane % cells == 0
     k_last = lane % cells == cells - 1
+
+    def two_tiles(pair, carry):
+        for it in range(cells // ROWS):
+            row = PAD + ROWS * it
+            centre = [
+                [src[f, 2 * pair + 1 + q, pl.ds(row, ROWS), :] for f in range(fields)]
+                for q in range(2)
+            ]
+            both = jnp.concatenate([jnp.concatenate(c, axis=0) for c in centre], axis=1)
+            both_high = both.astype(bf16)
+            both_low = (both - both_high.astype(f32)).astype(bf16)
+            stacked = jnp.concatenate([both_high, both_high, both_low], axis=0)
+            mixed = jnp.dot(own, stacked, preferred_element_type=f32)
+            for q in range(2):
+                t = 2 * pair + q
+                for f in range(fields):
+                    c = centre[q][f]
+                    minus_x = src[f, t + 1, pl.ds(row - 1, ROWS), :]
+                    plus_x = src[f, t + 1, pl.ds(row + 1, ROWS), :]
+                    left = src[f, t, pl.ds(row, ROWS), :]
+                    right = src[f, t + 2, pl.ds(row, ROWS), :]
+                    edge = 0.0 if edge_ref is None else edge_ref[f, t, pl.ds(ROWS * it, ROWS), :]
+                    minus_y = lane_roll(jnp.where(lane >= LANES - cells, left, c), cells)
+                    plus_y = lane_roll(jnp.where(lane < cells, right, c), -cells)
+                    minus_z = jnp.where(k_first, edge, lane_roll(c, 1))
+                    plus_z = jnp.where(k_last, edge, lane_roll(c, -1))
+                    near = (rates[f] + minus[0]) * minus_x + (rates[f] + plus[0]) * plus_x
+                    near += (rates[f] + minus[1]) * minus_y + (rates[f] + plus[1]) * plus_y
+                    near += (rates[f] + minus[2]) * minus_z + (rates[f] + plus[2]) * plus_z
+                    own_terms = mixed[ROWS * f : ROWS * f + ROWS, LANES * q : LANES * q + LANES]
+                    put(f, t, it, near + (c + own_terms))
+        return carry
+
+    lax.fori_loop(0, tiles // 2, two_tiles, 0)
+
+
+def first_kernel(per_dev, ints_ref, vals_ref, u_ref, o_ref, rk_out_ref, sa_ref):
+    _, fields, cells, plane = u_ref.shape
+    tiles = plane // LANES
+    blk = pl.program_id(0)
+    n, dt, minus, plus, rates = coefficients(ints_ref, vals_ref, blk, per_dev, fields)
+    reaction = lambda f, e: vals_ref[3 * per_dev + fields + f * fields + e]
+
+    @pl.when(blk == 0)
+    def _():
+        zeros = jnp.zeros((fields, cells + 2 * PAD, LANES), f32)
+        sa_ref[:, 0] = zeros
+        sa_ref[:, tiles + 1] = zeros
+        sa_ref[:, :, 0:PAD] = jnp.zeros((fields, tiles + 2, PAD, LANES), f32)
+        sa_ref[:, :, PAD + cells :] = jnp.zeros((fields, tiles + 2, PAD, LANES), f32)
 
     for t in range(tiles):
         for half in range(cells // 16):
@@ -124,49 +172,7 @@
                 0, :, pl.ds(16 * half, 16), pl.ds(LANES * t, LANES)
             ].astype(f32)
 
-    def pair_lanes(x, step):
-        even = ((lane // step) % 2 == 0)[None]
-        return x + jnp.where(even, lane_roll(x, -step), lane_roll(x, step))
-
-    def pair_rows(x):
-        even = (sub % 2 == 0)[None]
-        return x + jnp.where(even, pltpu.roll(x, ROWS - 1, 1), pltpu.roll(x, 1, 1))
-
-    def face(face_no, pair_a, pair_b):
-        q = blk * 6 + face_no
-        layer = arr_ref[lookup(q)].astype(f32).reshape(fields, ROWS, LANES)
-        return jnp.where(coarse(q) > 0, pair_b(pair_a(layer)) * 0.25, layer)
-
-    by_cells = lambda x: pair_lanes(x, cells)
-    by_one = lambda x: pair_lanes(x, 1)
-    states = (sa_ref, sb_ref)
-    low, high = face(0, by_cells, by_one), face(1, by_cells, by_one)
-    for state in states:
-        for t in range(tiles):
-            state[:, t + 1, PAD - 1 : PAD, :] = low[:, t : t + 1, :]
-            state[:, t + 1, PAD + cells : PAD + cells + 1, :] = high[:, t : t + 1, :]
-    low, high = face(2, by_one, pair_rows), face(3, by_one, pair_rows)
-    for b in range(groups):
-        low_b = lane_roll(low, cells * (groups - 1 - b))
-        high_b = lane_roll(high, -cells * b)
-        for state in states:
-            state[:, 0, pl.ds(PAD + ROWS * b, ROWS), :] = low_b
-            state[:, tiles + 1, pl.ds(PAD + ROWS * b, ROWS), :] = high_b
-    low, high = face(4, by_cells, pair_rows), face(5, by_cells, pair_rows)
-    for b in range(groups):
-        for t in range(tiles):
-            at = tiles * b + t
-            e_ref[:, t, pl.ds(ROWS * b, ROWS), :] = jnp.where(
-                k_first[None], lane_roll(low, -at), lane_roll(high, cells - 1 - at)
-            )
-
-    adv = dt * scale
-    dif = dt * scale * scale
-    minus = [adv * jnp.maximum(v, 0.0) for v in velocity]
-    plus = [-(adv * jnp.minimum(v, 0.0)) for v in velocity]
     outflow = sum(minus) + sum(plus)
-    rates = [dif * diffusivity(f) for f in range(fields)]
-
     size = fields * ROWS
     ri = lax.broadcasted_iota(jnp.int32, (size, size), 0)
     ci = lax.broadcasted_iota(jnp.int32, (size, size), 1)
@@ -180,47 +186,117 @@
             line = jnp.where(ci // ROWS == e, term, line)
         matrix = jnp.where(ri // ROWS == f, line, matrix)
     matrix = jnp.where(ri % ROWS == ci % ROWS, matrix, 0.0)
-    matrix_high = matrix.astype(bf16)
-    rk_ref[:, 0:size] = matrix_high
-    rk_ref[:, size : 2 * size] = (matrix - matrix_high.astype(f32)).astype(bf16)
-    rk_ref[:, 2 * size : 3 * size] = matrix_high
-
-    def substep(src, dst):
-        own = rk_ref[...]
-
-        def two_tiles(pair, carry):
-            for it in range(cells // ROWS):
-                row = PAD + ROWS * it
-                centre = [
-                    [src[f, 2 * pair + 1 + q, pl.ds(row, ROWS), :] for f in range(fields)]
-                    for q in range(2)
-                ]
-                both = jnp.concatenate([jnp.concatenate(c, axis=0) for c in centre], axis=1)
-                both_high = both.astype(bf16)
-                both_low = (both - both_high.astype(f32)).astype(bf16)
-                stacked = jnp.concatenate([both_high, both_high, both_low], axis=0)
-                mixed = jnp.dot(own, stacked, preferred_element_type=f32)
-                for q in range(2):
-                    t = 2 * pair + q
-                    for f in range(fields):
-                        c = centre[q][f]
-                        minus_x = src[f, t + 1, pl.ds(row - 1, ROWS), :]
-                        plus_x = src[f, t + 1, pl.ds(row + 1, ROWS), :]
-                        left = src[f, t, pl.ds(row, ROWS), :]
-                        right = src[f, t + 2, pl.ds(row, ROWS), :]
-                        edge = e_ref[f, t, pl.ds(ROWS * it, ROWS), :]
-                        minus_y = lane_roll(jnp.where(lane >= LANES - cells, left, c), cells)
-                        plus_y = lane_roll(jnp.where(lane < cells, right, c), -cells)
-                        minus_z = jnp.where(k_first, edge, lane_roll(c, 1))
-                        plus_z = jnp.where(k_last, edge, lane_roll(c, -1))
-                        near = (rates[f] + minus[0]) * minus_x + (rates[f] + plus[0]) * plus_x
-                        near += (rates[f] + minus[1]) * minus_y + (rates[f] + plus[1]) * plus_y
-                        near += (rates[f] + minus[2]) * minus_z + (rates[f] + plus[2]) * plus_z
-                        own_terms = mixed[ROWS * f : ROWS * f + ROWS, LANES * q : LANES * q + LANES]
-                        dst[f, t + 1, pl.ds(row, ROWS), :] = near + (c + own_terms)
-            return carry
-
-        lax.fori_loop(0, tiles // 2, two_tiles, 0)
+    high = matrix.astype(bf16)
+    rk_out_ref[0, :, 0:size] = high
+    rk_out_ref[0, :, size : 2 * size] = (matrix - high.astype(f32)).astype(bf16)
+    rk_out_ref[0, :, 2 * size : 3 * size] = high
+
+    def put(f, t, it, value):
+        o_ref[0, f, t, pl.ds(ROWS * it, ROWS), :] = value
+
+    substep(sa_ref, put, None, rk_out_ref[0], minus, plus, rates, fields, cells, tiles)
+
+
+def first_substep(ints, vals, blocks):
+    per_dev, fields, cells, plane = blocks.shape
+    tiles = plane // LANES
+    size = fields * ROWS
+    return pl.pallas_call(
+        functools.partial(first_kernel, per_dev),
+        grid_spec=pltpu.PrefetchScalarGridSpec(
+            num_scalar_prefetch=2,
+            grid=(per_dev,),
+            in_specs=[pl.BlockSpec((1, fields, cells, plane), lambda b, i, v: (b, 0, 0, 0))],
+            out_specs=[
+                pl.BlockSpec((1, fields, tiles, cells, LANES), lambda b, i, v: (b, 0, 0, 0, 0)),
+                pl.BlockSpec((1, size, 3 * size), lambda b, i, v: (b, 0, 0)),
+            ],
+            scratch_shapes=[pltpu.VMEM((fields, tiles + 2, cells + 2 * PAD, LANES), f32)],
+        ),
+        out_shape=[
+            jax.ShapeDtypeStruct((per_dev, fields, tiles, cells, LANES), f32),
+            jax.ShapeDtypeStruct((per_dev, size, 3 * size), bf16),
+        ],
+        compiler_params=pltpu.CompilerParams(vmem_limit_bytes=32 << 20),
+        name="first_substep",
+    )(ints, vals, blocks)
+
+
+def advance_kernel(first, per_dev, ints_ref, vals_ref, s_ref, rk_ref, arr_ref, o_ref, sa_ref, sb_ref, e_ref):
+    _, fields, tiles, cells, _ = s_ref.shape
+    groups = LANES // cells
+    blk = ints_ref[pl.program_id(0) + first]
+    lookup = lambda q: ints_ref[2 * per_dev + q]
+    coarse = lambda q: ints_ref[2 * per_dev + 6 * per_dev + q]
+    n, dt, minus, plus, rates = coefficients(ints_ref, vals_ref, blk, per_dev, fields)
+    lane = lax.broadcasted_iota(jnp.int32, (ROWS, LANES), 1)
+    sub = lax.broadcasted_iota(jnp.int32, (ROWS, LANES), 0)
+    k_first = lane % cells == 0
+    k_last = lane % cells == cells - 1
+
+    def pair_lanes(x, step):
+        even = ((lane // step) % 2 == 0)[None]
+        return x + jnp.where(even, lane_roll(x, -step), lane_roll(x, step))
+
+    def pair_rows(x):
+        even = (sub % 2 == 0)[None]
+        return x + jnp.where(even, pltpu.roll(x, ROWS - 1, 1), pltpu.roll(x, 1, 1))
+
+    def face(face_no, pair_a, pair_b):
+        q = blk * 6 + face_no
+        layer = arr_ref[lookup(q)].astype(f32).reshape(fields, ROWS, LANES)
+        return jnp.where(coarse(q) > 0, pair_b(pair_a(layer)) * 0.25, layer)
+
+    def per_field(terms):
+        return jnp.concatenate([jnp.full((1, ROWS, LANES), x, f32) for x in terms], axis=0)
+
+    by_cells = lambda x: pair_lanes(x, cells)
+    by_one = lambda x: pair_lanes(x, 1)
+    states = (sa_ref, sb_ref)
+    rate = per_field(rates)
+
+    low, high = face(4, by_cells, pair_rows), face(5, by_cells, pair_rows)
+    weight = jnp.where(
+        k_first[None], rate + minus[2], jnp.where(k_last[None], rate + plus[2], 0.0)
+    )
+    for b in range(groups):
+        rows = pl.ds(ROWS * b, ROWS)
+        for t in range(tiles):
+            at = tiles * b + t
+            edge = jnp.where(k_first[None], lane_roll(low, -at), lane_roll(high, cells - 1 - at))
+            e_ref[:, t, rows, :] = edge
+            sa_ref[:, t + 1, pl.ds(PAD + ROWS * b, ROWS), :] = s_ref[0, :, t, rows, :] + weight * edge
+
+    low, high = face(2, by_one, pair_rows), face(3, by_one, pair_rows)
+    for b in range(groups):
+        rows = pl.ds(PAD + ROWS * b, ROWS)
+        low_b = lane_roll(low, -cells * b)
+        high_b = lane_roll(high, cells * (groups - 1 - b))
+        sa_ref[:, 1, rows, :] += jnp.where(lane < cells, (rate + minus[1]) * low_b, 0.0)
+        sa_ref[:, tiles, rows, :] += jnp.where(lane >= LANES - cells, (rate + plus[1]) * high_b, 0.0)
+        low_b = lane_roll(low, cells * (groups - 1 - b))
+        high_b = lane_roll(high, -cells * b)
+        for state in states:
+            state[:, 0, rows, :] = low_b
+            state[:, tiles + 1, rows, :] = high_b
+
+    low, high = face(0, by_cells, by_one), face(1, by_cells, by_one)
+    low_part = (rate + minus[0]) * low
+    high_part = (rate + plus[0]) * high
+    for t in range(tiles):
+        sa_ref[:, t + 1, PAD : PAD + 1, :] += low_part[:, t : t + 1, :]
+        sa_ref[:, t + 1, PAD + cells - 1 : PAD + cells, :] += high_part[:, t : t + 1, :]
+        for state in states:
+            state[:, t + 1, PAD - 1 : PAD, :] = low[:, t : t + 1, :]
+            state[:, t + 1, PAD + cells : PAD + cells + 1, :] = high[:, t : t + 1, :]
+
+    own = rk_ref[0]
+
+    def step(src, dst):
+        def put(f, t, it, value):
+            dst[f, t + 1, pl.ds(PAD + ROWS * it, ROWS), :] = value
+
+        substep(src, put, e_ref, own, minus, plus, rates, fields, cells, tiles)
 
     def finish(src):
         for t in range(tiles):
@@ -231,23 +307,23 @@
 
     @pl.when(n == 1)
     def _():
-        substep(sa_ref, sb_ref)
-        finish(sb_ref)
+        finish(sa_ref)
 
     @pl.when(n > 1)
     def _():
         def two(i, carry):
-            substep(sa_ref, sb_ref)
-            substep(sb_ref, sa_ref)
+            step(sa_ref, sb_ref)
+            step(sb_ref, sa_ref)
             return carry
 
-        lax.fori_loop(0, n // 2, two, 0)
-        finish(sa_ref)
-
-
-def advance(ints, vals, blocks, arrived, first, count, slots_out):
-    per_dev, fields, cells, plane = blocks.shape
-    tiles = plane // LANES
+        lax.fori_loop(0, (n - 2) // 2, two, 0)
+        step(sa_ref, sb_ref)
+        finish(sb_ref)
+
+
+def advance(ints, vals, started, own, arrived, plane, first, count, slots_out):
+    per_dev, fields, tiles, cells, _ = started.shape
+    padded = (fields, tiles + 2, cells + 2 * PAD, LANES)
     shape = (1, fields, cells, plane)
     if slots_out == 1:
         out_map = lambda b, i, v: (0, 0, 0, 0)
@@ -259,21 +335,21 @@
             num_scalar_prefetch=2,
             grid=(count,),
             in_specs=[
-                pl.BlockSpec(shape, lambda b, i, v: (i[b + first], 0, 0, 0)),
+                pl.BlockSpec((1,) + started.shape[1:], lambda b, i, v: (i[b + first], 0, 0, 0, 0)),
+                pl.BlockSpec((1,) + own.shape[1:], lambda b, i, v: (i[b + first], 0, 0)),
                 pl.BlockSpec(arrived.shape, lambda b, i, v: (0, 0, 0)),
             ],
             out_specs=pl.BlockSpec(shape, out_map),
             scratch_shapes=[
-                pltpu.VMEM((fields, tiles + 2, cells + 2 * PAD, LANES), f32),
-                pltpu.VMEM((fields, tiles + 2, cells + 2 * PAD, LANES), f32),
+                pltpu.VMEM(padded, f32),
+                pltpu.VMEM(padded, f32),
                 pltpu.VMEM((fields, tiles, cells, LANES), f32),
-                pltpu.VMEM((fields * ROWS, 3 * fields * ROWS), bf16),
             ],
         ),
         out_shape=jax.ShapeDtypeStruct((slots_out, fields, cells, plane), bf16),
         compiler_params=pltpu.CompilerParams(vmem_limit_bytes=40 << 20),
         name="advance",
-    )(ints, vals, blocks, arrived)
+    )(ints, vals, started, own, arrived)
 
 
 def plan(wanted, my_index, per_dev):
@@ -326,11 +402,12 @@
     vals = jnp.concatenate(
         [block_velocity[0].astype(f32).reshape(-1), diffusivity, reaction_matrix.reshape(-1)]
     )
-    departing = advance(ints, vals, blocks, arrived, 0, 1, 1)
+    started, own = first_substep(ints, vals, blocks)
+    departing = advance(ints, vals, started, own, arrived, plane, 0, 1, 1)
     coming = departing
     for bit_no in range(lax.axis_size("gx").bit_length() - 1):
         coming = jnp.where(bit_here == bit_no, swapped(departing, "gx", bit_no), coming)
-    stay = advance(ints, vals, blocks, arrived, 1, per_dev - 1, per_dev)
+    stay = advance(ints, vals, started, own, arrived, plane, 1, per_dev - 1, per_dev)
     result = lax.dynamic_update_slice_in_dim(stay, coming, slot_here, 0)
     return result[None]
 

time: 98.5 us -> 95 us (0.964)
  waiting for transfers between devices: 32.3 us -> 21.7 us
  local copies, waits for them, and re-layouts: 4.01 us -> 12 us
    all_to_all x1, waiting for transfers between devices: 32.1 us -> 19.4 us  [local(): lax.all_to_all(outgoing, ('gy', 'gz'), split_axis=0, concat_axis=0, tiled...]
    pallas_call x2, Pallas kernels: 38.6 us -> 28.9 us  [advance(): pl.pallas_call(functools.partial(advance_kernel, first, per_dev), grid_sp...]
    pallas_call x0 -> x1, Pallas kernels: none -> 8.57 us  [first_substep(): pl.pallas_call(functools.partial(first_kernel, per_dev), grid_spec=pltpu....]
    unnamed x17 -> x21, local copies, waits for them, and re-layouts: 2.93 us -> 10.9 us
    ppermute x3, waiting for transfers between devices: 0.26 us -> 2.32 us  [swapped(): lax.ppermute(x, axis, [(i, i ^ 1 << bit) for i in range(lax.axis_size(axi...]
    pallas_call x1, Pallas kernels: 2.92 us -> 3.96 us  [pack_faces(): pl.pallas_call(pack_kernel, grid_spec=pltpu.PrefetchScalarGridSpec(num_sc...]
  transfers between devices with their start and end apart: 4 -> 4, of which waited for: 2 -> 2; matrix products, arithmetic and copies ran while one was open for 1% -> 1% of each run, Pallas kernels for 29% -> 32%
where the time goes in v2:
time: 95 us; the launch traced here: 94.6 us
  Pallas kernels  41.4 us (44%)
  waiting for transfers between devices  21.7 us (23%)
  starting transfers between devices  15.1 us (16%)
  local copies, waits for them, and re-layouts  12 us (13%)
  other arithmetic  2.91 us (3%)
  between operations  1.51 us (2%)
    pallas_call x2, Pallas kernels, advance(): pl.pallas_call(functools.partial(advance_kernel, first, per_dev), grid_sp...  28.9 us
    all_to_all x1, waiting for transfers between devices, local(): lax.all_to_all(outgoing, ('gy', 'gz'), split_axis=0, concat_axis=0, tiled...  19.4 us
    all_to_all x1, starting transfers between devices, local(): lax.all_to_all(outgoing, ('gy', 'gz'), split_axis=0, concat_axis=0, tiled...  11.2 us
    unnamed x21, local copies, waits for them, and re-layouts  10.9 us
    pallas_call x1, Pallas kernels, first_substep(): pl.pallas_call(functools.partial(first_kernel, per_dev), grid_spec=pltpu....  8.57 us
    pallas_call x1, Pallas kernels, pack_faces(): pl.pallas_call(pack_kernel, grid_spec=pltpu.PrefetchScalarGridSpec(num_sc...  3.96 us
    ppermute x3, starting transfers between devices, swapped(): lax.ppermute(x, axis, [(i, i ^ 1 << bit) for i in range(lax.axis_size(axi...  3.96 us
    ppermute x3, waiting for transfers between devices, swapped(): lax.ppermute(x, axis, [(i, i ^ 1 << bit) for i in range(lax.axis_size(axi...  2.32 us
  transfers between devices with their start and end apart: 4, of which 2 were waited for; matrix products, arithmetic and copies ran while one was open for 1% of the time, Pallas kernels for 32%

profile of v2, /device:TPU:32, one launch (start us, length us, event | category | flops | bytes accessed | tf_op | source)
XLA Modules:
  0.0 94.6 jit_solution(12786709254156264523)
XLA Ops:
  0.1 0.1 iota.72
  0.2 0.1 xor.16
  0.3 0.7 select_reduce_fusion.2
  1.2 0.1 reduce_max.18
  1.4 0.1 reduce_min.20
  1.6 0.1 reshape.204.send_ref
  1.7 1.7 %copy-done.3 = bf16[1,4,10,32,1024]{4,3,2,1,0:T(8,128)(2,1)S(1)} copy-done((bf16[1,4,10,32,1024]{4,3,2,1,0:T(8,128)(2,1)S(1)}, bf16[1,4,10,32,1024]{4,3,2,1,0:T(8,128)(2,1)}, u32[]{:S(2)}) %copy-start.3) | copy-done | bytes 2621464
  3.5 4.0 %pack_faces.1 = bf16[64,80,128]{2,1,0:T(8,128)(2,1)} custom-call(s32[64]{0:T(128)S(1)} %reshape.204.send_ref, bf16[4,10,32,1024]{3,2,1,0:T(8,128)(2,1)S(1)} %bitcast.28), custom_call_target="tpu_custom_call" | custom-call | tf_op jit(solution)/shard_map/pack_faces/pallas_call | solution.py:83
  7.4 11.2 %all-to-all-start = ((bf16[64,80,128]{2,1,0:T(8,128)(2,1)}), bf16[64,80,128]{2,1,0:T(8,128)(2,1)S(1)}, u32[]{:S(2)}, u32[]{:S(2)}) async-start(bf16[64,80,128]{2,1,0:T(8,128)(2,1)} %pack_faces.1), calls=%async_computation | async-start | bytes 2621440 | tf_op jit(solution)/shard_map/all_to_all | solution.py:391
  18.6 0.1 copy.16
  20.0 0.2 select_reduce_fusion
  20.1 0.2 fusion.1
  20.5 1.7 %copy-done.4 = bf16[1,4,10,32,1024]{4,3,2,1,0:T(8,128)(2,1)S(1)} copy-done((bf16[1,4,10,32,1024]{4,3,2,1,0:T(8,128)(2,1)S(1)}, bf16[1,4,10,32,1024]{4,3,2,1,0:T(8,128)(2,1)}, u32[]{:S(2)}) %copy-start.4) | copy-done | bytes 2621464
  22.2 8.6 %first_substep.1 = (f32[4,10,8,32,128]{4,3,2,1,0:T(8,128)S(1)}, bf16[4,80,240]{2,1,0:T(8,128)(2,1)S(1)}) custom-call(s32[56]{0:T(128)S(1)} %pad_add_fusion.1.ints_ref, f32[122]{0:T(128)S(1)} %pad_maximum_fusion.vals_ref, bf16[4,10,32,1024]{3,2,1,0:T(8,128)(2,1)S(1)} %bitcast.29), custom_call_target="tpu_custom_call" | custom-call | tf_op jit(solution)/shard_map/first_substep/pallas_call | solution.py:204
  30.8 2.3 %copy-done = f32[4,10,8,32,128]{4,3,2,1,0:T(8,128)} copy-done((f32[4,10,8,32,128]{4,3,2,1,0:T(8,128)}, f32[4,10,8,32,128]{4,3,2,1,0:T(8,128)S(1)}, u32[]{:S(2)}) %copy-start) | copy-done | bytes 5242904
  33.1 19.4 %all-to-all-done.arr_ref = bf16[64,80,128]{2,1,0:T(8,128)(2,1)S(1)} async-done(((bf16[64,80,128]{2,1,0:T(8,128)(2,1)}), bf16[64,80,128]{2,1,0:T(8,128)(2,1)S(1)}, u32[]{:S(2)}, u32[]{:S(2)}) %all-to-all-start) | async-done | bytes 1310752 | tf_op jit(solution)/shard_map/all_to_all | solution.py:391
  52.5 2.5 %copy-done.1 = f32[4,10,8,32,128]{4,3,2,1,0:T(8,128)S(1)} copy-done((f32[4,10,8,32,128]{4,3,2,1,0:T(8,128)S(1)}, f32[4,10,8,32,128]{4,3,2,1,0:T(8,128)}, u32[]{:S(2)}) %copy-start.1) | copy-done | bytes 5242904
  55.0 7.2 %advance.3 = bf16[1,10,32,1024]{3,2,1,0:T(8,128)(2,1)S(1)} custom-call(s32[56]{0:T(128)S(1)} %pad_add_fusion.1.ints_ref, f32[122]{0:T(128)S(1)} %pad_maximum_fusion.vals_ref, f32[4,10,8,32,128]{4,3,2,1,0:T(8,128)S(1)} %copy-done.1, bf16[4,80,240]{2,1,0:T(8,128)(2,1)S(1)} %get-tuple-element.8.rk_ref, bf16[64,80,128]{2,1,0:T(8,128)(2,1)S(1)} %all-to-all-done.arr_ref), custom_call_target="tpu_custom_call" | custom-call | tf_op jit(solution)/shard_map/advance/pallas_call | solution.py:332
  62.3 3.3 %collective-permute-start = (bf16[1,10,32,1024]{3,2,1,0:T(8,128)(2,1)S(1)}, bf16[1,10,32,1024]{3,2,1,0:T(8,128)(2,1)S(1)}, u32[]{:S(2)}, u32[]{:S(2)}) collective-permute-start(bf16[1,10,32,1024]{3,2,1,0:T(8,128)(2,1)S(1)} %advance.3), channel_id=1, source_target_pairs={{0,128},{32,160},{64,192},{96,224},{128,0},{160,32},{192,64},{224,... | collective-permute-start | bytes 1966088 | tf_op jit(solution)/shard_map/ppermute | solution.py:19
  65.5 0.7 collective-permute-start.1
  66.9 2.5 %copy-done.2 = f32[4,10,8,32,128]{4,3,2,1,0:T(8,128)S(1)} copy-done((f32[4,10,8,32,128]{4,3,2,1,0:T(8,128)S(1)}, f32[4,10,8,32,128]{4,3,2,1,0:T(8,128)}, u32[]{:S(2)}) %copy-start.2) | copy-done | bytes 5242904
  69.4 21.6 %advance.2 = bf16[4,10,32,1024]{3,2,1,0:T(8,128)(2,1)} custom-call(s32[56]{0:T(128)S(1)} %pad_add_fusion.1.ints_ref, f32[122]{0:T(128)S(1)} %pad_maximum_fusion.vals_ref, f32[4,10,8,32,128]{4,3,2,1,0:T(8,128)S(1)} %copy-done.2, bf16[4,80,240]{2,1,0:T(8,128)(2,1)S(1)} %get-tuple-element.8.rk_ref, bf16[64,80,128]{2,1,0:T(8,128)(2,1)S(1)} %all-to-all-done.arr_ref), custom_call_target="tpu_custom_call" | custom-call | tf_op jit(solution)/shard_map/advance/pallas_call | solution.py:332
  91.0 2.3 %collective-permute-done.1 = bf16[1,10,32,1024]{3,2,1,0:T(8,128)(2,1)S(1)} collective-permute-done((bf16[1,10,32,1024]{3,2,1,0:T(8,128)(2,1)S(1)}, bf16[1,10,32,1024]{3,2,1,0:T(8,128)(2,1)S(1)}, u32[]{:S(2)}, u32[]{:S(2)}) %collective-permute-start.1) | collective-permute-done | bytes 655392 | tf_op jit(solution)/shard_map/ppermute | solution.py:19
  93.3 1.3 %bitcast_dynamic-update-slice_fusion = bf16[1,4,10,32,1024]{4,3,2,1,0:T(8,128)(2,1)} fusion(bf16[1,4,10,32,1024]{4,3,2,1,0:T(8,128)(2,1)} %bitcast.30, s32[]{:T(128)S(6)} %select_n.130, bf16[1,10,32,1024]{3,2,1,0:T(8,128)(2,1)S(1)} %collective-permute-done, bf16[1,10,32,1024]{3,2,1,0:T(8,128)(2,1)S(1)} %collective-permute-done.1, ...), kind=kLoop, calls=%fused_computation | loop fusion | flops 983040 | bytes 3278340 | tf_op jit(solution)/shard_map/dynamic_update_slice | solution.py:411
  (42 shorter events, 1.1 us)
Async XLA Ops:
  1.7 1.7 %copy-start.3 = (bf16[1,4,10,32,1024]{4,3,2,1,0:T(8,128)(2,1)S(1)}, bf16[1,4,10,32,1024]{4,3,2,1,0:T(8,128)(2,1)}, u32[]{:S(2)}) copy-start(bf16[1,4,10,32,1024]{4,3,2,1,0:T(8,128)(2,1)} %param.8) | copy-start | bytes 7864324
  3.5 15.2 %copy-start.5 = (s32[1,128,6]{1,0,2:T(1,128)S(1)}, s32[1,128,6]{1,0,2:T(1,128)}, u32[]{:S(2)}) copy-start(s32[1,128,6]{1,0,2:T(1,128)} %param.13) | copy-start | bytes 9220
  3.5 15.4 %copy-start.9 = (s32[1,128]{1,0:T(1,128)S(1)}, s32[1,128]{1,0:T(1,128)}, u32[]{:S(2)}) copy-start(s32[1,128]{1,0:T(1,128)} %param.9) | copy-start | bytes 1540
  3.5 16.3 %copy-start.6 = (f32[10,10]{1,0:T(8,128)S(1)}, f32[10,10]{1,0:T(8,128)}, u32[]{:S(2)}) copy-start(f32[10,10]{1,0:T(8,128)} %param.12) | copy-start | bytes 1204
  3.5 16.4 %copy-start.8 = (bf16[1,4,3]{2,1,0:T(4,128)(2,1)S(1)}, bf16[1,4,3]{2,1,0:T(4,128)(2,1)}, u32[]{:S(2)}) copy-start(bf16[1,4,3]{2,1,0:T(4,128)(2,1)} %param.10) | copy-start | bytes 76
  3.5 17.0 %copy-start.7 = (f32[10]{0:T(128)S(1)}, f32[10]{0:T(128)}, u32[]{:S(2)}) copy-start(f32[10]{0:T(128)} %param.11) | copy-start | bytes 124
  7.4 45.1 %all-to-all-start = ((bf16[64,80,128]{2,1,0:T(8,128)(2,1)}), bf16[64,80,128]{2,1,0:T(8,128)(2,1)S(1)}, u32[]{:S(2)}, u32[]{:S(2)}) async-start(bf16[64,80,128]{2,1,0:T(8,128)(2,1)} %pack_faces.1), calls=%async_computation | async-start | bytes 2621440 | tf_op jit(solution)/shard_map/all_to_all | solution.py:391
  20.5 1.7 %copy-start.4 = (bf16[1,4,10,32,1024]{4,3,2,1,0:T(8,128)(2,1)S(1)}, bf16[1,4,10,32,1024]{4,3,2,1,0:T(8,128)(2,1)}, u32[]{:S(2)}) copy-start(bf16[1,4,10,32,1024]{4,3,2,1,0:T(8,128)(2,1)} %param.8) | copy-start | bytes 7864324
  30.8 2.3 %copy-start = (f32[4,10,8,32,128]{4,3,2,1,0:T(8,128)}, f32[4,10,8,32,128]{4,3,2,1,0:T(8,128)S(1)}, u32[]{:S(2)}) copy-start(f32[4,10,8,32,128]{4,3,2,1,0:T(8,128)S(1)} %get-tuple-element.7.s_ref) | copy-start | bytes 15728644
  52.5 2.5 %copy-start.1 = (f32[4,10,8,32,128]{4,3,2,1,0:T(8,128)S(1)}, f32[4,10,8,32,128]{4,3,2,1,0:T(8,128)}, u32[]{:S(2)}) copy-start(f32[4,10,8,32,128]{4,3,2,1,0:T(8,128)} %copy-done) | copy-start | bytes 15728644
  62.3 28.7 %collective-permute-start = (bf16[1,10,32,1024]{3,2,1,0:T(8,128)(2,1)S(1)}, bf16[1,10,32,1024]{3,2,1,0:T(8,128)(2,1)S(1)}, u32[]{:S(2)}, u32[]{:S(2)}) collective-permute-start(bf16[1,10,32,1024]{3,2,1,0:T(8,128)(2,1)S(1)} %advance.3), channel_id=1, source_target_pairs={{0,128},{32,160},{64,192},{96,224},{128,0},{160,32},{192,64},{224,... | collective-permute-start | bytes 1966088 | tf_op jit(solution)/shard_map/ppermute | solution.py:19
  65.5 27.8 %collective-permute-start.1 = (bf16[1,10,32,1024]{3,2,1,0:T(8,128)(2,1)S(1)}, bf16[1,10,32,1024]{3,2,1,0:T(8,128)(2,1)S(1)}, u32[]{:S(2)}, u32[]{:S(2)}) collective-permute-start(bf16[1,10,32,1024]{3,2,1,0:T(8,128)(2,1)S(1)} %advance.3), channel_id=1, source_target_pairs={{0,64},{32,96},{64,0},{96,32},{128,192},{160,224},{192,128},{224,1... | collective-permute-start | bytes 1966088 | tf_op jit(solution)/shard_map/ppermute | solution.py:19
  66.2 27.1 %collective-permute-start.2 = (bf16[1,10,32,1024]{3,2,1,0:T(8,128)(2,1)S(1)}, bf16[1,10,32,1024]{3,2,1,0:T(8,128)(2,1)}, u32[]{:S(2)}, u32[]{:S(2)}) collective-permute-start(bf16[1,10,32,1024]{3,2,1,0:T(8,128)(2,1)S(1)} %advance.3), channel_id=1, source_target_pairs={{0,32},{32,0},{64,96},{96,64},{128,160},{160,128},{192,224},{224,1... | collective-permute-start | bytes 1966088 | tf_op jit(solution)/shard_map/ppermute | solution.py:19
  66.9 2.5 %copy-start.2 = (f32[4,10,8,32,128]{4,3,2,1,0:T(8,128)S(1)}, f32[4,10,8,32,128]{4,3,2,1,0:T(8,128)}, u32[]{:S(2)}) copy-start(f32[4,10,8,32,128]{4,3,2,1,0:T(8,128)} %copy-done) | copy-start | bytes 15728644

commit v3 on v2

--- a/solution.py
+++ b/solution.py
@@ -22,6 +22,10 @@
 def lane_roll(x, shift):
     shift = shift % LANES
     return x if shift == 0 else pltpu.roll(x, shift, x.ndim - 1)
+
+
+def in_hbm(x):
+    return pltpu.with_memory_space_constraint(x, pltpu.HBM)
 
 
 def pack_kernel(send_ref, u_ref, o_ref, sel_ref, face_ref):
@@ -93,9 +97,9 @@
             ],
         ),
         out_shape=jax.ShapeDtypeStruct((slots, fields * ROWS, LANES), bf16),
-        compiler_params=pltpu.CompilerParams(vmem_limit_bytes=32 << 20),
+        compiler_params=pltpu.CompilerParams(vmem_limit_bytes=16 << 20),
         name="pack_faces",
-    )(send, blocks)
+    )(send, in_hbm(blocks))
 
 
 def coefficients(ints_ref, vals_ref, blk, per_dev, fields):
@@ -151,14 +155,14 @@
     lax.fori_loop(0, tiles // 2, two_tiles, 0)
 
 
-def first_kernel(per_dev, ints_ref, vals_ref, u_ref, o_ref, rk_out_ref, sa_ref):
+def first_kernel(first, per_dev, ints_ref, vals_ref, u_ref, o_ref, rk_out_ref, sa_ref):
     _, fields, cells, plane = u_ref.shape
     tiles = plane // LANES
-    blk = pl.program_id(0)
+    blk = ints_ref[pl.program_id(0) + first]
     n, dt, minus, plus, rates = coefficients(ints_ref, vals_ref, blk, per_dev, fields)
     reaction = lambda f, e: vals_ref[3 * per_dev + fields + f * fields + e]
 
-    @pl.when(blk == 0)
+    @pl.when(pl.program_id(0) == 0)
     def _():
         zeros = jnp.zeros((fields, cells + 2 * PAD, LANES), f32)
         sa_ref[:, 0] = zeros
@@ -197,16 +201,18 @@
     substep(sa_ref, put, None, rk_out_ref[0], minus, plus, rates, fields, cells, tiles)
 
 
-def first_substep(ints, vals, blocks):
+def first_substep(ints, vals, blocks, first, count):
     per_dev, fields, cells, plane = blocks.shape
     tiles = plane // LANES
     size = fields * ROWS
     return pl.pallas_call(
-        functools.partial(first_kernel, per_dev),
+        functools.partial(first_kernel, first, per_dev),
         grid_spec=pltpu.PrefetchScalarGridSpec(
             num_scalar_prefetch=2,
-            grid=(per_dev,),
-            in_specs=[pl.BlockSpec((1, fields, cells, plane), lambda b, i, v: (b, 0, 0, 0))],
+            grid=(count,),
+            in_specs=[
+                pl.BlockSpec((1, fields, cells, plane), lambda b, i, v: (i[b + first], 0, 0, 0))
+            ],
             out_specs=[
                 pl.BlockSpec((1, fields, tiles, cells, LANES), lambda b, i, v: (b, 0, 0, 0, 0)),
                 pl.BlockSpec((1, size, 3 * size), lambda b, i, v: (b, 0, 0)),
@@ -214,15 +220,16 @@
             scratch_shapes=[pltpu.VMEM((fields, tiles + 2, cells + 2 * PAD, LANES), f32)],
         ),
         out_shape=[
-            jax.ShapeDtypeStruct((per_dev, fields, tiles, cells, LANES), f32),
-            jax.ShapeDtypeStruct((per_dev, size, 3 * size), bf16),
+            jax.ShapeDtypeStruct((count, fields, tiles, cells, LANES), f32),
+            jax.ShapeDtypeStruct((count, size, 3 * size), bf16),
         ],
-        compiler_params=pltpu.CompilerParams(vmem_limit_bytes=32 << 20),
+        compiler_params=pltpu.CompilerParams(vmem_limit_bytes=16 << 20),
         name="first_substep",
-    )(ints, vals, blocks)
-
-
-def advance_kernel(first, per_dev, ints_ref, vals_ref, s_ref, rk_ref, arr_ref, o_ref, sa_ref, sb_ref, e_ref):
+    )(ints, vals, in_hbm(blocks))
+
+
+def advance_kernel(first, per_dev, ints_ref, vals_ref, s_ref, rk_ref, arr_ref, *rest):
+    o_ref, sa_ref, sb_ref, e_ref = rest[-4:]
     _, fields, tiles, cells, _ = s_ref.shape
     groups = LANES // cells
     blk = ints_ref[pl.program_id(0) + first]
@@ -321,35 +328,34 @@
         finish(sb_ref)
 
 
-def advance(ints, vals, started, own, arrived, plane, first, count, slots_out):
-    per_dev, fields, tiles, cells, _ = started.shape
+def advance(ints, vals, started, own, arrived, plane, first, per_dev, slots, out_at, into=None):
+    count, fields, tiles, cells, _ = started.shape
     padded = (fields, tiles + 2, cells + 2 * PAD, LANES)
     shape = (1, fields, cells, plane)
-    if slots_out == 1:
-        out_map = lambda b, i, v: (0, 0, 0, 0)
-    else:
-        out_map = lambda b, i, v: (i[b + first], 0, 0, 0)
+    whole = [] if into is None else [into]
     return pl.pallas_call(
         functools.partial(advance_kernel, first, per_dev),
         grid_spec=pltpu.PrefetchScalarGridSpec(
             num_scalar_prefetch=2,
             grid=(count,),
             in_specs=[
-                pl.BlockSpec((1,) + started.shape[1:], lambda b, i, v: (i[b + first], 0, 0, 0, 0)),
-                pl.BlockSpec((1,) + own.shape[1:], lambda b, i, v: (i[b + first], 0, 0)),
+                pl.BlockSpec((1,) + started.shape[1:], lambda b, i, v: (b, 0, 0, 0, 0)),
+                pl.BlockSpec((1,) + own.shape[1:], lambda b, i, v: (b, 0, 0)),
                 pl.BlockSpec(arrived.shape, lambda b, i, v: (0, 0, 0)),
-            ],
-            out_specs=pl.BlockSpec(shape, out_map),
+            ]
+            + [pl.BlockSpec(memory_space=pl.ANY) for _ in whole],
+            out_specs=pl.BlockSpec(shape, lambda b, i, v: (i[b + out_at], 0, 0, 0)),
             scratch_shapes=[
                 pltpu.VMEM(padded, f32),
                 pltpu.VMEM(padded, f32),
                 pltpu.VMEM((fields, tiles, cells, LANES), f32),
             ],
         ),
-        out_shape=jax.ShapeDtypeStruct((slots_out, fields, cells, plane), bf16),
-        compiler_params=pltpu.CompilerParams(vmem_limit_bytes=40 << 20),
+        out_shape=jax.ShapeDtypeStruct((slots, fields, cells, plane), bf16),
+        input_output_aliases={} if into is None else {5: 0},
+        compiler_params=pltpu.CompilerParams(vmem_limit_bytes=16 << 20),
         name="advance",
-    )(ints, vals, started, own, arrived)
+    )(ints, vals, started, own, arrived, *whole)
 
 
 def plan(wanted, my_index, per_dev):
@@ -399,16 +405,49 @@
     rest = jnp.arange(per_dev, dtype=jnp.int32)
     rest = jnp.where(rest == 0, slot_here, rest - (rest <= slot_here))
     ints = jnp.concatenate([rest, own_levels, lookup, coarse.reshape(-1)])
-    vals = jnp.concatenate(
-        [block_velocity[0].astype(f32).reshape(-1), diffusivity, reaction_matrix.reshape(-1)]
-    )
-    started, own = first_substep(ints, vals, blocks)
-    departing = advance(ints, vals, started, own, arrived, plane, 0, 1, 1)
-    coming = departing
-    for bit_no in range(lax.axis_size("gx").bit_length() - 1):
-        coming = jnp.where(bit_here == bit_no, swapped(departing, "gx", bit_no), coming)
-    stay = advance(ints, vals, started, own, arrived, plane, 1, per_dev - 1, per_dev)
-    result = lax.dynamic_update_slice_in_dim(stay, coming, slot_here, 0)
+    speeds = block_velocity[0]
+    vals = jnp.concatenate([speeds.astype(f32).reshape(-1), diffusivity, reaction_matrix.reshape(-1)])
+    pick = lambda x, size: lax.dynamic_slice_in_dim(x.reshape(-1), slot_here * size, size, 0)
+
+    facts = jnp.concatenate(
+        [pick(own_levels, 1).astype(bf16), pick(coarse, 6).astype(bf16), pick(speeds, 3)]
+    )
+    bits = range(lax.axis_size("gx").bit_length() - 1)
+
+    def trade(x):
+        coming = x
+        for bit_no in bits:
+            coming = jnp.where(bit_here == bit_no, swapped(x, "gx", bit_no), coming)
+        return coming
+
+    departing = lax.dynamic_slice_in_dim(blocks, slot_here, 1, 0).reshape(fields * cells, plane)
+    label = jnp.broadcast_to(jnp.pad(facts, (0, plane - facts.shape[0]))[None], (16, plane))
+    coming = trade(jnp.concatenate([departing, label], axis=0))
+    facts = coming[fields * cells]
+    traded_ints = jnp.concatenate(
+        [
+            jnp.zeros((1,), jnp.int32),
+            facts[0:1].astype(jnp.int32),
+            jnp.arange(6, dtype=jnp.int32),
+            facts[1:7].astype(jnp.int32),
+            slot_here[None],
+        ]
+    )
+    traded_vals = jnp.concatenate(
+        [facts[7:10].astype(f32), diffusivity, reaction_matrix.reshape(-1)]
+    )
+
+    stay = first_substep(ints, vals, blocks, 1, per_dev - 1)
+    coming, stay = lax.optimization_barrier((coming, stay))
+    traded = first_substep(
+        traded_ints, traded_vals, coming[: fields * cells].reshape(1, fields, cells, plane), 0, 1
+    )
+    arrived, traded, stay = lax.optimization_barrier((arrived, traded, stay))
+    layers = trade(jnp.take(arrived, pick(lookup, 6), axis=0))
+    result = advance(ints, vals, *stay, arrived, plane, 1, per_dev, per_dev, 1)
+    result = advance(
+        traded_ints, traded_vals, *traded, layers, plane, 0, 1, per_dev, 14, into=result
+    )
     return result[None]
 
 

time: 95 us -> 100 us (1.053)
  the two profiles are of different devices: /device:TPU:32 before, /device:TPU:49 now
where the time goes in v3:
time: 100 us; the launch traced here: 98.7 us
  Pallas kernels  46.9 us (47%)
  starting transfers between devices  20.5 us (20%)
  waiting for transfers between devices  16.5 us (16%)
  local copies, waits for them, and re-layouts  8.52 us (9%)
  other arithmetic  4.01 us (4%)
  between operations  2.21 us (2%)
    pallas_call x2, Pallas kernels, advance(): pl.pallas_call(functools.partial(advance_kernel, first, per_dev), grid_sp...  29.7 us
    ppermute x6, waiting for transfers between devices, swapped(): lax.ppermute(x, axis, [(i, i ^ 1 << bit) for i in range(lax.axis_size(axi...  16.5 us
    pallas_call x2, Pallas kernels, first_substep(): pl.pallas_call(functools.partial(first_kernel, first, per_dev), grid_spec...  11.4 us
    all_to_all x1, starting transfers between devices, local(): lax.all_to_all(outgoing, ('gy', 'gz'), split_axis=0, concat_axis=0, tiled...  10.8 us
    ppermute x6, starting transfers between devices, swapped(): lax.ppermute(x, axis, [(i, i ^ 1 << bit) for i in range(lax.axis_size(axi...  9.73 us
    pallas_call x1, Pallas kernels, pack_faces(): pl.pallas_call(pack_kernel, grid_spec=pltpu.PrefetchScalarGridSpec(num_sc...  5.75 us
    unnamed x15, local copies, waits for them, and re-layouts  4.09 us
  transfers between devices with their start and end apart: 7, of which 2 were waited for; matrix products, arithmetic and copies ran while one was open for 6% of the time, Pallas kernels for 34%

profile of v3, /device:TPU:49, one launch (start us, length us, event | category | flops | bytes accessed | tf_op | source)
XLA Modules:
  0.0 98.7 jit_solution(6732353874952382370)
XLA Ops:
  0.3 0.7 select_reduce_fusion.2
  1.7 5.7 %pack_faces.1 = bf16[64,80,128]{2,1,0:T(8,128)(2,1)} custom-call(s32[64]{0:T(128)S(1)} %reshape.228.send_ref, bf16[4,10,32,1024]{3,2,1,0:T(8,128)(2,1)} %bitcast.45), custom_call_target="tpu_custom_call" | custom-call | tf_op jit(solution)/shard_map/pack_faces/pallas_call | solution.py:87
  7.5 10.8 %all-to-all-start = ((bf16[64,80,128]{2,1,0:T(8,128)(2,1)}), bf16[64,80,128]{2,1,0:T(8,128)(2,1)S(1)}, u32[]{:S(2)}, u32[]{:S(2)}) async-start(bf16[64,80,128]{2,1,0:T(8,128)(2,1)} %pack_faces.1), calls=%async_computation | async-start | bytes 2621440 | tf_op jit(solution)/shard_map/all_to_all | solution.py:397
  19.4 0.6 fusion.25
  20.4 0.7 fusion.16
  21.1 1.2 %constant_dynamic-slice_fusion.3 = bf16[1,1,10,32,1024]{4,3,2,1,0:T(8,128)(2,1)S(1)} fusion(bf16[1,4,10,32,1024]{4,3,2,1,0:T(8,128)(2,1)} %param.8, s32[]{:T(128)S(6)} %select_n.153), kind=kLoop, calls=%fused_computation.60 | loop fusion | bytes 1310724 | tf_op jit(solution)/shard_map/dynamic_slice | solution.py:423
  22.5 1.9 %collective-permute-start.1 = (bf16[336,1024]{1,0:T(8,128)(2,1)S(1)}, bf16[336,1024]{1,0:T(8,128)(2,1)}, u32[]{:S(2)}, u32[]{:S(2)}) collective-permute-start(bf16[336,1024]{1,0:T(8,128)(2,1)S(1)} %pad_maximum_fusion), channel_id=1, source_target_pairs={{0,64},{32,96},{64,0},{96,32},{128,192},{160,224},{192,128},{224,1... | collective-permute-start | bytes 2064392 | tf_op jit(solution)/shard_map/ppermute | solution.py:19
  24.4 1.8 %collective-permute-start.2 = (bf16[336,1024]{1,0:T(8,128)(2,1)S(1)}, bf16[336,1024]{1,0:T(8,128)(2,1)}, u32[]{:S(2)}, u32[]{:S(2)}) collective-permute-start(bf16[336,1024]{1,0:T(8,128)(2,1)S(1)} %pad_maximum_fusion), channel_id=1, source_target_pairs={{0,32},{32,0},{64,96},{96,64},{128,160},{160,128},{192,224},{224,1... | collective-permute-start | bytes 2064392 | tf_op jit(solution)/shard_map/ppermute | solution.py:19
  26.2 0.2 fusion.1
  27.3 7.7 %first_substep.2 = (f32[3,10,8,32,128]{4,3,2,1,0:T(8,128)S(1)}, bf16[3,80,240]{2,1,0:T(8,128)(2,1)S(1)}) custom-call(s32[56]{0:T(128)S(1)} %pad_add_fusion.1.ints_ref, f32[122]{0:T(128)S(1)} %pad_maximum_fusion.2.vals_ref, bf16[4,10,32,1024]{3,2,1,0:T(8,128)(2,1)} %bitcast.46), custom_call_target="tpu_custom_call" | custom-call | tf_op jit(solution)/shard_map/first_substep/pallas_call | solution.py:208
  35.0 1.8 %copy-done = f32[3,10,8,32,128]{4,3,2,1,0:T(8,128)} copy-done((f32[3,10,8,32,128]{4,3,2,1,0:T(8,128)}, f32[3,10,8,32,128]{4,3,2,1,0:T(8,128)S(1)}, u32[]{:S(2)}) %copy-start) | copy-done | bytes 3932184
  37.0 2.7 %collective-permute-done = bf16[336,1024]{1,0:T(8,128)(2,1)S(1)} collective-permute-done((bf16[336,1024]{1,0:T(8,128)(2,1)S(1)}, bf16[336,1024]{1,0:T(8,128)(2,1)S(1)}, u32[]{:S(2)}, u32[]{:S(2)}) %collective-permute-start) | collective-permute-done | bytes 688160 | tf_op jit(solution)/shard_map/ppermute | solution.py:19
  39.6 13.8 %collective-permute-done.1 = bf16[336,1024]{1,0:T(8,128)(2,1)} collective-permute-done((bf16[336,1024]{1,0:T(8,128)(2,1)S(1)}, bf16[336,1024]{1,0:T(8,128)(2,1)}, u32[]{:S(2)}, u32[]{:S(2)}) %collective-permute-start.1) | collective-permute-done | bytes 688160 | tf_op jit(solution)/shard_map/ppermute | solution.py:19
  53.5 0.5 select_select_fusion
  54.0 0.6 slice.25
  54.6 0.9 slice.22
  56.4 3.7 %first_substep.3 = (f32[1,10,8,32,128]{4,3,2,1,0:T(8,128)S(1)}, bf16[1,80,240]{2,1,0:T(8,128)(2,1)S(1)}) custom-call(s32[15]{0:T(128)S(1)} %concatenate.20.ints_ref, f32[113]{0:T(128)S(1)} %pad_maximum_fusion.1.vals_ref, bf16[1,10,32,1024]{3,2,1,0:T(8,128)(2,1)} %bitcast.49), custom_call_target="tpu_custom_call" | custom-call | tf_op jit(solution)/shard_map/first_substep/pallas_call | solution.py:208
  60.2 0.6 gather_fusion
  60.8 1.5 %collective-permute-start.3 = (bf16[6,80,128]{2,1,0:T(8,128)(2,1)S(1)}, bf16[6,80,128]{2,1,0:T(8,128)(2,1)S(1)}, u32[]{:S(2)}, u32[]{:S(2)}) collective-permute-start(bf16[6,80,128]{2,1,0:T(8,128)(2,1)S(1)} %broadcast_select_fusion), channel_id=1, source_target_pairs={{0,128},{32,160},{64,192},{96,224},{128,0},{160,32},{192,64},{224,... | collective-permute-start | bytes 368648 | tf_op jit(solution)/shard_map/ppermute | solution.py:19
  62.3 1.7 %collective-permute-start.4 = (bf16[6,80,128]{2,1,0:T(8,128)(2,1)S(1)}, bf16[6,80,128]{2,1,0:T(8,128)(2,1)S(1)}, u32[]{:S(2)}, u32[]{:S(2)}) collective-permute-start(bf16[6,80,128]{2,1,0:T(8,128)(2,1)S(1)} %broadcast_select_fusion), channel_id=1, source_target_pairs={{0,64},{32,96},{64,0},{96,32},{128,192},{160,224},{192,128},{224,1... | collective-permute-start | bytes 368648 | tf_op jit(solution)/shard_map/ppermute | solution.py:19
  64.0 2.7 %collective-permute-start.5 = (bf16[6,80,128]{2,1,0:T(8,128)(2,1)S(1)}, bf16[6,80,128]{2,1,0:T(8,128)(2,1)S(1)}, u32[]{:S(2)}, u32[]{:S(2)}) collective-permute-start(bf16[6,80,128]{2,1,0:T(8,128)(2,1)S(1)} %broadcast_select_fusion), channel_id=1, source_target_pairs={{0,32},{32,0},{64,96},{96,64},{128,160},{160,128},{192,224},{224,1... | collective-permute-start | bytes 368648 | tf_op jit(solution)/shard_map/ppermute | solution.py:19
  66.7 2.1 %copy-done.1 = f32[3,10,8,32,128]{4,3,2,1,0:T(8,128)S(1)} copy-done((f32[3,10,8,32,128]{4,3,2,1,0:T(8,128)S(1)}, f32[3,10,8,32,128]{4,3,2,1,0:T(8,128)}, u32[]{:S(2)}) %copy-start.1) | copy-done | bytes 3932184
  68.8 21.6 %advance.2.rest_0_ = bf16[4,10,32,1024]{3,2,1,0:T(8,128)(2,1)} custom-call(s32[56]{0:T(128)S(1)} %pad_add_fusion.1.ints_ref, f32[122]{0:T(128)S(1)} %pad_maximum_fusion.2.vals_ref, f32[3,10,8,32,128]{4,3,2,1,0:T(8,128)S(1)} %copy-done.1, bf16[3,80,240]{2,1,0:T(8,128)(2,1)S(1)} %get-tuple-element.28.rk_ref, bf16[64,80,128]{2,1,0:T(8,128)(2,1)S(1)} %all-to-all-done.arr_ref), custom_call_target="tpu_custom_call" | custom-call | tf_op jit(solution)/shard_map/advance/pallas_call | solution.py:336
  90.6 8.1 %advance.3 = bf16[4,10,32,1024]{3,2,1,0:T(8,128)(2,1)} custom-call(s32[15]{0:T(128)S(1)} %concatenate.20.ints_ref, f32[113]{0:T(128)S(1)} %pad_maximum_fusion.1.vals_ref, f32[1,10,8,32,128]{4,3,2,1,0:T(8,128)S(1)} %get-tuple-element.24.s_ref, bf16[1,80,240]{2,1,0:T(8,128)(2,1)S(1)} %get-tuple-element.25.rk_ref, ...), custom_call_target="tpu_custom_call", output_to_operand_aliasing={{}: (5, {})} | custom-call | tf_op jit(solution)/shard_map/advance/pallas_call | solution.py:336
  (63 shorter events, 2.8 us)
Async XLA Ops:
  7.5 10.8 %copy-start.2 = (s32[1,128,6]{1,0,2:T(1,128)S(1)}, s32[1,128,6]{1,0,2:T(1,128)}, u32[]{:S(2)}) copy-start(s32[1,128,6]{1,0,2:T(1,128)} %param.13) | copy-start | bytes 9220
  7.5 10.9 %copy-start.6 = (s32[1,128]{1,0:T(1,128)S(1)}, s32[1,128]{1,0:T(1,128)}, u32[]{:S(2)}) copy-start(s32[1,128]{1,0:T(1,128)} %param.9) | copy-start | bytes 1540
  7.5 12.5 %copy-start.5 = (bf16[1,4,3]{2,1,0:T(4,128)(2,1)S(1)}, bf16[1,4,3]{2,1,0:T(4,128)(2,1)}, u32[]{:S(2)}) copy-start(bf16[1,4,3]{2,1,0:T(4,128)(2,1)} %param.10) | copy-start | bytes 76
  7.5 52.7 %all-to-all-start = ((bf16[64,80,128]{2,1,0:T(8,128)(2,1)}), bf16[64,80,128]{2,1,0:T(8,128)(2,1)S(1)}, u32[]{:S(2)}, u32[]{:S(2)}) async-start(bf16[64,80,128]{2,1,0:T(8,128)(2,1)} %pack_faces.1), calls=%async_computation | async-start | bytes 2621440 | tf_op jit(solution)/shard_map/all_to_all | solution.py:397
  20.3 6.7 %copy-start.3 = (f32[10,10]{1,0:T(8,128)S(1)}, f32[10,10]{1,0:T(8,128)}, u32[]{:S(2)}) copy-start(f32[10,10]{1,0:T(8,128)} %param.12) | copy-start | bytes 1204
  21.1 6.1 %copy-start.4 = (f32[10]{0:T(128)S(1)}, f32[10]{0:T(128)}, u32[]{:S(2)}) copy-start(f32[10]{0:T(128)} %param.11) | copy-start | bytes 124
  22.3 17.3 %collective-permute-start = (bf16[336,1024]{1,0:T(8,128)(2,1)S(1)}, bf16[336,1024]{1,0:T(8,128)(2,1)S(1)}, u32[]{:S(2)}, u32[]{:S(2)}) collective-permute-start(bf16[336,1024]{1,0:T(8,128)(2,1)S(1)} %pad_maximum_fusion), channel_id=1, source_target_pairs={{0,128},{32,160},{64,192},{96,224},{128,0},{160,32},{192,64},{224,... | collective-permute-start | bytes 2064392 | tf_op jit(solution)/shard_map/ppermute | solution.py:19
  22.5 31.0 %collective-permute-start.1 = (bf16[336,1024]{1,0:T(8,128)(2,1)S(1)}, bf16[336,1024]{1,0:T(8,128)(2,1)}, u32[]{:S(2)}, u32[]{:S(2)}) collective-permute-start(bf16[336,1024]{1,0:T(8,128)(2,1)S(1)} %pad_maximum_fusion), channel_id=1, source_target_pairs={{0,64},{32,96},{64,0},{96,32},{128,192},{160,224},{192,128},{224,1... | collective-permute-start | bytes 2064392 | tf_op jit(solution)/shard_map/ppermute | solution.py:19
  24.4 29.1 %collective-permute-start.2 = (bf16[336,1024]{1,0:T(8,128)(2,1)S(1)}, bf16[336,1024]{1,0:T(8,128)(2,1)}, u32[]{:S(2)}, u32[]{:S(2)}) collective-permute-start(bf16[336,1024]{1,0:T(8,128)(2,1)S(1)} %pad_maximum_fusion), channel_id=1, source_target_pairs={{0,32},{32,0},{64,96},{96,64},{128,160},{160,128},{192,224},{224,1... | collective-permute-start | bytes 2064392 | tf_op jit(solution)/shard_map/ppermute | solution.py:19
  35.0 1.9 %copy-start = (f32[3,10,8,32,128]{4,3,2,1,0:T(8,128)}, f32[3,10,8,32,128]{4,3,2,1,0:T(8,128)S(1)}, u32[]{:S(2)}) copy-start(f32[3,10,8,32,128]{4,3,2,1,0:T(8,128)S(1)} %get-tuple-element.27.s_ref) | copy-start | bytes 11796484
  60.8 29.6 %collective-permute-start.3 = (bf16[6,80,128]{2,1,0:T(8,128)(2,1)S(1)}, bf16[6,80,128]{2,1,0:T(8,128)(2,1)S(1)}, u32[]{:S(2)}, u32[]{:S(2)}) collective-permute-start(bf16[6,80,128]{2,1,0:T(8,128)(2,1)S(1)} %broadcast_select_fusion), channel_id=1, source_target_pairs={{0,128},{32,160},{64,192},{96,224},{128,0},{160,32},{192,64},{224,... | collective-permute-start | bytes 368648 | tf_op jit(solution)/shard_map/ppermute | solution.py:19
  62.3 28.2 %collective-permute-start.4 = (bf16[6,80,128]{2,1,0:T(8,128)(2,1)S(1)}, bf16[6,80,128]{2,1,0:T(8,128)(2,1)S(1)}, u32[]{:S(2)}, u32[]{:S(2)}) collective-permute-start(bf16[6,80,128]{2,1,0:T(8,128)(2,1)S(1)} %broadcast_select_fusion), channel_id=1, source_target_pairs={{0,64},{32,96},{64,0},{96,32},{128,192},{160,224},{192,128},{224,1... | collective-permute-start | bytes 368648 | tf_op jit(solution)/shard_map/ppermute | solution.py:19
  64.0 26.5 %collective-permute-start.5 = (bf16[6,80,128]{2,1,0:T(8,128)(2,1)S(1)}, bf16[6,80,128]{2,1,0:T(8,128)(2,1)S(1)}, u32[]{:S(2)}, u32[]{:S(2)}) collective-permute-start(bf16[6,80,128]{2,1,0:T(8,128)(2,1)S(1)} %broadcast_select_fusion), channel_id=1, source_target_pairs={{0,32},{32,0},{64,96},{96,64},{128,160},{160,128},{192,224},{224,1... | collective-permute-start | bytes 368648 | tf_op jit(solution)/shard_map/ppermute | solution.py:19
  66.7 2.1 %copy-start.1 = (f32[3,10,8,32,128]{4,3,2,1,0:T(8,128)S(1)}, f32[3,10,8,32,128]{4,3,2,1,0:T(8,128)}, u32[]{:S(2)}) copy-start(f32[3,10,8,32,128]{4,3,2,1,0:T(8,128)} %copy-done) | copy-start | bytes 11796484

commit v4 on v3

v4 whole, which is shorter than its diff:
```python
import functools

import jax
import jax.numpy as jnp
from jax import lax
from jax.experimental import pallas as pl
from jax.experimental.pallas import tpu as pltpu
from jax.sharding import PartitionSpec as P

f32 = jnp.float32
bf16 = jnp.bfloat16
dt_base = 0.05
LANES = 128
ROWS = 8
PAD = 8
LABEL = (16, LANES)


def swapped(x, axis, bit):
    return lax.ppermute(x, axis, [(i, i ^ 1 << bit) for i in range(lax.axis_size(axis))])


def lane_roll(x, shift):
    shift = shift % LANES
    return x if shift == 0 else pltpu.roll(x, shift, x.ndim - 1)


def lane_ids():
    return lax.broadcasted_iota(jnp.int32, (1, ROWS, LANES), 2)


def row_ids():
    return lax.broadcasted_iota(jnp.int32, (1, ROWS, LANES), 1)


def pack_kernel(send_ref, u_ref, o_ref, sel_ref, face_ref):
    blk = pl.program_id(0)
    _, fields, cells, plane = u_ref.shape
    groups = LANES // cells
    tiles = plane // LANES

    @pl.when(blk == 0)
    def _():
        row = lax.broadcasted_iota(jnp.int32, sel_ref.shape, 0)
        col = lax.broadcasted_iota(jnp.int32, sel_ref.shape, 1)
        high = col // LANES
        within = col % LANES
        r = within % cells
        b = within // cells
        source = (tiles * b + r) * cells + high * (cells - 1)
        sel_ref[...] = jnp.where((r < tiles) & (row == source), 1.0, 0.0).astype(bf16)

    lane = lane_ids()
    group = lane // cells
    at_row = row_ids()

    def put(face_no, value):
        face_ref[blk * 6 + face_no] = value.reshape(fields * ROWS, LANES).astype(bf16)

    for face_no, edge in ((0, 0), (1, cells - 1)):
        pieces = [
            u_ref[0, :, edge : edge + 1, pl.ds(LANES * t, LANES)].astype(f32)
            for t in range(tiles)
        ]
        natural = jnp.concatenate(pieces, axis=1)
        total = jnp.zeros((fields, ROWS, LANES), f32)
        for d in range(groups):
            moved = lane_roll(natural, cells * d)
            for b in range(groups):
                for half in range(tiles // groups):
                    r = groups * half + (b - d) % groups
                    t = (tiles // groups) * b + half
                    shift = (r - t) % ROWS
                    here = pltpu.roll(moved, shift, 1) if shift else moved
                    total = jnp.where((group == b) & (at_row == r), here, total)
        put(face_no, total)
    for face_no, tile, source in ((2, 0, 0), (3, tiles - 1, groups - 1)):
        strip = u_ref[0, :, :, pl.ds(LANES * tile, LANES)].astype(f32)
        total = jnp.zeros((fields, ROWS, LANES), f32)
        for b in range(groups):
            moved = lane_roll(strip[:, ROWS * b : ROWS * b + ROWS], cells * (b - source))
            total = jnp.where(group == b, moved, total)
        put(face_no, total)
    picked = jnp.dot(
        u_ref[0].reshape(fields * cells, plane), sel_ref[...], preferred_element_type=f32
    ).reshape(fields, cells, 2 * LANES)
    for face_no, high in ((4, 0), (5, 1)):
        total = jnp.zeros((fields, ROWS, LANES), f32)
        for b in range(groups):
            part = picked[:, ROWS * b : ROWS * b + ROWS, LANES * high : LANES * high + LANES]
            total = total + lane_roll(part, tiles * b)
        put(face_no, total)

    @pl.when(blk == pl.num_programs(0) - 1)
    def _():
        def copy(slot, carry):
            o_ref[slot] = face_ref[send_ref[slot]]
            return carry

        lax.fori_loop(0, o_ref.shape[0], copy, 0)


def in_hbm(x):
    return pltpu.with_memory_space_constraint(x, pltpu.HBM)


def pack_faces(blocks, send, slots):
    per_dev, fields, cells, plane = blocks.shape
    return pl.pallas_call(
        pack_kernel,
        grid_spec=pltpu.PrefetchScalarGridSpec(
            num_scalar_prefetch=1,
            grid=(per_dev,),
            in_specs=[pl.BlockSpec((1, fields, cells, plane), lambda b, s: (b, 0, 0, 0))],
            out_specs=pl.BlockSpec((slots, fields * ROWS, LANES), lambda b, s: (0, 0, 0)),
            scratch_shapes=[
                pltpu.VMEM((plane, 2 * LANES), bf16),
                pltpu.VMEM((per_dev * 6, fields * ROWS, LANES), bf16),
            ],
        ),
        out_shape=jax.ShapeDtypeStruct((slots, fields * ROWS, LANES), bf16),
        compiler_params=pltpu.CompilerParams(vmem_limit_bytes=16 << 20),
        name="pack_faces",
    )(send, in_hbm(blocks))


class Facts:
    def __init__(self, ints_ref, vals_ref, blk, per_dev, fields):
        self.lookup = lambda face: ints_ref[2 * per_dev + blk * 6 + face]
        self.coarse = lambda face: ints_ref[8 * per_dev + blk * 6 + face]
        self.reaction = lambda f, e: vals_ref[3 * per_dev + fields + f * fields + e]
        self.n = jnp.left_shift(jnp.int32(1), ints_ref[per_dev + blk])
        scale = self.n.astype(f32)
        self.dt = dt_base / scale
        adv = self.dt * scale
        dif = self.dt * scale * scale
        velocity = [vals_ref[blk * 3 + d] for d in range(3)]
        self.minus = [adv * jnp.maximum(v, 0.0) for v in velocity]
        self.plus = [-(adv * jnp.minimum(v, 0.0)) for v in velocity]
        self.rates = [dif * vals_ref[3 * per_dev + f] for f in range(fields)]


def own_matrix(facts, fields, write):
    outflow = sum(facts.minus) + sum(facts.plus)
    size = fields * ROWS
    ri = lax.broadcasted_iota(jnp.int32, (size, size), 0)
    ci = lax.broadcasted_iota(jnp.int32, (size, size), 1)
    matrix = jnp.zeros((size, size), f32)
    for f in range(fields):
        line = jnp.zeros((size, size), f32)
        for e in range(fields):
            term = facts.dt * facts.reaction(f, e)
            if e == f:
                term = term - (6.0 * facts.rates[f] + outflow)
            line = jnp.where(ci // ROWS == e, term, line)
        matrix = jnp.where(ri // ROWS == f, line, matrix)
    matrix = jnp.where(ri % ROWS == ci % ROWS, matrix, 0.0)
    high = matrix.astype(bf16)
    write(0, high)
    write(size, (matrix - high.astype(f32)).astype(bf16))
    write(2 * size, high)


def to_planes(load, state, cells, tiles):
    groups = LANES // cells
    group = lane_ids() // cells
    for it in range(cells // ROWS):
        for half in range(tiles // groups):
            source = [load((tiles // groups) * b + half, it) for b in range(groups)]
            shifted = []
            for d in range(groups):
                x = source[d % groups]
                for g in range(1, groups):
                    x = jnp.where(group == g, source[(g + d) % groups], x)
                shifted.append(lane_roll(x, cells * d))
            for jj in range(groups):
                out = shifted[(0 - jj) % groups]
                for b in range(1, groups):
                    out = jnp.where(group == b, shifted[(b - jj) % groups], out)
                state[:, groups * half + jj + 1, pl.ds(PAD + ROWS * it, ROWS), :] = out


def from_planes(state, store, cells, tiles):
    groups = LANES // cells
    group = lane_ids() // cells
    for it in range(cells // 16):
        for half in range(tiles // groups):
            outs = [[] for _ in range(groups)]
            for sub in range(2):
                rows = pl.ds(PAD + 16 * it + ROWS * sub, ROWS)
                source = [state[:, groups * half + jj + 1, rows, :] for jj in range(groups)]
                shifted = []
                for d in range(groups):
                    x = source[(0 - d) % groups]
                    for g in range(1, groups):
                        x = jnp.where(group == g, source[(g - d) % groups], x)
                    shifted.append(lane_roll(x, -cells * d))
                for b in range(groups):
                    out = shifted[b % groups]
                    for jj in range(1, groups):
                        out = jnp.where(group == jj, shifted[(b - jj) % groups], out)
                    outs[b].append(out)
            for b in range(groups):
                both = jnp.concatenate(outs[b], axis=1).astype(bf16)
                store((tiles // groups) * b + half, it, both)


def wrap_planes(state, side_ref, cells, tiles):
    lane = lane_ids()
    for it in range(cells // ROWS):
        rows = pl.ds(PAD + ROWS * it, ROWS)
        side = 0.0 if side_ref is None else side_ref[:, pl.ds(ROWS * it, ROWS), :]
        state[:, 0, rows, :] = jnp.where(lane < cells, side, lane_roll(state[:, tiles, rows, :], cells))
        state[:, tiles + 1, rows, :] = jnp.where(
            lane >= LANES - cells, side, lane_roll(state[:, 1, rows, :], -cells)
        )


def substep(src, put, edge_ref, own, facts, fields, cells, tiles):
    lane = lax.broadcasted_iota(jnp.int32, (ROWS, LANES), 1)
    k_first = lane % cells == 0
    k_last = lane % cells == cells - 1
    minus, plus, rates = facts.minus, facts.plus, facts.rates

    def two_tiles(pair, carry):
        for it in range(cells // ROWS):
            row = PAD + ROWS * it
            centre = [
                [src[f, 2 * pair + 1 + q, pl.ds(row, ROWS), :] for f in range(fields)]
                for q in range(2)
            ]
            both = jnp.concatenate([jnp.concatenate(c, axis=0) for c in centre], axis=1)
            both_high = both.astype(bf16)
            both_low = (both - both_high.astype(f32)).astype(bf16)
            stacked = jnp.concatenate([both_high, both_high, both_low], axis=0)
            mixed = jnp.dot(own, stacked, preferred_element_type=f32)
            for q in range(2):
                t = 2 * pair + q
                for f in range(fields):
                    c = centre[q][f]
                    minus_x = src[f, t + 1, pl.ds(row - 1, ROWS), :]
                    plus_x = src[f, t + 1, pl.ds(row + 1, ROWS), :]
                    minus_y = src[f, t, pl.ds(row, ROWS), :]
                    plus_y = src[f, t + 2, pl.ds(row, ROWS), :]
                    edge = 0.0 if edge_ref is None else edge_ref[f, t, pl.ds(ROWS * it, ROWS), :]
                    minus_z = jnp.where(k_first, edge, lane_roll(c, 1))
                    plus_z = jnp.where(k_last, edge, lane_roll(c, -1))
                    near = (rates[f] + minus[0]) * minus_x + (rates[f] + plus[0]) * plus_x
                    near += (rates[f] + minus[1]) * minus_y + (rates[f] + plus[1]) * plus_y
                    near += (rates[f] + minus[2]) * minus_z + (rates[f] + plus[2]) * plus_z
                    own_terms = mixed[ROWS * f : ROWS * f + ROWS, LANES * q : LANES * q + LANES]
                    put(f, t, it, near + (c + own_terms))
        return carry

    lax.fori_loop(0, tiles // 2, two_tiles, 0)


def first_kernel(first, per_dev, ints_ref, vals_ref, u_ref, o_ref, rk_out_ref, sa_ref):
    _, fields, cells, plane = u_ref.shape
    tiles = plane // LANES
    facts = Facts(ints_ref, vals_ref, ints_ref[pl.program_id(0) + first], per_dev, fields)

    @pl.when(pl.program_id(0) == 0)
    def _():
        sa_ref[:, :, 0:PAD] = jnp.zeros((fields, tiles + 2, PAD, LANES), f32)
        sa_ref[:, :, PAD + cells :] = jnp.zeros((fields, tiles + 2, PAD, LANES), f32)

    load_block(u_ref, sa_ref, cells, tiles)
    wrap_planes(sa_ref, None, cells, tiles)

    def write(at, value):
        rk_out_ref[0, :, at : at + value.shape[1]] = value

    own_matrix(facts, fields, write)

    def put(f, t, it, value):
        o_ref[0, f, t, pl.ds(ROWS * it, ROWS), :] = value

    substep(sa_ref, put, None, rk_out_ref[0], facts, fields, cells, tiles)


def load_block(u_ref, state, cells, tiles):
    whole = {}

    def load(t, it):
        if (t, it // 2) not in whole:
            whole[t, it // 2] = u_ref[
                0, :, pl.ds(16 * (it // 2), 16), pl.ds(LANES * t, LANES)
            ].astype(f32)
        return whole[t, it // 2][:, ROWS * (it % 2) : ROWS * (it % 2) + ROWS]

    to_planes(load, state, cells, tiles)


def first_substep(ints, vals, blocks, first, count):
    per_dev, fields, cells, plane = blocks.shape
    tiles = plane // LANES
    size = fields * ROWS
    return pl.pallas_call(
        functools.partial(first_kernel, first, per_dev),
        grid_spec=pltpu.PrefetchScalarGridSpec(
            num_scalar_prefetch=2,
            grid=(count,),
            in_specs=[
                pl.BlockSpec((1, fields, cells, plane), lambda b, i, v: (i[b + first], 0, 0, 0))
            ],
            out_specs=[
                pl.BlockSpec((1, fields, tiles, cells, LANES), lambda b, i, v: (b, 0, 0, 0, 0)),
                pl.BlockSpec((1, size, 3 * size), lambda b, i, v: (b, 0, 0)),
            ],
            scratch_shapes=[pltpu.VMEM((fields, tiles + 2, cells + 2 * PAD, LANES), f32)],
        ),
        out_shape=[
            pltpu.HBM((count, fields, tiles, cells, LANES), f32),
            jax.ShapeDtypeStruct((count, size, 3 * size), bf16),
        ],
        compiler_params=pltpu.CompilerParams(vmem_limit_bytes=16 << 20),
        name="first_substep",
    )(ints, vals, in_hbm(blocks))


def place_layers(layer_of, facts, sa_ref, sb_ref, e_ref, side_ref, s_ref, fields, cells, tiles):
    groups = LANES // cells
    lane = lane_ids()
    at_row = row_ids()
    k_first = lane % cells == 0
    k_last = lane % cells == cells - 1
    minus, plus = facts.minus, facts.plus
    odd_lane = lane % 2 == 1
    odd_row = at_row % 2 == 1

    def face(face_no):
        layer = layer_of(face_no).astype(f32).reshape(fields, ROWS, LANES)
        mean = layer + jnp.where(odd_lane, lane_roll(layer, 1), lane_roll(layer, -1))
        mean = mean + jnp.where(odd_row, pltpu.roll(mean, 1, 1), pltpu.roll(mean, ROWS - 1, 1))
        return jnp.where(facts.coarse(face_no) > 0, mean * 0.25, layer)

    states = (sa_ref, sb_ref)
    rate = jnp.concatenate([jnp.full((1, ROWS, LANES), x, f32) for x in facts.rates], axis=0)

    low, high = face(4), lane_roll(face(5), cells - 1)
    weight = jnp.where(k_first, rate + minus[2], jnp.where(k_last, rate + plus[2], 0.0))
    for it in range(cells // ROWS):
        rows = pl.ds(ROWS * it, ROWS)
        for t in range(tiles):
            at = tiles * it + t
            edge = lane_roll(jnp.where(lane % cells == at, low, high), -at)
            e_ref[:, t, rows, :] = edge
            if s_ref is not None:
                sa_ref[:, t + 1, pl.ds(PAD + ROWS * it, ROWS), :] = (
                    s_ref[0, :, t, rows, :] + weight * edge
                )

    low, high = face(2), face(3)
    for it in range(cells // ROWS):
        rows = pl.ds(PAD + ROWS * it, ROWS)
        side = jnp.where(
            lane < cells,
            lane_roll(low, -cells * it),
            lane_roll(high, cells * (groups - 1 - it)),
        )
        side_ref[:, pl.ds(ROWS * it, ROWS), :] = side
        if s_ref is not None:
            sa_ref[:, 1, rows, :] += jnp.where(lane < cells, (rate + minus[1]) * side, 0.0)
            sa_ref[:, tiles, rows, :] += jnp.where(
                lane >= LANES - cells, (rate + plus[1]) * side, 0.0
            )

    low, high = face(0), face(1)
    low_part = (rate + minus[0]) * low
    high_part = (rate + plus[0]) * high
    for t in range(tiles):
        if s_ref is not None:
            sa_ref[:, t + 1, PAD : PAD + 1, :] += low_part[:, t : t + 1, :]
            sa_ref[:, t + 1, PAD + cells - 1 : PAD + cells, :] += high_part[:, t : t + 1, :]
        for state in states:
            state[:, t + 1, PAD - 1 : PAD, :] = low[:, t : t + 1, :]
            state[:, t + 1, PAD + cells : PAD + cells + 1, :] = high[:, t : t + 1, :]
    wrap_planes(sa_ref, side_ref, cells, tiles)


def make_step(own, facts, e_ref, side_ref, fields, cells, tiles):
    def step(src, dst):
        def put(f, t, it, value):
            dst[f, t + 1, pl.ds(PAD + ROWS * it, ROWS), :] = value

        substep(src, put, e_ref, own, facts, fields, cells, tiles)
        wrap_planes(dst, side_ref, cells, tiles)

    return step


def make_finish(o_ref, cells, tiles):
    def finish(src):
        def store(t, it, value):
            o_ref[0, :, pl.ds(16 * it, 16), pl.ds(LANES * t, LANES)] = value

        from_planes(src, store, cells, tiles)

    return finish


def stay_kernel(first, per_dev, ints_ref, vals_ref, s_ref, rk_ref, arr_ref, o_ref, sa_ref, sb_ref, e_ref, side_ref):
    _, fields, tiles, cells, _ = s_ref.shape
    facts = Facts(ints_ref, vals_ref, ints_ref[pl.program_id(0) + first], per_dev, fields)
    place_layers(
        lambda face_no: arr_ref[facts.lookup(face_no)],
        facts, sa_ref, sb_ref, e_ref, side_ref, s_ref, fields, cells, tiles,
    )
    step = make_step(rk_ref[0], facts, e_ref, side_ref, fields, cells, tiles)
    finish = make_finish(o_ref, cells, tiles)

    @pl.when(facts.n == 1)
    def _():
        finish(sa_ref)

    @pl.when(facts.n > 1)
    def _():
        def two(i, carry):
            step(sa_ref, sb_ref)
            step(sb_ref, sa_ref)
            return carry

        lax.fori_loop(0, (facts.n - 2) // 2, two, 0)
        step(sa_ref, sb_ref)
        finish(sb_ref)


def state_scratch(fields, cells, tiles):
    padded = (fields, tiles + 2, cells + 2 * PAD, LANES)
    return [
        pltpu.VMEM(padded, f32),
        pltpu.VMEM(padded, f32),
        pltpu.VMEM((fields, tiles, cells, LANES), f32),
        pltpu.VMEM((fields, cells, LANES), f32),
    ]


def advance_stay(ints, vals, started, own, arrived, plane, first, per_dev):
    count, fields, tiles, cells, _ = started.shape
    shape = (1, fields, cells, plane)
    return pl.pallas_call(
        functools.partial(stay_kernel, first, per_dev),
        grid_spec=pltpu.PrefetchScalarGridSpec(
            num_scalar_prefetch=2,
            grid=(count,),
            in_specs=[
                pl.BlockSpec((1,) + started.shape[1:], lambda b, i, v: (b, 0, 0, 0, 0)),
                pl.BlockSpec((1,) + own.shape[1:], lambda b, i, v: (b, 0, 0)),
                pl.BlockSpec(arrived.shape, lambda b, i, v: (0, 0, 0)),
            ],
            out_specs=pl.BlockSpec(shape, lambda b, i, v: (i[b + first], 0, 0, 0)),
            scratch_shapes=state_scratch(fields, cells, tiles),
        ),
        out_shape=jax.ShapeDtypeStruct((per_dev, fields, cells, plane), bf16),
        compiler_params=pltpu.CompilerParams(vmem_limit_bytes=20 << 20),
        name="advance_stay",
    )(ints, vals, in_hbm(started), own, arrived)


def traded_kernel(choices, ints_ref, vals_ref, *refs):
    raw_refs, layer_refs, refs = refs[:choices], refs[choices : 2 * choices], refs[2 * choices + 1 :]
    o_ref, sa_ref, sb_ref, e_ref, side_ref, rk_ref, raw_ref, layer_ref, sems = refs
    _, fields, cells, plane = raw_ref.shape
    tiles = plane // LANES
    facts = Facts(ints_ref, vals_ref, 0, 1, fields)
    choice = ints_ref[15]
    for c in range(choices):

        @pl.when(choice == c)
        def _():
            raw_copy = pltpu.make_async_copy(raw_refs[c], raw_ref, sems.at[0])
            layer_copy = pltpu.make_async_copy(layer_refs[c], layer_ref, sems.at[1])
            raw_copy.start()
            layer_copy.start()
            raw_copy.wait()
            layer_copy.wait()

    def write(at, value):
        rk_ref[:, at : at + value.shape[1]] = value

    own_matrix(facts, fields, write)
    load_block(raw_ref, sa_ref, cells, tiles)
    place_layers(
        lambda face_no: layer_ref[face_no],
        facts, sa_ref, sb_ref, e_ref, side_ref, None, fields, cells, tiles,
    )
    step = make_step(rk_ref[...], facts, e_ref, side_ref, fields, cells, tiles)
    finish = make_finish(o_ref, cells, tiles)

    @pl.when(facts.n == 1)
    def _():
        step(sa_ref, sb_ref)
        finish(sb_ref)

    @pl.when(facts.n > 1)
    def _():
        def two(i, carry):
            step(sa_ref, sb_ref)
            step(sb_ref, sa_ref)
            return carry

        lax.fori_loop(0, facts.n // 2, two, 0)
        finish(sa_ref)


def advance_traded(ints, vals, raws, layers, into):
    per_dev, fields, cells, plane = into.shape
    tiles = plane // LANES
    choices = len(raws)
    size = fields * ROWS
    anywhere = pl.BlockSpec(memory_space=pl.ANY)
    return pl.pallas_call(
        functools.partial(traded_kernel, choices),
        grid_spec=pltpu.PrefetchScalarGridSpec(
            num_scalar_prefetch=2,
            grid=(1,),
            in_specs=[anywhere] * (2 * choices + 1),
            out_specs=pl.BlockSpec((1, fields, cells, plane), lambda b, i, v: (i[14], 0, 0, 0)),
            scratch_shapes=state_scratch(fields, cells, tiles)
            + [
                pltpu.VMEM((size, 3 * size), bf16),
                pltpu.VMEM((1, fields, cells, plane), bf16),
                pltpu.VMEM((6, size, LANES), bf16),
                pltpu.SemaphoreType.DMA((2,)),
            ],
        ),
        out_shape=jax.ShapeDtypeStruct(into.shape, bf16),
        input_output_aliases={2 + 2 * choices: 0},
        compiler_params=pltpu.CompilerParams(vmem_limit_bytes=20 << 20),
        name="advance_traded",
    )(ints, vals, *raws, *layers, into)


def plan(wanted, my_index, per_dev):
    peers, requests = wanted.shape
    at = lax.broadcasted_iota(jnp.int32, wanted.shape, 1)
    source_dev = wanted // per_dev
    code = wanted % per_dev * 6 + jnp.bitwise_xor(at % 6, 1)
    key = at * 64 + code
    match = source_dev == my_index
    first = jnp.min(jnp.where(match, key, 64 * requests), axis=1) % 64
    second = jnp.max(jnp.where(match, key, 0), axis=1) % 64
    send = jnp.stack([first, second], axis=1).reshape(2 * peers)
    mine = lax.dynamic_slice_in_dim(wanted, my_index, 1, 0)[0]
    my_source = mine // per_dev
    order = jnp.arange(requests, dtype=jnp.int32)
    repeated = (my_source[:, None] == my_source[None, :]) & (order[None, :] < order[:, None])
    lookup = my_source * 2 + jnp.any(repeated, axis=1).astype(jnp.int32)
    return send, mine, lookup


def local(
    block_state,
    block_level,
    block_velocity,
    diffusivity,
    reaction_matrix,
    ghost_source,
    swap_bit,
    swap_slot,
):
    blocks = block_state[0]
    per_dev, fields, cells, plane = blocks.shape
    peers = lax.axis_size(("gy", "gz"))
    my_index = lax.axis_index(("gy", "gz"))
    levels = block_level[0]
    wanted = ghost_source[0].reshape(peers, per_dev * 6)
    send, mine, lookup = plan(wanted, my_index, per_dev)
    outgoing = pack_faces(blocks, send, 2 * peers)
    arrived = lax.all_to_all(outgoing, ("gy", "gz"), split_axis=0, concat_axis=0, tiled=True)

    own_levels = lax.dynamic_slice_in_dim(levels, my_index * per_dev, per_dev, 0)
    known = mine[:, None] == jnp.arange(levels.shape[0], dtype=jnp.int32)[None, :]
    source_levels = jnp.sum(jnp.where(known, levels[None, :], 0), axis=1)
    coarse = (source_levels.reshape(per_dev, 6) != own_levels[:, None]).astype(jnp.int32)
    bit_here = swap_bit[0, 0, 0]
    slot_here = swap_slot[0, 0, 0]
    rest = jnp.arange(per_dev, dtype=jnp.int32)
    rest = jnp.where(rest == 0, slot_here, rest - (rest <= slot_here))
    ints = jnp.concatenate([rest, own_levels, lookup, coarse.reshape(-1)])
    speeds = block_velocity[0]
    vals = jnp.concatenate([speeds.astype(f32).reshape(-1), diffusivity, reaction_matrix.reshape(-1)])
    pick = lambda x, size: lax.dynamic_slice_in_dim(x.reshape(-1), slot_here * size, size, 0)
    bits = range(lax.axis_size("gx").bit_length() - 1)
    offers = lambda x: [x] + [swapped(x, "gx", bit_no) for bit_no in bits]

    raws = offers(lax.dynamic_slice_in_dim(blocks, slot_here, 1, 0))
    label = jnp.concatenate(
        [pick(own_levels, 1).astype(bf16), pick(coarse, 6).astype(bf16), pick(speeds, 3)]
    )
    label = jnp.broadcast_to(jnp.pad(label, (0, LABEL[1] - label.shape[0]))[None], LABEL)
    label, *others = offers(label)
    for bit_no in bits:
        label = jnp.where(bit_here == bit_no, others[bit_no], label)
    label = label[0]
    traded_ints = jnp.concatenate(
        [
            jnp.zeros((1,), jnp.int32),
            label[0:1].astype(jnp.int32),
            jnp.arange(6, dtype=jnp.int32),
            label[1:7].astype(jnp.int32),
            slot_here[None],
            bit_here[None] + 1,
        ]
    )
    traded_vals = jnp.concatenate([label[7:10].astype(f32), diffusivity, reaction_matrix.reshape(-1)])

    stay = first_substep(ints, vals, blocks, 1, per_dev - 1)
    arrived, stay, traded_ints, traded_vals = lax.optimization_barrier(
        (arrived, stay, traded_ints, traded_vals)
    )
    layers = offers(jnp.take(arrived, pick(lookup, 6), axis=0))
    result = advance_stay(ints, vals, *stay, arrived, plane, 1, per_dev)
    raws, layers, result = lax.optimization_barrier((raws, layers, result))
    result = advance_traded(traded_ints, traded_vals, raws, layers, result)
    return result[None]


def solution(mesh):
    in_specs = (
        P("gx", ("gy", "gz"), None, None, None),
        P("gx", None),
        P("gx", ("gy", "gz"), None),
        P(),
        P(),
        P("gx", None, None),
        P("gx", "gy", "gz"),
        P("gx", "gy", "gz"),
    )
    out_specs = P("gx", ("gy", "gz"), None, None, None)
    return jax.shard_map(local, mesh=mesh, in_specs=in_specs, out_specs=out_specs, check_vma=False)
```

time: 100 us -> 86.2 us (0.86)
  the two profiles are of different devices: /device:TPU:49 before, /device:TPU:32 now
where the time goes in v4:
time: 86.2 us; the launch traced here: 85.7 us
  Pallas kernels  41.3 us (48%)
  starting transfers between devices  22.3 us (26%)
  waiting for transfers between devices  12.6 us (15%)
  local copies, waits for them, and re-layouts  3.68 us (4%)
  other arithmetic  3.38 us (4%)
  between operations  2.43 us (3%)
    pallas_call x1, Pallas kernels, advance_stay(): pl.pallas_call(functools.partial(stay_kernel, first, per_dev), grid_spec=...  18.3 us
    all_to_all x1, waiting for transfers between devices, local(): lax.all_to_all(outgoing, ('gy', 'gz'), split_axis=0, concat_axis=0, tiled...  12.5 us
    all_to_all x1, starting transfers between devices, local(): lax.all_to_all(outgoing, ('gy', 'gz'), split_axis=0, concat_axis=0, tiled...  11.3 us
    ppermute x9, starting transfers between devices, swapped(): lax.ppermute(x, axis, [(i, i ^ 1 << bit) for i in range(lax.axis_size(axi...  11 us
    pallas_call x1, Pallas kernels, advance_traded(): pl.pallas_call(functools.partial(traded_kernel, choices), grid_spec=pltpu...  8.79 us
    pallas_call x1, Pallas kernels, first_substep(): pl.pallas_call(functools.partial(first_kernel, first, per_dev), grid_spec...  8.11 us
    pallas_call x1, Pallas kernels, pack_faces(): pl.pallas_call(pack_kernel, grid_spec=pltpu.PrefetchScalarGridSpec(num_sc...  6.02 us
  transfers between devices with their start and end apart: 10, of which 1 were waited for; matrix products, arithmetic and copies ran while one was open for 6% of the time, Pallas kernels for 31%

profile of v4, /device:TPU:32, one launch (start us, length us, event | category | flops | bytes accessed | tf_op | source)
XLA Modules:
  0.0 85.7 jit_solution(14109597766675261926)
XLA Ops:
  0.3 0.7 select_reduce_fusion.2
  1.1 0.1 reduce_max.20
  1.4 0.1 reduce_min.20
  1.8 6.0 %pack_faces.1 = bf16[64,80,128]{2,1,0:T(8,128)(2,1)} custom-call(s32[64]{0:T(128)S(1)} %reshape.229.send_ref, bf16[4,10,32,1024]{3,2,1,0:T(8,128)(2,1)} %bitcast.46), custom_call_target="tpu_custom_call" | custom-call | tf_op jit(solution)/shard_map/pack_faces/pallas_call | solution.py:109
  7.8 11.3 %all-to-all-start = ((bf16[64,80,128]{2,1,0:T(8,128)(2,1)}), bf16[64,80,128]{2,1,0:T(8,128)(2,1)S(1)}, u32[]{:S(2)}, u32[]{:S(2)}) async-start(bf16[64,80,128]{2,1,0:T(8,128)(2,1)} %pack_faces.1), calls=%async_computation | async-start | bytes 2621440 | tf_op jit(solution)/shard_map/all_to_all | solution.py:571
  19.1 0.1 copy.22
  20.3 0.6 fusion.21
  21.0 0.2 select_reduce_fusion
  21.3 0.7 select_maximum_fusion
  22.0 3.2 %collective-permute-start = (bf16[16,128]{1,0:T(8,128)(2,1)S(1)}, bf16[16,128]{1,0:T(8,128)(2,1)S(1)}, u32[]{:S(2)}, u32[]{:S(2)}) collective-permute-start(bf16[16,128]{1,0:T(8,128)(2,1)S(1)} %broadcast_in_dim.55), channel_id=1, source_target_pairs={{0,128},{32,160},{64,192},{96,224},{128,0},{160,32},{192,64},{224,... | collective-permute-start | bytes 12296 | tf_op jit(solution)/shard_map/ppermute | solution.py:20
  25.2 0.7 collective-permute-start.1
  25.9 1.1 %dynamic-slice_bitcast_fusion.refs_0_ = bf16[1,10,32,1024]{3,2,1,0:T(8,128)(2,1)S(1)} fusion(bf16[1,4,10,32,1024]{4,3,2,1,0:T(8,128)(2,1)} %param.8, s32[]{:T(128)S(6)} %select_n.146), kind=kLoop, calls=%fused_computation.1 | loop fusion | bytes 1310724 | tf_op jit(solution)/shard_map/dynamic_slice | solution.py:588
  27.1 0.6 collective-permute-start.3
  27.6 1.3 %collective-permute-start.4 = (bf16[1,10,32,1024]{3,2,1,0:T(8,128)(2,1)S(1)}, bf16[1,10,32,1024]{3,2,1,0:T(8,128)(2,1)S(1)}, u32[]{:S(2)}, u32[]{:S(2)}) collective-permute-start(bf16[1,10,32,1024]{3,2,1,0:T(8,128)(2,1)S(1)} %dynamic-slice_bitcast_fusion.refs_0_), channel_id=1, source_target_pairs={{0,64},{32,96},{64,0},{96,32},{128,192},{160,224},{192,128},{224,1... | collective-permute-start | bytes 1966088 | tf_op jit(solution)/shard_map/ppermute | solution.py:20
  29.1 0.2 fusion.1
  30.2 8.1 %first_substep.1 = (f32[3,10,8,32,128]{4,3,2,1,0:T(8,128)}, bf16[3,80,240]{2,1,0:T(8,128)(2,1)S(1)}) custom-call(s32[56]{0:T(128)S(1)} %pad_add_fusion.1.ints_ref, f32[122]{0:T(128)S(1)} %pad_maximum_fusion.vals_ref, bf16[4,10,32,1024]{3,2,1,0:T(8,128)(2,1)} %bitcast.47), custom_call_target="tpu_custom_call" | custom-call | tf_op jit(solution)/shard_map/first_substep/pallas_call | solution.py:299
  38.3 0.5 collective-permute-start.5
  38.9 0.6 slice.21
  40.4 12.5 %all-to-all-done.arr_ref = bf16[64,80,128]{2,1,0:T(8,128)(2,1)S(1)} async-done(((bf16[64,80,128]{2,1,0:T(8,128)(2,1)}), bf16[64,80,128]{2,1,0:T(8,128)(2,1)S(1)}, u32[]{:S(2)}, u32[]{:S(2)}) %all-to-all-start) | async-done | bytes 1310752 | tf_op jit(solution)/shard_map/all_to_all | solution.py:571
  53.0 0.6 gather_fusion
  53.8 1.7 %collective-permute-start.7 = (bf16[6,80,128]{2,1,0:T(8,128)(2,1)S(1)}, bf16[6,80,128]{2,1,0:T(8,128)(2,1)S(1)}, u32[]{:S(2)}, u32[]{:S(2)}) collective-permute-start(bf16[6,80,128]{2,1,0:T(8,128)(2,1)S(1)} %broadcast_select_fusion.refs_4_), channel_id=1, source_target_pairs={{0,64},{32,96},{64,0},{96,32},{128,192},{160,224},{192,128},{224,1... | collective-permute-start | bytes 368648 | tf_op jit(solution)/shard_map/ppermute | solution.py:20
  55.4 2.9 %collective-permute-start.8 = (bf16[6,80,128]{2,1,0:T(8,128)(2,1)S(1)}, bf16[6,80,128]{2,1,0:T(8,128)(2,1)S(1)}, u32[]{:S(2)}, u32[]{:S(2)}) collective-permute-start(bf16[6,80,128]{2,1,0:T(8,128)(2,1)S(1)} %broadcast_select_fusion.refs_4_), channel_id=1, source_target_pairs={{0,128},{32,160},{64,192},{96,224},{128,0},{160,32},{192,64},{224,... | collective-permute-start | bytes 368648 | tf_op jit(solution)/shard_map/ppermute | solution.py:20
  58.3 18.3 %advance_stay.1.refs_8_ = bf16[4,10,32,1024]{3,2,1,0:T(8,128)(2,1)} custom-call(s32[56]{0:T(128)S(1)} %pad_add_fusion.1.ints_ref, f32[122]{0:T(128)S(1)} %pad_maximum_fusion.vals_ref, f32[3,10,8,32,128]{4,3,2,1,0:T(8,128)} %get-tuple-element.26.s_ref, bf16[3,80,240]{2,1,0:T(8,128)(2,1)S(1)} %get-tuple-element.27.rk_ref, ...), custom_call_target="tpu_custom_call" | custom-call | tf_op jit(solution)/shard_map/advance_stay/pallas_call | solution.py:442
  76.7 8.8 %advance_traded.1 = bf16[4,10,32,1024]{3,2,1,0:T(8,128)(2,1)} custom-call(s32[16]{0:T(128)S(1)} %concatenate.18.ints_ref, f32[113]{0:T(128)S(1)} %pad_maximum_fusion.1.vals_ref, bf16[1,10,32,1024]{3,2,1,0:T(8,128)(2,1)S(1)} %dynamic-slice_bitcast_fusion.refs_0_, ...), custom_call_target="tpu_custom_call", output_to_operand_aliasing={{}: (10, {})} | custom-call | tf_op jit(solution)/shard_map/advance_traded/pallas_call | solution.py:513
  (61 shorter events, 2.2 us)
Async XLA Ops:
  1.7 17.4 %copy-start = (s32[1,128,6]{1,0,2:T(1,128)S(1)}, s32[1,128,6]{1,0,2:T(1,128)}, u32[]{:S(2)}) copy-start(s32[1,128,6]{1,0,2:T(1,128)} %param.13) | copy-start | bytes 9220
  1.7 17.6 %copy-start.4 = (s32[1,128]{1,0:T(1,128)S(1)}, s32[1,128]{1,0:T(1,128)}, u32[]{:S(2)}) copy-start(s32[1,128]{1,0:T(1,128)} %param.9) | copy-start | bytes 1540
  1.7 19.1 %copy-start.3 = (bf16[1,4,3]{2,1,0:T(4,128)(2,1)S(1)}, bf16[1,4,3]{2,1,0:T(4,128)(2,1)}, u32[]{:S(2)}) copy-start(bf16[1,4,3]{2,1,0:T(4,128)(2,1)} %param.10) | copy-start | bytes 76
  7.8 21.2 %copy-start.1 = (f32[10,10]{1,0:T(8,128)S(1)}, f32[10,10]{1,0:T(8,128)}, u32[]{:S(2)}) copy-start(f32[10,10]{1,0:T(8,128)} %param.12) | copy-start | bytes 1204
  7.8 21.7 %copy-start.2 = (f32[10]{0:T(128)S(1)}, f32[10]{0:T(128)}, u32[]{:S(2)}) copy-start(f32[10]{0:T(128)} %param.11) | copy-start | bytes 124
  7.8 45.2 %all-to-all-start = ((bf16[64,80,128]{2,1,0:T(8,128)(2,1)}), bf16[64,80,128]{2,1,0:T(8,128)(2,1)S(1)}, u32[]{:S(2)}, u32[]{:S(2)}) async-start(bf16[64,80,128]{2,1,0:T(8,128)(2,1)} %pack_faces.1), calls=%async_computation | async-start | bytes 2621440 | tf_op jit(solution)/shard_map/all_to_all | solution.py:571
  22.0 16.3 %collective-permute-start = (bf16[16,128]{1,0:T(8,128)(2,1)S(1)}, bf16[16,128]{1,0:T(8,128)(2,1)S(1)}, u32[]{:S(2)}, u32[]{:S(2)}) collective-permute-start(bf16[16,128]{1,0:T(8,128)(2,1)S(1)} %broadcast_in_dim.55), channel_id=1, source_target_pairs={{0,128},{32,160},{64,192},{96,224},{128,0},{160,32},{192,64},{224,... | collective-permute-start | bytes 12296 | tf_op jit(solution)/shard_map/ppermute | solution.py:20
  25.2 13.6 %collective-permute-start.1 = (bf16[16,128]{1,0:T(8,128)(2,1)S(1)}, bf16[16,128]{1,0:T(8,128)(2,1)S(1)}, u32[]{:S(2)}, u32[]{:S(2)}) collective-permute-start(bf16[16,128]{1,0:T(8,128)(2,1)S(1)} %broadcast_in_dim.55), channel_id=1, source_target_pairs={{0,64},{32,96},{64,0},{96,32},{128,192},{160,224},{192,128},{224,1... | collective-permute-start | bytes 12296 | tf_op jit(solution)/shard_map/ppermute | solution.py:20
  25.9 12.9 %collective-permute-start.2 = (bf16[16,128]{1,0:T(8,128)(2,1)S(1)}, bf16[16,128]{1,0:T(8,128)(2,1)S(1)}, u32[]{:S(2)}, u32[]{:S(2)}) collective-permute-start(bf16[16,128]{1,0:T(8,128)(2,1)S(1)} %broadcast_in_dim.55), channel_id=1, source_target_pairs={{0,32},{32,0},{64,96},{96,64},{128,160},{160,128},{192,224},{224,1... | collective-permute-start | bytes 12296 | tf_op jit(solution)/shard_map/ppermute | solution.py:20
  27.1 28.4 %collective-permute-start.3 = (bf16[1,10,32,1024]{3,2,1,0:T(8,128)(2,1)S(1)}, bf16[1,10,32,1024]{3,2,1,0:T(8,128)(2,1)S(1)}, u32[]{:S(2)}, u32[]{:S(2)}) collective-permute-start(bf16[1,10,32,1024]{3,2,1,0:T(8,128)(2,1)S(1)} %dynamic-slice_bitcast_fusion.refs_0_), channel_id=1, source_target_pairs={{0,32},{32,0},{64,96},{96,64},{128,160},{160,128},{192,224},{224,1... | collective-permute-start | bytes 1966088 | tf_op jit(solution)/shard_map/ppermute | solution.py:20
  27.6 49.0 %collective-permute-start.4 = (bf16[1,10,32,1024]{3,2,1,0:T(8,128)(2,1)S(1)}, bf16[1,10,32,1024]{3,2,1,0:T(8,128)(2,1)S(1)}, u32[]{:S(2)}, u32[]{:S(2)}) collective-permute-start(bf16[1,10,32,1024]{3,2,1,0:T(8,128)(2,1)S(1)} %dynamic-slice_bitcast_fusion.refs_0_), channel_id=1, source_target_pairs={{0,64},{32,96},{64,0},{96,32},{128,192},{160,224},{192,128},{224,1... | collective-permute-start | bytes 1966088 | tf_op jit(solution)/shard_map/ppermute | solution.py:20
  38.3 38.3 %collective-permute-start.5 = (bf16[1,10,32,1024]{3,2,1,0:T(8,128)(2,1)S(1)}, bf16[1,10,32,1024]{3,2,1,0:T(8,128)(2,1)}, u32[]{:S(2)}, u32[]{:S(2)}) collective-permute-start(bf16[1,10,32,1024]{3,2,1,0:T(8,128)(2,1)S(1)} %dynamic-slice_bitcast_fusion.refs_0_), channel_id=1, source_target_pairs={{0,128},{32,160},{64,192},{96,224},{128,0},{160,32},{192,64},{224,... | collective-permute-start | bytes 1966088 | tf_op jit(solution)/shard_map/ppermute | solution.py:20
  53.7 23.0 %collective-permute-start.6 = (bf16[6,80,128]{2,1,0:T(8,128)(2,1)S(1)}, bf16[6,80,128]{2,1,0:T(8,128)(2,1)S(1)}, u32[]{:S(2)}, u32[]{:S(2)}) collective-permute-start(bf16[6,80,128]{2,1,0:T(8,128)(2,1)S(1)} %broadcast_select_fusion.refs_4_), channel_id=1, source_target_pairs={{0,32},{32,0},{64,96},{96,64},{128,160},{160,128},{192,224},{224,1... | collective-permute-start | bytes 368648 | tf_op jit(solution)/shard_map/ppermute | solution.py:20
  53.8 22.9 %collective-permute-start.7 = (bf16[6,80,128]{2,1,0:T(8,128)(2,1)S(1)}, bf16[6,80,128]{2,1,0:T(8,128)(2,1)S(1)}, u32[]{:S(2)}, u32[]{:S(2)}) collective-permute-start(bf16[6,80,128]{2,1,0:T(8,128)(2,1)S(1)} %broadcast_select_fusion.refs_4_), channel_id=1, source_target_pairs={{0,64},{32,96},{64,0},{96,32},{128,192},{160,224},{192,128},{224,1... | collective-permute-start | bytes 368648 | tf_op jit(solution)/shard_map/ppermute | solution.py:20
  55.4 21.3 %collective-permute-start.8 = (bf16[6,80,128]{2,1,0:T(8,128)(2,1)S(1)}, bf16[6,80,128]{2,1,0:T(8,128)(2,1)S(1)}, u32[]{:S(2)}, u32[]{:S(2)}) collective-permute-start(bf16[6,80,128]{2,1,0:T(8,128)(2,1)S(1)} %broadcast_select_fusion.refs_4_), channel_id=1, source_target_pairs={{0,128},{32,160},{64,192},{96,224},{128,0},{160,32},{192,64},{224,... | collective-permute-start | bytes 368648 | tf_op jit(solution)/shard_map/ppermute | solution.py:20

commit v5 on v4

--- a/solution.py
+++ b/solution.py
@@ -400,11 +400,28 @@
     return finish
 
 
-def stay_kernel(first, per_dev, ints_ref, vals_ref, s_ref, rk_ref, arr_ref, o_ref, sa_ref, sb_ref, e_ref, side_ref):
+def stay_kernel(first, count, per_dev, ints_ref, vals_ref, s_ref, rk_ref, arr_ref, *refs):
+    o_ref, sa_ref, sb_ref, e_ref, side_ref, layer_ref, sems = refs[-7:]
     _, fields, tiles, cells, _ = s_ref.shape
-    facts = Facts(ints_ref, vals_ref, ints_ref[pl.program_id(0) + first], per_dev, fields)
+    at = pl.program_id(0)
+    facts = Facts(ints_ref, vals_ref, ints_ref[at + first], per_dev, fields)
+
+    def fetch(place, face_no, lookup):
+        return pltpu.make_async_copy(
+            arr_ref.at[lookup], layer_ref.at[place, face_no], sems.at[place, face_no]
+        )
+
+    @pl.when(at == 0)
+    def _():
+        for place in range(count):
+            blk = ints_ref[place + first]
+            for face_no in range(6):
+                fetch(place, face_no, ints_ref[2 * per_dev + blk * 6 + face_no]).start()
+
+    for face_no in range(6):
+        fetch(at, face_no, facts.lookup(face_no)).wait()
     place_layers(
-        lambda face_no: arr_ref[facts.lookup(face_no)],
+        lambda face_no: layer_ref[at, face_no],
         facts, sa_ref, sb_ref, e_ref, side_ref, s_ref, fields, cells, tiles,
     )
     step = make_step(rk_ref[0], facts, e_ref, side_ref, fields, cells, tiles)
@@ -436,26 +453,34 @@
     ]
 
 
-def advance_stay(ints, vals, started, own, arrived, plane, first, per_dev):
-    count, fields, tiles, cells, _ = started.shape
+def advance_stay(ints, vals, started, own, arrived, plane, first, per_dev, skip, count, into=None):
+    _, fields, tiles, cells, _ = started.shape
     shape = (1, fields, cells, plane)
+    at = first + skip
+    whole = [] if into is None else [into]
     return pl.pallas_call(
-        functools.partial(stay_kernel, first, per_dev),
+        functools.partial(stay_kernel, at, count, per_dev),
         grid_spec=pltpu.PrefetchScalarGridSpec(
             num_scalar_prefetch=2,
             grid=(count,),
             in_specs=[
-                pl.BlockSpec((1,) + started.shape[1:], lambda b, i, v: (b, 0, 0, 0, 0)),
-                pl.BlockSpec((1,) + own.shape[1:], lambda b, i, v: (b, 0, 0)),
-                pl.BlockSpec(arrived.shape, lambda b, i, v: (0, 0, 0)),
+                pl.BlockSpec((1,) + started.shape[1:], lambda b, i, v: (b + skip, 0, 0, 0, 0)),
+                pl.BlockSpec((1,) + own.shape[1:], lambda b, i, v: (b + skip, 0, 0)),
+                pl.BlockSpec(memory_space=pl.ANY),
+            ]
+            + [pl.BlockSpec(memory_space=pl.ANY) for _ in whole],
+            out_specs=pl.BlockSpec(shape, lambda b, i, v: (i[b + at], 0, 0, 0)),
+            scratch_shapes=state_scratch(fields, cells, tiles)
+            + [
+                pltpu.VMEM((count, 6) + arrived.shape[1:], bf16),
+                pltpu.SemaphoreType.DMA((count, 6)),
             ],
-            out_specs=pl.BlockSpec(shape, lambda b, i, v: (i[b + first], 0, 0, 0)),
-            scratch_shapes=state_scratch(fields, cells, tiles),
         ),
         out_shape=jax.ShapeDtypeStruct((per_dev, fields, cells, plane), bf16),
+        input_output_aliases={} if into is None else {5: 0},
         compiler_params=pltpu.CompilerParams(vmem_limit_bytes=20 << 20),
         name="advance_stay",
-    )(ints, vals, in_hbm(started), own, arrived)
+    )(ints, vals, in_hbm(started), own, arrived, *whole)
 
 
 def traded_kernel(choices, ints_ref, vals_ref, *refs):
@@ -610,8 +635,11 @@
     arrived, stay, traded_ints, traded_vals = lax.optimization_barrier(
         (arrived, stay, traded_ints, traded_vals)
     )
-    layers = offers(jnp.take(arrived, pick(lookup, 6), axis=0))
-    result = advance_stay(ints, vals, *stay, arrived, plane, 1, per_dev)
+    layers = jnp.take(arrived, pick(lookup, 6), axis=0, mode="clip")
+    result = advance_stay(ints, vals, *stay, arrived, plane, 1, per_dev, 0, 1)
+    layers, result = lax.optimization_barrier((layers, result))
+    layers = offers(layers)
+    result = advance_stay(ints, vals, *stay, arrived, plane, 1, per_dev, 1, per_dev - 2, result)
     raws, layers, result = lax.optimization_barrier((raws, layers, result))
     result = advance_traded(traded_ints, traded_vals, raws, layers, result)
     return result[None]

time: 86.2 us -> 89.5 us (1.038)
  Pallas kernels: 41.3 us -> 44.7 us
    pallas_call x1 -> x2, Pallas kernels: 18.3 us -> 21.9 us  [advance_stay(): pl.pallas_call(functools.partial(stay_kernel, at, count, per_dev), grid_s...]
  transfers between devices with their start and end apart: 10 -> 10, of which waited for: 1 -> 1; matrix products, arithmetic and copies ran while one was open for 6% -> 6% of each run, Pallas kernels for 31% -> 34%
where the time goes in v5:
time: 89.5 us; the launch traced here: 89 us
  Pallas kernels  44.7 us (50%)
  starting transfers between devices  22.3 us (25%)
  waiting for transfers between devices  12.6 us (14%)
  local copies, waits for them, and re-layouts  3.7 us (4%)
  other arithmetic  3.27 us (4%)
  between operations  2.39 us (3%)
    pallas_call x2, Pallas kernels, advance_stay(): pl.pallas_call(functools.partial(stay_kernel, at, count, per_dev), grid_s...  21.9 us
    all_to_all x1, waiting for transfers between devices, local(): lax.all_to_all(outgoing, ('gy', 'gz'), split_axis=0, concat_axis=0, tiled...  12.6 us
    all_to_all x1, starting transfers between devices, local(): lax.all_to_all(outgoing, ('gy', 'gz'), split_axis=0, concat_axis=0, tiled...  11.3 us
    ppermute x9, starting transfers between devices, swapped(): lax.ppermute(x, axis, [(i, i ^ 1 << bit) for i in range(lax.axis_size(axi...  11 us
    pallas_call x1, Pallas kernels, advance_traded(): pl.pallas_call(functools.partial(traded_kernel, choices), grid_spec=pltpu...  8.61 us
    pallas_call x1, Pallas kernels, first_substep(): pl.pallas_call(functools.partial(first_kernel, first, per_dev), grid_spec...  8.12 us
    pallas_call x1, Pallas kernels, pack_faces(): pl.pallas_call(pack_kernel, grid_spec=pltpu.PrefetchScalarGridSpec(num_sc...  6.02 us
  transfers between devices with their start and end apart: 10, of which 1 were waited for; matrix products, arithmetic and copies ran while one was open for 6% of the time, Pallas kernels for 34%

profile of v5, /device:TPU:32, one launch (start us, length us, event | category | flops | bytes accessed | tf_op | source)
XLA Modules:
  0.0 89.0 jit_solution(5062722339239175057)
XLA Ops:
  0.3 0.7 select_reduce_fusion.2
  1.1 0.1 reduce_max.20
  1.4 0.1 reduce_min.20
  1.8 6.0 %pack_faces.1 = bf16[64,80,128]{2,1,0:T(8,128)(2,1)} custom-call(s32[64]{0:T(128)S(1)} %reshape.224.send_ref, bf16[4,10,32,1024]{3,2,1,0:T(8,128)(2,1)} %bitcast.46), custom_call_target="tpu_custom_call" | custom-call | tf_op jit(solution)/shard_map/pack_faces/pallas_call | solution.py:109
  7.8 11.3 %all-to-all-start = ((bf16[64,80,128]{2,1,0:T(8,128)(2,1)}), bf16[64,80,128]{2,1,0:T(8,128)(2,1)S(1)}, u32[]{:S(2)}, u32[]{:S(2)}) async-start(bf16[64,80,128]{2,1,0:T(8,128)(2,1)} %pack_faces.1), calls=%async_computation | async-start | bytes 2621440 | tf_op jit(solution)/shard_map/all_to_all | solution.py:596
  20.2 0.7 fusion.21
  21.1 0.2 select_reduce_fusion
  21.3 0.7 select_maximum_fusion
  22.0 3.2 %collective-permute-start = (bf16[16,128]{1,0:T(8,128)(2,1)S(1)}, bf16[16,128]{1,0:T(8,128)(2,1)S(1)}, u32[]{:S(2)}, u32[]{:S(2)}) collective-permute-start(bf16[16,128]{1,0:T(8,128)(2,1)S(1)} %broadcast_in_dim.47), channel_id=1, source_target_pairs={{0,128},{32,160},{64,192},{96,224},{128,0},{160,32},{192,64},{224,... | collective-permute-start | bytes 12296 | tf_op jit(solution)/shard_map/ppermute | solution.py:20
  25.3 0.7 collective-permute-start.1
  26.0 1.1 %dynamic-slice_bitcast_fusion.refs_0_ = bf16[1,10,32,1024]{3,2,1,0:T(8,128)(2,1)S(1)} fusion(bf16[1,4,10,32,1024]{4,3,2,1,0:T(8,128)(2,1)} %param.8, s32[]{:T(128)S(6)} %select_n.137), kind=kLoop, calls=%fused_computation.1 | loop fusion | bytes 1310724 | tf_op jit(solution)/shard_map/dynamic_slice | solution.py:613
  27.1 0.6 collective-permute-start.3
  27.7 1.3 %collective-permute-start.4 = (bf16[1,10,32,1024]{3,2,1,0:T(8,128)(2,1)S(1)}, bf16[1,10,32,1024]{3,2,1,0:T(8,128)(2,1)S(1)}, u32[]{:S(2)}, u32[]{:S(2)}) collective-permute-start(bf16[1,10,32,1024]{3,2,1,0:T(8,128)(2,1)S(1)} %dynamic-slice_bitcast_fusion.refs_0_), channel_id=1, source_target_pairs={{0,64},{32,96},{64,0},{96,32},{128,192},{160,224},{192,128},{224,1... | collective-permute-start | bytes 1966088 | tf_op jit(solution)/shard_map/ppermute | solution.py:20
  29.1 0.2 fusion.1
  30.3 8.1 %first_substep.1 = (f32[3,10,8,32,128]{4,3,2,1,0:T(8,128)}, bf16[3,80,240]{2,1,0:T(8,128)(2,1)S(1)}) custom-call(s32[56]{0:T(128)S(1)} %pad_add_fusion.1.ints_ref, f32[122]{0:T(128)S(1)} %pad_maximum_fusion.vals_ref, bf16[4,10,32,1024]{3,2,1,0:T(8,128)(2,1)} %bitcast.47), custom_call_target="tpu_custom_call" | custom-call | tf_op jit(solution)/shard_map/first_substep/pallas_call | solution.py:299
  38.4 0.5 collective-permute-start.5
  38.9 0.5 slice.21
  40.4 12.6 %all-to-all-done.arr_ref = bf16[64,80,128]{2,1,0:T(8,128)(2,1)S(1)} async-done(((bf16[64,80,128]{2,1,0:T(8,128)(2,1)}), bf16[64,80,128]{2,1,0:T(8,128)(2,1)S(1)}, u32[]{:S(2)}, u32[]{:S(2)}) %all-to-all-start) | async-done | bytes 1310752 | tf_op jit(solution)/shard_map/all_to_all | solution.py:596
  53.0 0.6 gather_fusion
  53.6 8.2 %advance_stay.2.refs_0_ = bf16[4,10,32,1024]{3,2,1,0:T(8,128)(2,1)} custom-call(s32[56]{0:T(128)S(1)} %pad_add_fusion.1.ints_ref, f32[122]{0:T(128)S(1)} %pad_maximum_fusion.vals_ref, f32[3,10,8,32,128]{4,3,2,1,0:T(8,128)} %get-tuple-element.28.s_ref, bf16[3,80,240]{2,1,0:T(8,128)(2,1)S(1)} %get-tuple-element.29.rk_ref, ...), custom_call_target="tpu_custom_call" | custom-call | tf_op jit(solution)/shard_map/advance_stay/pallas_call | solution.py:461
  61.9 1.7 %collective-permute-start.7 = (bf16[6,80,128]{2,1,0:T(8,128)(2,1)S(1)}, bf16[6,80,128]{2,1,0:T(8,128)(2,1)S(1)}, u32[]{:S(2)}, u32[]{:S(2)}) collective-permute-start(bf16[6,80,128]{2,1,0:T(8,128)(2,1)S(1)} %gather_fusion), channel_id=1, source_target_pairs={{0,64},{32,96},{64,0},{96,32},{128,192},{160,224},{192,128},{224,1... | collective-permute-start | bytes 368648 | tf_op jit(solution)/shard_map/ppermute | solution.py:20
  63.5 2.9 %collective-permute-start.8 = (bf16[6,80,128]{2,1,0:T(8,128)(2,1)S(1)}, bf16[6,80,128]{2,1,0:T(8,128)(2,1)S(1)}, u32[]{:S(2)}, u32[]{:S(2)}) collective-permute-start(bf16[6,80,128]{2,1,0:T(8,128)(2,1)S(1)} %gather_fusion), channel_id=1, source_target_pairs={{0,128},{32,160},{64,192},{96,224},{128,0},{160,32},{192,64},{224,... | collective-permute-start | bytes 368648 | tf_op jit(solution)/shard_map/ppermute | solution.py:20
  66.4 13.8 %advance_stay.3.refs_8_ = bf16[4,10,32,1024]{3,2,1,0:T(8,128)(2,1)} custom-call(s32[56]{0:T(128)S(1)} %pad_add_fusion.1.ints_ref, f32[122]{0:T(128)S(1)} %pad_maximum_fusion.vals_ref, f32[3,10,8,32,128]{4,3,2,1,0:T(8,128)} %get-tuple-element.28.s_ref, bf16[3,80,240]{2,1,0:T(8,128)(2,1)S(1)} %get-tuple-element.29.rk_ref, ...), custom_call_target="tpu_custom_call", output_to_operand_aliasing={{}: (5, {})} | custom-call | tf_op jit(solution)/shard_map/advance_stay/pallas_call | solution.py:461
  80.2 8.6 %advance_traded.1 = bf16[4,10,32,1024]{3,2,1,0:T(8,128)(2,1)} custom-call(s32[16]{0:T(128)S(1)} %concatenate.18.ints_ref, f32[113]{0:T(128)S(1)} %pad_maximum_fusion.1.vals_ref, bf16[1,10,32,1024]{3,2,1,0:T(8,128)(2,1)S(1)} %dynamic-slice_bitcast_fusion.refs_0_, ...), custom_call_target="tpu_custom_call", output_to_operand_aliasing={{}: (10, {})} | custom-call | tf_op jit(solution)/shard_map/advance_traded/pallas_call | solution.py:538
  (61 shorter events, 2.2 us)
Async XLA Ops:
  1.7 17.4 %copy-start.4 = (s32[1,128]{1,0:T(1,128)S(1)}, s32[1,128]{1,0:T(1,128)}, u32[]{:S(2)}) copy-start(s32[1,128]{1,0:T(1,128)} %param.9) | copy-start | bytes 1540
  1.7 17.5 %copy-start = (s32[1,128,6]{1,0,2:T(1,128)S(1)}, s32[1,128,6]{1,0,2:T(1,128)}, u32[]{:S(2)}) copy-start(s32[1,128,6]{1,0,2:T(1,128)} %param.13) | copy-start | bytes 9220
  1.7 19.1 %copy-start.3 = (bf16[1,4,3]{2,1,0:T(4,128)(2,1)S(1)}, bf16[1,4,3]{2,1,0:T(4,128)(2,1)}, u32[]{:S(2)}) copy-start(bf16[1,4,3]{2,1,0:T(4,128)(2,1)} %param.10) | copy-start | bytes 76
  7.8 21.3 %copy-start.1 = (f32[10,10]{1,0:T(8,128)S(1)}, f32[10,10]{1,0:T(8,128)}, u32[]{:S(2)}) copy-start(f32[10,10]{1,0:T(8,128)} %param.12) | copy-start | bytes 1204
  7.8 21.7 %copy-start.2 = (f32[10]{0:T(128)S(1)}, f32[10]{0:T(128)}, u32[]{:S(2)}) copy-start(f32[10]{0:T(128)} %param.11) | copy-start | bytes 124
  7.8 45.2 %all-to-all-start = ((bf16[64,80,128]{2,1,0:T(8,128)(2,1)}), bf16[64,80,128]{2,1,0:T(8,128)(2,1)S(1)}, u32[]{:S(2)}, u32[]{:S(2)}) async-start(bf16[64,80,128]{2,1,0:T(8,128)(2,1)} %pack_faces.1), calls=%async_computation | async-start | bytes 2621440 | tf_op jit(solution)/shard_map/all_to_all | solution.py:596
  22.0 16.3 %collective-permute-start = (bf16[16,128]{1,0:T(8,128)(2,1)S(1)}, bf16[16,128]{1,0:T(8,128)(2,1)S(1)}, u32[]{:S(2)}, u32[]{:S(2)}) collective-permute-start(bf16[16,128]{1,0:T(8,128)(2,1)S(1)} %broadcast_in_dim.47), channel_id=1, source_target_pairs={{0,128},{32,160},{64,192},{96,224},{128,0},{160,32},{192,64},{224,... | collective-permute-start | bytes 12296 | tf_op jit(solution)/shard_map/ppermute | solution.py:20
  25.3 13.6 %collective-permute-start.1 = (bf16[16,128]{1,0:T(8,128)(2,1)S(1)}, bf16[16,128]{1,0:T(8,128)(2,1)S(1)}, u32[]{:S(2)}, u32[]{:S(2)}) collective-permute-start(bf16[16,128]{1,0:T(8,128)(2,1)S(1)} %broadcast_in_dim.47), channel_id=1, source_target_pairs={{0,64},{32,96},{64,0},{96,32},{128,192},{160,224},{192,128},{224,1... | collective-permute-start | bytes 12296 | tf_op jit(solution)/shard_map/ppermute | solution.py:20
  25.9 12.9 %collective-permute-start.2 = (bf16[16,128]{1,0:T(8,128)(2,1)S(1)}, bf16[16,128]{1,0:T(8,128)(2,1)S(1)}, u32[]{:S(2)}, u32[]{:S(2)}) collective-permute-start(bf16[16,128]{1,0:T(8,128)(2,1)S(1)} %broadcast_in_dim.47), channel_id=1, source_target_pairs={{0,32},{32,0},{64,96},{96,64},{128,160},{160,128},{192,224},{224,1... | collective-permute-start | bytes 12296 | tf_op jit(solution)/shard_map/ppermute | solution.py:20
  27.1 36.4 %collective-permute-start.3 = (bf16[1,10,32,1024]{3,2,1,0:T(8,128)(2,1)S(1)}, bf16[1,10,32,1024]{3,2,1,0:T(8,128)(2,1)S(1)}, u32[]{:S(2)}, u32[]{:S(2)}) collective-permute-start(bf16[1,10,32,1024]{3,2,1,0:T(8,128)(2,1)S(1)} %dynamic-slice_bitcast_fusion.refs_0_), channel_id=1, source_target_pairs={{0,32},{32,0},{64,96},{96,64},{128,160},{160,128},{192,224},{224,1... | collective-permute-start | bytes 1966088 | tf_op jit(solution)/shard_map/ppermute | solution.py:20
  27.7 52.5 %collective-permute-start.4 = (bf16[1,10,32,1024]{3,2,1,0:T(8,128)(2,1)S(1)}, bf16[1,10,32,1024]{3,2,1,0:T(8,128)(2,1)S(1)}, u32[]{:S(2)}, u32[]{:S(2)}) collective-permute-start(bf16[1,10,32,1024]{3,2,1,0:T(8,128)(2,1)S(1)} %dynamic-slice_bitcast_fusion.refs_0_), channel_id=1, source_target_pairs={{0,64},{32,96},{64,0},{96,32},{128,192},{160,224},{192,128},{224,1... | collective-permute-start | bytes 1966088 | tf_op jit(solution)/shard_map/ppermute | solution.py:20
  38.4 41.8 %collective-permute-start.5 = (bf16[1,10,32,1024]{3,2,1,0:T(8,128)(2,1)S(1)}, bf16[1,10,32,1024]{3,2,1,0:T(8,128)(2,1)}, u32[]{:S(2)}, u32[]{:S(2)}) collective-permute-start(bf16[1,10,32,1024]{3,2,1,0:T(8,128)(2,1)S(1)} %dynamic-slice_bitcast_fusion.refs_0_), channel_id=1, source_target_pairs={{0,128},{32,160},{64,192},{96,224},{128,0},{160,32},{192,64},{224,... | collective-permute-start | bytes 1966088 | tf_op jit(solution)/shard_map/ppermute | solution.py:20
  61.8 18.5 %collective-permute-start.6 = (bf16[6,80,128]{2,1,0:T(8,128)(2,1)S(1)}, bf16[6,80,128]{2,1,0:T(8,128)(2,1)S(1)}, u32[]{:S(2)}, u32[]{:S(2)}) collective-permute-start(bf16[6,80,128]{2,1,0:T(8,128)(2,1)S(1)} %gather_fusion), channel_id=1, source_target_pairs={{0,32},{32,0},{64,96},{96,64},{128,160},{160,128},{192,224},{224,1... | collective-permute-start | bytes 368648 | tf_op jit(solution)/shard_map/ppermute | solution.py:20
  61.9 18.4 %collective-permute-start.7 = (bf16[6,80,128]{2,1,0:T(8,128)(2,1)S(1)}, bf16[6,80,128]{2,1,0:T(8,128)(2,1)S(1)}, u32[]{:S(2)}, u32[]{:S(2)}) collective-permute-start(bf16[6,80,128]{2,1,0:T(8,128)(2,1)S(1)} %gather_fusion), channel_id=1, source_target_pairs={{0,64},{32,96},{64,0},{96,32},{128,192},{160,224},{192,128},{224,1... | collective-permute-start | bytes 368648 | tf_op jit(solution)/shard_map/ppermute | solution.py:20
  63.5 16.7 %collective-permute-start.8 = (bf16[6,80,128]{2,1,0:T(8,128)(2,1)S(1)}, bf16[6,80,128]{2,1,0:T(8,128)(2,1)S(1)}, u32[]{:S(2)}, u32[]{:S(2)}) collective-permute-start(bf16[6,80,128]{2,1,0:T(8,128)(2,1)S(1)} %gather_fusion), channel_id=1, source_target_pairs={{0,128},{32,160},{64,192},{96,224},{128,0},{160,32},{192,64},{224,... | collective-permute-start | bytes 368648 | tf_op jit(solution)/shard_map/ppermute | solution.py:20

commit v6 on v5

--- a/solution.py
+++ b/solution.py
@@ -453,23 +453,20 @@
     ]
 
 
-def advance_stay(ints, vals, started, own, arrived, plane, first, per_dev, skip, count, into=None):
-    _, fields, tiles, cells, _ = started.shape
+def advance_stay(ints, vals, started, own, arrived, plane, first, per_dev):
+    count, fields, tiles, cells, _ = started.shape
     shape = (1, fields, cells, plane)
-    at = first + skip
-    whole = [] if into is None else [into]
     return pl.pallas_call(
-        functools.partial(stay_kernel, at, count, per_dev),
+        functools.partial(stay_kernel, first, count, per_dev),
         grid_spec=pltpu.PrefetchScalarGridSpec(
             num_scalar_prefetch=2,
             grid=(count,),
             in_specs=[
-                pl.BlockSpec((1,) + started.shape[1:], lambda b, i, v: (b + skip, 0, 0, 0, 0)),
-                pl.BlockSpec((1,) + own.shape[1:], lambda b, i, v: (b + skip, 0, 0)),
+                pl.BlockSpec((1,) + started.shape[1:], lambda b, i, v: (b, 0, 0, 0, 0)),
+                pl.BlockSpec((1,) + own.shape[1:], lambda b, i, v: (b, 0, 0)),
                 pl.BlockSpec(memory_space=pl.ANY),
-            ]
-            + [pl.BlockSpec(memory_space=pl.ANY) for _ in whole],
-            out_specs=pl.BlockSpec(shape, lambda b, i, v: (i[b + at], 0, 0, 0)),
+            ],
+            out_specs=pl.BlockSpec(shape, lambda b, i, v: (i[b + first], 0, 0, 0)),
             scratch_shapes=state_scratch(fields, cells, tiles)
             + [
                 pltpu.VMEM((count, 6) + arrived.shape[1:], bf16),
@@ -477,29 +474,29 @@
             ],
         ),
         out_shape=jax.ShapeDtypeStruct((per_dev, fields, cells, plane), bf16),
-        input_output_aliases={} if into is None else {5: 0},
         compiler_params=pltpu.CompilerParams(vmem_limit_bytes=20 << 20),
         name="advance_stay",
-    )(ints, vals, in_hbm(started), own, arrived, *whole)
+    )(ints, vals, in_hbm(started), own, arrived)
 
 
 def traded_kernel(choices, ints_ref, vals_ref, *refs):
-    raw_refs, layer_refs, refs = refs[:choices], refs[choices : 2 * choices], refs[2 * choices + 1 :]
+    raw_refs, layers_ref, refs = refs[:choices], refs[choices], refs[choices + 2 :]
     o_ref, sa_ref, sb_ref, e_ref, side_ref, rk_ref, raw_ref, layer_ref, sems = refs
     _, fields, cells, plane = raw_ref.shape
     tiles = plane // LANES
     facts = Facts(ints_ref, vals_ref, 0, 1, fields)
     choice = ints_ref[15]
+    layer_copy = pltpu.make_async_copy(layers_ref, layer_ref, sems.at[1])
+    layer_copy.start()
     for c in range(choices):
 
         @pl.when(choice == c)
         def _():
             raw_copy = pltpu.make_async_copy(raw_refs[c], raw_ref, sems.at[0])
-            layer_copy = pltpu.make_async_copy(layer_refs[c], layer_ref, sems.at[1])
             raw_copy.start()
-            layer_copy.start()
             raw_copy.wait()
-            layer_copy.wait()
+
+    layer_copy.wait()
 
     def write(at, value):
         rk_ref[:, at : at + value.shape[1]] = value
@@ -540,7 +537,7 @@
         grid_spec=pltpu.PrefetchScalarGridSpec(
             num_scalar_prefetch=2,
             grid=(1,),
-            in_specs=[anywhere] * (2 * choices + 1),
+            in_specs=[anywhere] * (choices + 2),
             out_specs=pl.BlockSpec((1, fields, cells, plane), lambda b, i, v: (i[14], 0, 0, 0)),
             scratch_shapes=state_scratch(fields, cells, tiles)
             + [
@@ -551,10 +548,10 @@
             ],
         ),
         out_shape=jax.ShapeDtypeStruct(into.shape, bf16),
-        input_output_aliases={2 + 2 * choices: 0},
+        input_output_aliases={3 + choices: 0},
         compiler_params=pltpu.CompilerParams(vmem_limit_bytes=20 << 20),
         name="advance_traded",
-    )(ints, vals, *raws, *layers, into)
+    )(ints, vals, *raws, layers, into)
 
 
 def plan(wanted, my_index, per_dev):
@@ -610,15 +607,19 @@
     bits = range(lax.axis_size("gx").bit_length() - 1)
     offers = lambda x: [x] + [swapped(x, "gx", bit_no) for bit_no in bits]
 
+    flip = jnp.where(bit_here < 0, 0, jnp.left_shift(1, jnp.maximum(bit_here, 0)))
+    partner = jnp.bitwise_xor(lax.axis_index("gx").astype(jnp.int32), flip)
+
+    def to_partner(x):
+        to = jnp.arange(lax.axis_size("gx"), dtype=jnp.int32)[:, None, None, None] == partner
+        return lax.psum_scatter(jnp.where(to, x[None], 0), "gx", scatter_dimension=0, tiled=True)[0]
+
     raws = offers(lax.dynamic_slice_in_dim(blocks, slot_here, 1, 0))
     label = jnp.concatenate(
         [pick(own_levels, 1).astype(bf16), pick(coarse, 6).astype(bf16), pick(speeds, 3)]
     )
     label = jnp.broadcast_to(jnp.pad(label, (0, LABEL[1] - label.shape[0]))[None], LABEL)
-    label, *others = offers(label)
-    for bit_no in bits:
-        label = jnp.where(bit_here == bit_no, others[bit_no], label)
-    label = label[0]
+    label = to_partner(label[None])[0, 0]
     traded_ints = jnp.concatenate(
         [
             jnp.zeros((1,), jnp.int32),
@@ -632,14 +633,10 @@
     traded_vals = jnp.concatenate([label[7:10].astype(f32), diffusivity, reaction_matrix.reshape(-1)])
 
     stay = first_substep(ints, vals, blocks, 1, per_dev - 1)
-    arrived, stay, traded_ints, traded_vals = lax.optimization_barrier(
-        (arrived, stay, traded_ints, traded_vals)
-    )
+    arrived, stay, raws = lax.optimization_barrier((arrived, stay, raws))
     layers = jnp.take(arrived, pick(lookup, 6), axis=0, mode="clip")
-    result = advance_stay(ints, vals, *stay, arrived, plane, 1, per_dev, 0, 1)
-    layers, result = lax.optimization_barrier((layers, result))
-    layers = offers(layers)
-    result = advance_stay(ints, vals, *stay, arrived, plane, 1, per_dev, 1, per_dev - 2, result)
+    layers = to_partner(layers)
+    result = advance_stay(ints, vals, *stay, arrived, plane, 1, per_dev)
     raws, layers, result = lax.optimization_barrier((raws, layers, result))
     result = advance_traded(traded_ints, traded_vals, raws, layers, result)
     return result[None]

time: 89.5 us -> 122 us (1.36)
  waiting for transfers between devices: 12.6 us -> 35.2 us
  between operations: 2.39 us -> 15.6 us
  starting transfers between devices: 22.3 us -> 16.1 us
  other arithmetic: 3.27 us -> 6.46 us
  Pallas kernels: 44.7 us -> 42.1 us
  local copies, waits for them, and re-layouts: 3.7 us -> 5.23 us
    reduce_scatter x0 -> x2, waiting for transfers between devices: none -> 18.2 us  [to_partner(): lax.psum_scatter(jnp.where(to, x[None], 0), 'gx', scatter_dimension=0, ti...]
    ppermute x9 -> x3, waiting for transfers between devices: 0.02 us -> 17 us  [swapped(): lax.ppermute(x, axis, [(i, i ^ 1 << bit) for i in range(lax.axis_size(axi...]
    all_to_all x1, waiting for transfers between devices: 12.6 us -> 0.01 us  [local(): lax.all_to_all(outgoing, ('gy', 'gz'), split_axis=0, concat_axis=0, tiled...]
    ppermute x9 -> x3, starting transfers between devices: 11 us -> 4.66 us  [swapped(): lax.ppermute(x, axis, [(i, i ^ 1 << bit) for i in range(lax.axis_size(axi...]
    pallas_call x2 -> x1, Pallas kernels: 21.9 us -> 19.3 us  [advance_stay(): pl.pallas_call(functools.partial(stay_kernel, first, count, per_dev), gri...]
    select_n x2, other arithmetic: 0.02 us -> 1.78 us  [to_partner(): jnp.where(to, x[None], 0)]
  transfers between devices with their start and end apart: 10 -> 6, of which waited for: 1 -> 4; matrix products, arithmetic and copies ran while one was open for 6% -> 8% of each run, Pallas kernels for 34% -> 23%
where the time goes in v6:
time: 122 us; the launch traced here: 121 us
  Pallas kernels  42.1 us (35%)
  waiting for transfers between devices  35.2 us (29%)
  starting transfers between devices  16.1 us (13%)
  between operations  15.6 us (13%)
  other arithmetic  6.46 us (5%)
  local copies, waits for them, and re-layouts  5.23 us (4%)
    pallas_call x1, Pallas kernels, advance_stay(): pl.pallas_call(functools.partial(stay_kernel, first, count, per_dev), gri...  19.3 us
    reduce_scatter x2, waiting for transfers between devices, to_partner(): lax.psum_scatter(jnp.where(to, x[None], 0), 'gx', scatter_dimension=0, ti...  18.2 us
    ppermute x3, waiting for transfers between devices, swapped(): lax.ppermute(x, axis, [(i, i ^ 1 << bit) for i in range(lax.axis_size(axi...  17 us
    all_to_all x1, starting transfers between devices, local(): lax.all_to_all(outgoing, ('gy', 'gz'), split_axis=0, concat_axis=0, tiled...  11.3 us
    pallas_call x1, Pallas kernels, advance_traded(): pl.pallas_call(functools.partial(traded_kernel, choices), grid_spec=pltpu...  8.6 us
    pallas_call x1, Pallas kernels, first_substep(): pl.pallas_call(functools.partial(first_kernel, first, per_dev), grid_spec...  8.14 us
    pallas_call x1, Pallas kernels, pack_faces(): pl.pallas_call(pack_kernel, grid_spec=pltpu.PrefetchScalarGridSpec(num_sc...  6.03 us
    ppermute x3, starting transfers between devices, swapped(): lax.ppermute(x, axis, [(i, i ^ 1 << bit) for i in range(lax.axis_size(axi...  4.66 us
  transfers between devices with their start and end apart: 6, of which 4 were waited for; matrix products, arithmetic and copies ran while one was open for 8% of the time, Pallas kernels for 23%

profile of v6, /device:TPU:32, one launch (start us, length us, event | category | flops | bytes accessed | tf_op | source)
XLA Modules:
  0.0 120.6 jit_solution(9539592047997800979)
XLA Ops:
  6.9 0.7 select_reduce_fusion.2
  8.2 6.0 %pack_faces.1 = bf16[64,80,128]{2,1,0:T(8,128)(2,1)} custom-call(s32[64]{0:T(128)S(1)} %reshape.238.send_ref, bf16[4,10,32,1024]{3,2,1,0:T(8,128)(2,1)} %bitcast.47), custom_call_target="tpu_custom_call" | custom-call | tf_op jit(solution)/shard_map/pack_faces/pallas_call | solution.py:109
  14.3 11.3 %all-to-all-start = ((bf16[64,80,128]{2,1,0:T(8,128)(2,1)}), bf16[64,80,128]{2,1,0:T(8,128)(2,1)S(1)}, u32[]{:S(2)}, u32[]{:S(2)}) async-start(bf16[64,80,128]{2,1,0:T(8,128)(2,1)} %pack_faces.1), calls=%async_computation.1 | async-start | bytes 2621440 | tf_op jit(solution)/shard_map/all_to_all | solution.py:593
  26.3 1.1 dynamic-slice_bitcast_fusion.refs_0_
  27.6 1.7 %collective-permute-start.1 = (bf16[1,10,32,1024]{3,2,1,0:T(8,128)(2,1)S(1)}, bf16[1,10,32,1024]{3,2,1,0:T(8,128)(2,1)S(1)}, u32[]{:S(2)}, u32[]{:S(2)}) collective-permute-start(bf16[1,10,32,1024]{3,2,1,0:T(8,128)(2,1)S(1)} %dynamic-slice_bitcast_fusion.refs_0_), channel_id=1, source_target_pairs={{0,64},{32,96},{64,0},{96,32},{128,192},{160,224},{192,128},{224,1... | collective-permute-start | bytes 1966088 | tf_op jit(solution)/shard_map/ppermute | solution.py:20
  29.2 2.9 %collective-permute-start.2 = (bf16[1,10,32,1024]{3,2,1,0:T(8,128)(2,1)S(1)}, bf16[1,10,32,1024]{3,2,1,0:T(8,128)(2,1)}, u32[]{:S(2)}, u32[]{:S(2)}) collective-permute-start(bf16[1,10,32,1024]{3,2,1,0:T(8,128)(2,1)S(1)} %dynamic-slice_bitcast_fusion.refs_0_), channel_id=1, source_target_pairs={{0,128},{32,160},{64,192},{96,224},{128,0},{160,32},{192,64},{224,... | collective-permute-start | bytes 1966088 | tf_op jit(solution)/shard_map/ppermute | solution.py:20
  33.3 0.7 fusion.21
  34.1 0.2 select_reduce_fusion
  34.4 0.8 select_maximum_fusion
  35.1 0.7 broadcast_select_fusion.1
  36.0 0.2 fusion.1
  36.4 8.1 %first_substep.1 = (f32[3,10,8,32,128]{4,3,2,1,0:T(8,128)}, bf16[3,80,240]{2,1,0:T(8,128)(2,1)S(1)}) custom-call(s32[56]{0:T(128)S(1)} %pad_add_fusion.1.ints_ref, f32[122]{0:T(128)S(1)} %pad_maximum_fusion.1.vals_ref, bf16[4,10,32,1024]{3,2,1,0:T(8,128)(2,1)} %bitcast.48), custom_call_target="tpu_custom_call" | custom-call | tf_op jit(solution)/shard_map/first_substep/pallas_call | solution.py:299
  44.6 0.6 collective-permute-done.1.refs_2_
  45.2 16.3 %collective-permute-done.2.refs_3_ = bf16[1,10,32,1024]{3,2,1,0:T(8,128)(2,1)} collective-permute-done((bf16[1,10,32,1024]{3,2,1,0:T(8,128)(2,1)S(1)}, bf16[1,10,32,1024]{3,2,1,0:T(8,128)(2,1)}, u32[]{:S(2)}, u32[]{:S(2)}) %collective-permute-start.2) | collective-permute-done | bytes 655392 | tf_op jit(solution)/shard_map/ppermute | solution.py:20
  61.6 0.6 gather_fusion
  62.1 1.1 broadcast_select_fusion
  63.3 5.0 %reduce-scatter.3.cloned.1.call-done = bf16[1,1,16,128]{3,2,1,0:T(8,128)(2,1)} async-done(((bf16[8,1,16,128]{3,2,1,0:T(8,128)(2,1)}), bf16[1,1,16,128]{3,2,1,0:T(8,128)(2,1)}) %reduce-scatter.3.cloned.1.call-update) | async-done | bytes 4112 | tf_op jit(solution)/shard_map/reduce_scatter | solution.py:615
  68.3 1.2 slice.21
  70.1 0.7 fusion.17
  71.0 0.7 fusion.16
  71.8 19.3 %advance_stay.1.refs_5_ = bf16[4,10,32,1024]{3,2,1,0:T(8,128)(2,1)} custom-call(s32[56]{0:T(128)S(1)} %pad_add_fusion.1.ints_ref, f32[122]{0:T(128)S(1)} %pad_maximum_fusion.1.vals_ref, f32[3,10,8,32,128]{4,3,2,1,0:T(8,128)} %get-tuple-element.27.s_ref, bf16[3,80,240]{2,1,0:T(8,128)(2,1)S(1)} %get-tuple-element.28.rk_ref, ...), custom_call_target="tpu_custom_call" | custom-call | tf_op jit(solution)/shard_map/advance_stay/pallas_call | solution.py:459
  91.1 13.1 %reduce-scatter.5.cloned.1.call-done = bf16[1,6,80,128]{3,2,1,0:T(8,128)(2,1)} async-done(((bf16[8,6,80,128]{3,2,1,0:T(8,128)(2,1)}), bf16[1,6,80,128]{3,2,1,0:T(8,128)(2,1)}) %reduce-scatter.5.cloned.1.call-update) | async-done | bytes 122896 | tf_op jit(solution)/shard_map/reduce_scatter | solution.py:615
  104.2 0.9 copy-done
  105.1 8.6 %advance_traded.1 = bf16[4,10,32,1024]{3,2,1,0:T(8,128)(2,1)} custom-call(s32[16]{0:T(128)S(1)} %concatenate.16.ints_ref, f32[113]{0:T(128)S(1)} %pad_maximum_fusion.vals_ref, bf16[1,10,32,1024]{3,2,1,0:T(8,128)(2,1)S(1)} %dynamic-slice_bitcast_fusion.refs_0_, ...), custom_call_target="tpu_custom_call", output_to_operand_aliasing={{}: (7, {})} | custom-call | tf_op jit(solution)/shard_map/advance_traded/pallas_call | solution.py:535
  (57 shorter events, 2.4 us)
Async XLA Ops:
  14.3 17.9 %copy-start.1 = (s32[1,128,6]{1,0,2:T(1,128)S(1)}, s32[1,128,6]{1,0,2:T(1,128)}, u32[]{:S(2)}) copy-start(s32[1,128,6]{1,0,2:T(1,128)} %param.13) | copy-start | bytes 9220
  14.3 18.7 %copy-start.5 = (s32[1,128]{1,0:T(1,128)S(1)}, s32[1,128]{1,0:T(1,128)}, u32[]{:S(2)}) copy-start(s32[1,128]{1,0:T(1,128)} %param.9) | copy-start | bytes 1540
  14.3 19.0 %copy-start.4 = (bf16[1,4,3]{2,1,0:T(4,128)(2,1)S(1)}, bf16[1,4,3]{2,1,0:T(4,128)(2,1)}, u32[]{:S(2)}) copy-start(bf16[1,4,3]{2,1,0:T(4,128)(2,1)} %param.10) | copy-start | bytes 76
  14.3 21.6 %copy-start.2 = (f32[10,10]{1,0:T(8,128)S(1)}, f32[10,10]{1,0:T(8,128)}, u32[]{:S(2)}) copy-start(f32[10,10]{1,0:T(8,128)} %param.12) | copy-start | bytes 1204
  14.3 22.1 %copy-start.3 = (f32[10]{0:T(128)S(1)}, f32[10]{0:T(128)}, u32[]{:S(2)}) copy-start(f32[10]{0:T(128)} %param.11) | copy-start | bytes 124
  14.3 47.3 %all-to-all-start = ((bf16[64,80,128]{2,1,0:T(8,128)(2,1)}), bf16[64,80,128]{2,1,0:T(8,128)(2,1)S(1)}, u32[]{:S(2)}, u32[]{:S(2)}) async-start(bf16[64,80,128]{2,1,0:T(8,128)(2,1)} %pack_faces.1), calls=%async_computation.1 | async-start | bytes 2621440 | tf_op jit(solution)/shard_map/all_to_all | solution.py:593
  25.6 42.7 %reduce-scatter.3.cloned.1.call-start = ((), (), s32[]{:S(2)}) async-start(), calls=%async_computation.3 | async-start | bytes 36864 | tf_op jit(solution)/shard_map/reduce_scatter | solution.py:615
  27.5 17.1 %collective-permute-start = (bf16[1,10,32,1024]{3,2,1,0:T(8,128)(2,1)S(1)}, bf16[1,10,32,1024]{3,2,1,0:T(8,128)(2,1)S(1)}, u32[]{:S(2)}, u32[]{:S(2)}) collective-permute-start(bf16[1,10,32,1024]{3,2,1,0:T(8,128)(2,1)S(1)} %dynamic-slice_bitcast_fusion.refs_0_), channel_id=1, source_target_pairs={{0,32},{32,0},{64,96},{96,64},{128,160},{160,128},{192,224},{224,1... | collective-permute-start | bytes 1966088 | tf_op jit(solution)/shard_map/ppermute | solution.py:20
  27.6 17.6 %collective-permute-start.1 = (bf16[1,10,32,1024]{3,2,1,0:T(8,128)(2,1)S(1)}, bf16[1,10,32,1024]{3,2,1,0:T(8,128)(2,1)S(1)}, u32[]{:S(2)}, u32[]{:S(2)}) collective-permute-start(bf16[1,10,32,1024]{3,2,1,0:T(8,128)(2,1)S(1)} %dynamic-slice_bitcast_fusion.refs_0_), channel_id=1, source_target_pairs={{0,64},{32,96},{64,0},{96,32},{128,192},{160,224},{192,128},{224,1... | collective-permute-start | bytes 1966088 | tf_op jit(solution)/shard_map/ppermute | solution.py:20
  29.2 32.3 %collective-permute-start.2 = (bf16[1,10,32,1024]{3,2,1,0:T(8,128)(2,1)S(1)}, bf16[1,10,32,1024]{3,2,1,0:T(8,128)(2,1)}, u32[]{:S(2)}, u32[]{:S(2)}) collective-permute-start(bf16[1,10,32,1024]{3,2,1,0:T(8,128)(2,1)S(1)} %dynamic-slice_bitcast_fusion.refs_0_), channel_id=1, source_target_pairs={{0,128},{32,160},{64,192},{96,224},{128,0},{160,32},{192,64},{224,... | collective-permute-start | bytes 1966088 | tf_op jit(solution)/shard_map/ppermute | solution.py:20
  35.8 68.4 %reduce-scatter.5.cloned.1.call-start = ((), (), s32[]{:S(2)}) async-start(), calls=%async_computation.4 | async-start | bytes 1105920 | tf_op jit(solution)/shard_map/reduce_scatter | solution.py:615
  104.2 0.9 copy-start
Sparse Core Ops, SparseCore 0:
  36.0 32.2 reduce-scatter.2
  71.0 33.1 reduce-scatter.4

commit v7 on v6

--- a/solution.py
+++ b/solution.py
@@ -121,7 +121,7 @@
         out_shape=jax.ShapeDtypeStruct((slots, fields * ROWS, LANES), bf16),
         compiler_params=pltpu.CompilerParams(vmem_limit_bytes=16 << 20),
         name="pack_faces",
-    )(send, in_hbm(blocks))
+    )(send, blocks)
 
 
 class Facts:
@@ -479,35 +479,30 @@
     )(ints, vals, in_hbm(started), own, arrived)
 
 
-def traded_kernel(choices, ints_ref, vals_ref, *refs):
-    raw_refs, layers_ref, refs = refs[:choices], refs[choices], refs[choices + 2 :]
-    o_ref, sa_ref, sb_ref, e_ref, side_ref, rk_ref, raw_ref, layer_ref, sems = refs
+def traded_kernel(choices, ints_ref, vals_ref, own_ref, *refs):
+    raw_refs, layer_refs, refs = refs[:choices], refs[choices : 2 * choices], refs[2 * choices + 1 :]
+    o_ref, sa_ref, sb_ref, e_ref, side_ref, raw_ref, layer_ref, sems = refs
     _, fields, cells, plane = raw_ref.shape
     tiles = plane // LANES
     facts = Facts(ints_ref, vals_ref, 0, 1, fields)
     choice = ints_ref[15]
-    layer_copy = pltpu.make_async_copy(layers_ref, layer_ref, sems.at[1])
-    layer_copy.start()
     for c in range(choices):
 
         @pl.when(choice == c)
         def _():
             raw_copy = pltpu.make_async_copy(raw_refs[c], raw_ref, sems.at[0])
+            layer_copy = pltpu.make_async_copy(layer_refs[c], layer_ref, sems.at[1])
             raw_copy.start()
+            layer_copy.start()
             raw_copy.wait()
-
-    layer_copy.wait()
-
-    def write(at, value):
-        rk_ref[:, at : at + value.shape[1]] = value
-
-    own_matrix(facts, fields, write)
+            layer_copy.wait()
+
     load_block(raw_ref, sa_ref, cells, tiles)
     place_layers(
         lambda face_no: layer_ref[face_no],
         facts, sa_ref, sb_ref, e_ref, side_ref, None, fields, cells, tiles,
     )
-    step = make_step(rk_ref[...], facts, e_ref, side_ref, fields, cells, tiles)
+    step = make_step(own_ref[...], facts, e_ref, side_ref, fields, cells, tiles)
     finish = make_finish(o_ref, cells, tiles)
 
     @pl.when(facts.n == 1)
@@ -526,7 +521,29 @@
         finish(sa_ref)
 
 
-def advance_traded(ints, vals, raws, layers, into):
+def matrix_kernel(fields, ints_ref, vals_ref, o_ref):
+    def write(at, value):
+        o_ref[:, at : at + value.shape[1]] = value
+
+    own_matrix(Facts(ints_ref, vals_ref, 0, 1, fields), fields, write)
+
+
+def traded_matrix(ints, vals, fields):
+    shape = (fields * ROWS, 3 * fields * ROWS)
+    return pl.pallas_call(
+        functools.partial(matrix_kernel, fields),
+        grid_spec=pltpu.PrefetchScalarGridSpec(
+            num_scalar_prefetch=2,
+            grid=(1,),
+            in_specs=[],
+            out_specs=pl.BlockSpec(shape, lambda b, i, v: (0, 0)),
+        ),
+        out_shape=jax.ShapeDtypeStruct(shape, bf16),
+        name="traded_matrix",
+    )(ints, vals)
+
+
+def advance_traded(ints, vals, own, raws, layers, into):
     per_dev, fields, cells, plane = into.shape
     tiles = plane // LANES
     choices = len(raws)
@@ -537,21 +554,20 @@
         grid_spec=pltpu.PrefetchScalarGridSpec(
             num_scalar_prefetch=2,
             grid=(1,),
-            in_specs=[anywhere] * (choices + 2),
+            in_specs=[pl.BlockSpec(own.shape, lambda b, i, v: (0, 0))] + [anywhere] * (2 * choices + 1),
             out_specs=pl.BlockSpec((1, fields, cells, plane), lambda b, i, v: (i[14], 0, 0, 0)),
             scratch_shapes=state_scratch(fields, cells, tiles)
             + [
-                pltpu.VMEM((size, 3 * size), bf16),
                 pltpu.VMEM((1, fields, cells, plane), bf16),
                 pltpu.VMEM((6, size, LANES), bf16),
                 pltpu.SemaphoreType.DMA((2,)),
             ],
         ),
         out_shape=jax.ShapeDtypeStruct(into.shape, bf16),
-        input_output_aliases={3 + choices: 0},
+        input_output_aliases={3 + 2 * choices: 0},
         compiler_params=pltpu.CompilerParams(vmem_limit_bytes=20 << 20),
         name="advance_traded",
-    )(ints, vals, *raws, layers, into)
+    )(ints, vals, own, *raws, *layers, into)
 
 
 def plan(wanted, my_index, per_dev):
@@ -607,19 +623,15 @@
     bits = range(lax.axis_size("gx").bit_length() - 1)
     offers = lambda x: [x] + [swapped(x, "gx", bit_no) for bit_no in bits]
 
-    flip = jnp.where(bit_here < 0, 0, jnp.left_shift(1, jnp.maximum(bit_here, 0)))
-    partner = jnp.bitwise_xor(lax.axis_index("gx").astype(jnp.int32), flip)
-
-    def to_partner(x):
-        to = jnp.arange(lax.axis_size("gx"), dtype=jnp.int32)[:, None, None, None] == partner
-        return lax.psum_scatter(jnp.where(to, x[None], 0), "gx", scatter_dimension=0, tiled=True)[0]
-
     raws = offers(lax.dynamic_slice_in_dim(blocks, slot_here, 1, 0))
     label = jnp.concatenate(
         [pick(own_levels, 1).astype(bf16), pick(coarse, 6).astype(bf16), pick(speeds, 3)]
     )
     label = jnp.broadcast_to(jnp.pad(label, (0, LABEL[1] - label.shape[0]))[None], LABEL)
-    label = to_partner(label[None])[0, 0]
+    label, *others = offers(label)
+    for bit_no in bits:
+        label = jnp.where(bit_here == bit_no, others[bit_no], label)
+    label = label[0]
     traded_ints = jnp.concatenate(
         [
             jnp.zeros((1,), jnp.int32),
@@ -633,12 +645,15 @@
     traded_vals = jnp.concatenate([label[7:10].astype(f32), diffusivity, reaction_matrix.reshape(-1)])
 
     stay = first_substep(ints, vals, blocks, 1, per_dev - 1)
-    arrived, stay, raws = lax.optimization_barrier((arrived, stay, raws))
+    own = traded_matrix(traded_ints, traded_vals, fields)
+    arrived, stay, traded_ints, traded_vals, own = lax.optimization_barrier(
+        (arrived, stay, traded_ints, traded_vals, own)
+    )
     layers = jnp.take(arrived, pick(lookup, 6), axis=0, mode="clip")
-    layers = to_partner(layers)
+    layers = offers(layers)
     result = advance_stay(ints, vals, *stay, arrived, plane, 1, per_dev)
     raws, layers, result = lax.optimization_barrier((raws, layers, result))
-    result = advance_traded(traded_ints, traded_vals, raws, layers, result)
+    result = advance_traded(traded_ints, traded_vals, own, raws, layers, result)
     return result[None]
 
 

time: 122 us -> 87 us (0.71)
  waiting for transfers between devices: 35.2 us -> 9.94 us
  between operations: 15.6 us -> 2.42 us
  starting transfers between devices: 16.1 us -> 22.3 us
  other arithmetic: 6.46 us -> 3.85 us
    reduce_scatter x2 -> x0, waiting for transfers between devices: 18.2 us -> none  [to_partner(): lax.psum_scatter(jnp.where(to, x[None], 0), 'gx', scatter_dimension=0, ti...]
    ppermute x3 -> x9, waiting for transfers between devices: 17 us -> 0.02 us  [swapped(): lax.ppermute(x, axis, [(i, i ^ 1 << bit) for i in range(lax.axis_size(axi...]
    all_to_all x1, waiting for transfers between devices: 0.01 us -> 9.92 us  [local(): lax.all_to_all(outgoing, ('gy', 'gz'), split_axis=0, concat_axis=0, tiled...]
    ppermute x3 -> x9, starting transfers between devices: 4.66 us -> 11 us  [swapped(): lax.ppermute(x, axis, [(i, i ^ 1 << bit) for i in range(lax.axis_size(axi...]
    select_n x2, other arithmetic: 1.78 us -> 0.02 us  [the longest x1 0.01 us: plan(): first = jnp.min(jnp.where(match, key, 64 * requests), axis=1) % 64]
    pallas_call x1, Pallas kernels: 6.03 us -> 4.35 us  [pack_faces(): pl.pallas_call(pack_kernel, grid_spec=pltpu.PrefetchScalarGridSpec(num_sc...]
    pallas_call x0 -> x1, Pallas kernels: none -> 1.5 us  [traded_matrix(): pl.pallas_call(functools.partial(matrix_kernel, fields), grid_spec=pltpu....]
  transfers between devices with their start and end apart: 6 -> 10, of which waited for: 4 -> 1; matrix products, arithmetic and copies ran while one was open for 8% -> 8% of each run, Pallas kernels for 23% -> 33%
where the time goes in v7:
time: 87 us; the launch traced here: 86.5 us
  Pallas kernels  41.9 us (48%)
  starting transfers between devices  22.3 us (26%)
  waiting for transfers between devices  9.94 us (11%)
  local copies, waits for them, and re-layouts  6.07 us (7%)
  other arithmetic  3.85 us (4%)
  between operations  2.42 us (3%)
    pallas_call x1, Pallas kernels, advance_stay(): pl.pallas_call(functools.partial(stay_kernel, first, count, per_dev), gri...  19.3 us
    all_to_all x1, starting transfers between devices, local(): lax.all_to_all(outgoing, ('gy', 'gz'), split_axis=0, concat_axis=0, tiled...  11.3 us
    ppermute x9, starting transfers between devices, swapped(): lax.ppermute(x, axis, [(i, i ^ 1 << bit) for i in range(lax.axis_size(axi...  11 us
    all_to_all x1, waiting for transfers between devices, local(): lax.all_to_all(outgoing, ('gy', 'gz'), split_axis=0, concat_axis=0, tiled...  9.92 us
    pallas_call x1, Pallas kernels, advance_traded(): pl.pallas_call(functools.partial(traded_kernel, choices), grid_spec=pltpu...  8.67 us
    pallas_call x1, Pallas kernels, first_substep(): pl.pallas_call(functools.partial(first_kernel, first, per_dev), grid_spec...  8.11 us
    pallas_call x1, Pallas kernels, pack_faces(): pl.pallas_call(pack_kernel, grid_spec=pltpu.PrefetchScalarGridSpec(num_sc...  4.35 us
    unnamed x19, local copies, waits for them, and re-layouts  1.88 us
  transfers between devices with their start and end apart: 10, of which 1 were waited for; matrix products, arithmetic and copies ran while one was open for 8% of the time, Pallas kernels for 33%

profile of v7, /device:TPU:32, one launch (start us, length us, event | category | flops | bytes accessed | tf_op | source)
XLA Modules:
  0.0 86.5 jit_solution(11061018045381739972)
XLA Ops:
  0.3 0.7 select_reduce_fusion.2
  1.7 1.7 %copy-done = bf16[1,4,10,32,1024]{4,3,2,1,0:T(8,128)(2,1)S(1)} copy-done((bf16[1,4,10,32,1024]{4,3,2,1,0:T(8,128)(2,1)S(1)}, bf16[1,4,10,32,1024]{4,3,2,1,0:T(8,128)(2,1)}, u32[]{:S(2)}) %copy-start) | copy-done | bytes 2621464
  3.5 4.3 %pack_faces.1 = bf16[64,80,128]{2,1,0:T(8,128)(2,1)} custom-call(s32[64]{0:T(128)S(1)} %reshape.224.send_ref, bf16[4,10,32,1024]{3,2,1,0:T(8,128)(2,1)S(1)} %bitcast.47), custom_call_target="tpu_custom_call" | custom-call | tf_op jit(solution)/shard_map/pack_faces/pallas_call | solution.py:109
  7.8 11.3 %all-to-all-start = ((bf16[64,80,128]{2,1,0:T(8,128)(2,1)}), bf16[64,80,128]{2,1,0:T(8,128)(2,1)S(1)}, u32[]{:S(2)}, u32[]{:S(2)}) async-start(bf16[64,80,128]{2,1,0:T(8,128)(2,1)} %pack_faces.1), calls=%async_computation | async-start | bytes 2621440 | tf_op jit(solution)/shard_map/all_to_all | solution.py:609
  20.3 0.7 fusion.21
  21.4 0.8 select_maximum_fusion
  22.2 3.2 %collective-permute-start = (bf16[16,128]{1,0:T(8,128)(2,1)S(1)}, bf16[16,128]{1,0:T(8,128)(2,1)S(1)}, u32[]{:S(2)}, u32[]{:S(2)}) collective-permute-start(bf16[16,128]{1,0:T(8,128)(2,1)S(1)} %broadcast_in_dim.47), channel_id=1, source_target_pairs={{0,128},{32,160},{64,192},{96,224},{128,0},{160,32},{192,64},{224,... | collective-permute-start | bytes 12296 | tf_op jit(solution)/shard_map/ppermute | solution.py:20
  25.4 0.7 collective-permute-start.1
  26.1 1.1 %dynamic-slice_bitcast_fusion.refs_0_ = bf16[1,10,32,1024]{3,2,1,0:T(8,128)(2,1)S(1)} fusion(bf16[1,4,10,32,1024]{4,3,2,1,0:T(8,128)(2,1)} %param.8, s32[]{:T(128)S(6)} %select_n.137), kind=kLoop, calls=%fused_computation.1 | loop fusion | bytes 1310724 | tf_op jit(solution)/shard_map/dynamic_slice | solution.py:626
  27.2 0.6 collective-permute-start.3
  27.8 1.3 %collective-permute-start.4 = (bf16[1,10,32,1024]{3,2,1,0:T(8,128)(2,1)S(1)}, bf16[1,10,32,1024]{3,2,1,0:T(8,128)(2,1)S(1)}, u32[]{:S(2)}, u32[]{:S(2)}) collective-permute-start(bf16[1,10,32,1024]{3,2,1,0:T(8,128)(2,1)S(1)} %dynamic-slice_bitcast_fusion.refs_0_), channel_id=1, source_target_pairs={{0,64},{32,96},{64,0},{96,32},{128,192},{160,224},{192,128},{224,1... | collective-permute-start | bytes 1966088 | tf_op jit(solution)/shard_map/ppermute | solution.py:20
  29.3 0.2 fusion.1
  30.4 8.1 %first_substep.1 = (f32[3,10,8,32,128]{4,3,2,1,0:T(8,128)}, bf16[3,80,240]{2,1,0:T(8,128)(2,1)S(1)}) custom-call(s32[56]{0:T(128)S(1)} %pad_add_fusion.1.ints_ref, f32[122]{0:T(128)S(1)} %pad_maximum_fusion.vals_ref, bf16[4,10,32,1024]{3,2,1,0:T(8,128)(2,1)} %bitcast.46), custom_call_target="tpu_custom_call" | custom-call | tf_op jit(solution)/shard_map/first_substep/pallas_call | solution.py:299
  38.5 0.5 collective-permute-start.5
  39.0 0.6 slice.21
  40.3 0.7 concatenate.18.ints_ref
  41.0 0.6 pad_maximum_fusion.1.vals_ref
  41.6 1.5 %traded_matrix.1.own_ref = bf16[80,240]{1,0:T(8,128)(2,1)} custom-call(s32[16]{0:T(128)} %concatenate.18.ints_ref, f32[113]{0:T(128)} %pad_maximum_fusion.1.vals_ref), custom_call_target="tpu_custom_call" | custom-call | tf_op jit(solution)/shard_map/traded_matrix/pallas_call | solution.py:533
  43.1 9.9 %all-to-all-done.arr_ref = bf16[64,80,128]{2,1,0:T(8,128)(2,1)S(1)} async-done(((bf16[64,80,128]{2,1,0:T(8,128)(2,1)}), bf16[64,80,128]{2,1,0:T(8,128)(2,1)S(1)}, u32[]{:S(2)}, u32[]{:S(2)}) %all-to-all-start) | async-done | bytes 1310752 | tf_op jit(solution)/shard_map/all_to_all | solution.py:609
  53.0 0.6 gather_fusion
  53.7 1.7 %collective-permute-start.7 = (bf16[6,80,128]{2,1,0:T(8,128)(2,1)S(1)}, bf16[6,80,128]{2,1,0:T(8,128)(2,1)S(1)}, u32[]{:S(2)}, u32[]{:S(2)}) collective-permute-start(bf16[6,80,128]{2,1,0:T(8,128)(2,1)S(1)} %gather_fusion), channel_id=1, source_target_pairs={{0,64},{32,96},{64,0},{96,32},{128,192},{160,224},{192,128},{224,1... | collective-permute-start | bytes 368648 | tf_op jit(solution)/shard_map/ppermute | solution.py:20
  55.4 2.9 %collective-permute-start.8 = (bf16[6,80,128]{2,1,0:T(8,128)(2,1)S(1)}, bf16[6,80,128]{2,1,0:T(8,128)(2,1)S(1)}, u32[]{:S(2)}, u32[]{:S(2)}) collective-permute-start(bf16[6,80,128]{2,1,0:T(8,128)(2,1)S(1)} %gather_fusion), channel_id=1, source_target_pairs={{0,128},{32,160},{64,192},{96,224},{128,0},{160,32},{192,64},{224,... | collective-permute-start | bytes 368648 | tf_op jit(solution)/shard_map/ppermute | solution.py:20
  58.3 19.3 %advance_stay.1.refs_8_ = bf16[4,10,32,1024]{3,2,1,0:T(8,128)(2,1)} custom-call(s32[56]{0:T(128)S(1)} %pad_add_fusion.1.ints_ref, f32[122]{0:T(128)S(1)} %pad_maximum_fusion.vals_ref, f32[3,10,8,32,128]{4,3,2,1,0:T(8,128)} %get-tuple-element.28.s_ref, bf16[3,80,240]{2,1,0:T(8,128)(2,1)S(1)} %get-tuple-element.29.rk_ref, ...), custom_call_target="tpu_custom_call" | custom-call | tf_op jit(solution)/shard_map/advance_stay/pallas_call | solution.py:459
  77.7 8.7 %advance_traded.1 = bf16[4,10,32,1024]{3,2,1,0:T(8,128)(2,1)} custom-call(s32[16]{0:T(128)S(1)} %copy-done.2, f32[113]{0:T(128)S(1)} %copy-done.3, bf16[80,240]{1,0:T(8,128)(2,1)S(1)} %copy-done.1, bf16[1,10,32,1024]{3,2,1,0:T(8,128)(2,1)S(1)} %dynamic-slice_bitcast_fusion.refs_0_, ...), custom_call_target="tpu_custom_call", output_to_operand_aliasing={{}: (11, {})} | custom-call | tf_op jit(solution)/shard_map/advance_traded/pallas_call | solution.py:552
  (69 shorter events, 2.4 us)
Async XLA Ops:
  1.7 1.7 %copy-start = (bf16[1,4,10,32,1024]{4,3,2,1,0:T(8,128)(2,1)S(1)}, bf16[1,4,10,32,1024]{4,3,2,1,0:T(8,128)(2,1)}, u32[]{:S(2)}) copy-start(bf16[1,4,10,32,1024]{4,3,2,1,0:T(8,128)(2,1)} %param.8) | copy-start | bytes 7864324
  3.5 15.7 %copy-start.8 = (s32[1,128]{1,0:T(1,128)S(1)}, s32[1,128]{1,0:T(1,128)}, u32[]{:S(2)}) copy-start(s32[1,128]{1,0:T(1,128)} %param.9) | copy-start | bytes 1540
  3.5 15.8 %copy-start.4 = (s32[1,128,6]{1,0,2:T(1,128)S(1)}, s32[1,128,6]{1,0,2:T(1,128)}, u32[]{:S(2)}) copy-start(s32[1,128,6]{1,0,2:T(1,128)} %param.13) | copy-start | bytes 9220
  3.5 17.5 %copy-start.7 = (bf16[1,4,3]{2,1,0:T(4,128)(2,1)S(1)}, bf16[1,4,3]{2,1,0:T(4,128)(2,1)}, u32[]{:S(2)}) copy-start(bf16[1,4,3]{2,1,0:T(4,128)(2,1)} %param.10) | copy-start | bytes 76
  7.8 21.3 %copy-start.5 = (f32[10,10]{1,0:T(8,128)S(1)}, f32[10,10]{1,0:T(8,128)}, u32[]{:S(2)}) copy-start(f32[10,10]{1,0:T(8,128)} %param.12) | copy-start | bytes 1204
  7.8 21.8 %copy-start.6 = (f32[10]{0:T(128)S(1)}, f32[10]{0:T(128)}, u32[]{:S(2)}) copy-start(f32[10]{0:T(128)} %param.11) | copy-start | bytes 124
  7.8 45.2 %all-to-all-start = ((bf16[64,80,128]{2,1,0:T(8,128)(2,1)}), bf16[64,80,128]{2,1,0:T(8,128)(2,1)S(1)}, u32[]{:S(2)}, u32[]{:S(2)}) async-start(bf16[64,80,128]{2,1,0:T(8,128)(2,1)} %pack_faces.1), calls=%async_computation | async-start | bytes 2621440 | tf_op jit(solution)/shard_map/all_to_all | solution.py:609
  22.2 16.3 %collective-permute-start = (bf16[16,128]{1,0:T(8,128)(2,1)S(1)}, bf16[16,128]{1,0:T(8,128)(2,1)S(1)}, u32[]{:S(2)}, u32[]{:S(2)}) collective-permute-start(bf16[16,128]{1,0:T(8,128)(2,1)S(1)} %broadcast_in_dim.47), channel_id=1, source_target_pairs={{0,128},{32,160},{64,192},{96,224},{128,0},{160,32},{192,64},{224,... | collective-permute-start | bytes 12296 | tf_op jit(solution)/shard_map/ppermute | solution.py:20
  25.4 13.6 %collective-permute-start.1 = (bf16[16,128]{1,0:T(8,128)(2,1)S(1)}, bf16[16,128]{1,0:T(8,128)(2,1)S(1)}, u32[]{:S(2)}, u32[]{:S(2)}) collective-permute-start(bf16[16,128]{1,0:T(8,128)(2,1)S(1)} %broadcast_in_dim.47), channel_id=1, source_target_pairs={{0,64},{32,96},{64,0},{96,32},{128,192},{160,224},{192,128},{224,1... | collective-permute-start | bytes 12296 | tf_op jit(solution)/shard_map/ppermute | solution.py:20
  26.1 12.9 %collective-permute-start.2 = (bf16[16,128]{1,0:T(8,128)(2,1)S(1)}, bf16[16,128]{1,0:T(8,128)(2,1)S(1)}, u32[]{:S(2)}, u32[]{:S(2)}) collective-permute-start(bf16[16,128]{1,0:T(8,128)(2,1)S(1)} %broadcast_in_dim.47), channel_id=1, source_target_pairs={{0,32},{32,0},{64,96},{96,64},{128,160},{160,128},{192,224},{224,1... | collective-permute-start | bytes 12296 | tf_op jit(solution)/shard_map/ppermute | solution.py:20
  27.2 28.2 %collective-permute-start.3 = (bf16[1,10,32,1024]{3,2,1,0:T(8,128)(2,1)S(1)}, bf16[1,10,32,1024]{3,2,1,0:T(8,128)(2,1)S(1)}, u32[]{:S(2)}, u32[]{:S(2)}) collective-permute-start(bf16[1,10,32,1024]{3,2,1,0:T(8,128)(2,1)S(1)} %dynamic-slice_bitcast_fusion.refs_0_), channel_id=1, source_target_pairs={{0,32},{32,0},{64,96},{96,64},{128,160},{160,128},{192,224},{224,1... | collective-permute-start | bytes 1966088 | tf_op jit(solution)/shard_map/ppermute | solution.py:20
  27.8 49.8 %collective-permute-start.4 = (bf16[1,10,32,1024]{3,2,1,0:T(8,128)(2,1)S(1)}, bf16[1,10,32,1024]{3,2,1,0:T(8,128)(2,1)S(1)}, u32[]{:S(2)}, u32[]{:S(2)}) collective-permute-start(bf16[1,10,32,1024]{3,2,1,0:T(8,128)(2,1)S(1)} %dynamic-slice_bitcast_fusion.refs_0_), channel_id=1, source_target_pairs={{0,64},{32,96},{64,0},{96,32},{128,192},{160,224},{192,128},{224,1... | collective-permute-start | bytes 1966088 | tf_op jit(solution)/shard_map/ppermute | solution.py:20
  38.5 39.2 %collective-permute-start.5 = (bf16[1,10,32,1024]{3,2,1,0:T(8,128)(2,1)S(1)}, bf16[1,10,32,1024]{3,2,1,0:T(8,128)(2,1)}, u32[]{:S(2)}, u32[]{:S(2)}) collective-permute-start(bf16[1,10,32,1024]{3,2,1,0:T(8,128)(2,1)S(1)} %dynamic-slice_bitcast_fusion.refs_0_), channel_id=1, source_target_pairs={{0,128},{32,160},{64,192},{96,224},{128,0},{160,32},{192,64},{224,... | collective-permute-start | bytes 1966088 | tf_op jit(solution)/shard_map/ppermute | solution.py:20
  53.6 24.1 %copy-start.1 = (bf16[80,240]{1,0:T(8,128)(2,1)S(1)}, bf16[80,240]{1,0:T(8,128)(2,1)}, u32[]{:S(2)}) copy-start(bf16[80,240]{1,0:T(8,128)(2,1)} %traded_matrix.1.own_ref) | copy-start | bytes 115204
  53.6 24.1 %copy-start.2 = (s32[16]{0:T(128)S(1)}, s32[16]{0:T(128)}, u32[]{:S(2)}) copy-start(s32[16]{0:T(128)} %concatenate.18.ints_ref) | copy-start | bytes 196
  53.6 24.1 %copy-start.3 = (f32[113]{0:T(128)S(1)}, f32[113]{0:T(128)}, u32[]{:S(2)}) copy-start(f32[113]{0:T(128)} %pad_maximum_fusion.1.vals_ref) | copy-start | bytes 1360
  53.6 24.0 %collective-permute-start.6 = (bf16[6,80,128]{2,1,0:T(8,128)(2,1)S(1)}, bf16[6,80,128]{2,1,0:T(8,128)(2,1)S(1)}, u32[]{:S(2)}, u32[]{:S(2)}) collective-permute-start(bf16[6,80,128]{2,1,0:T(8,128)(2,1)S(1)} %gather_fusion), channel_id=1, source_target_pairs={{0,32},{32,0},{64,96},{96,64},{128,160},{160,128},{192,224},{224,1... | collective-permute-start | bytes 368648 | tf_op jit(solution)/shard_map/ppermute | solution.py:20
  53.7 23.9 %collective-permute-start.7 = (bf16[6,80,128]{2,1,0:T(8,128)(2,1)S(1)}, bf16[6,80,128]{2,1,0:T(8,128)(2,1)S(1)}, u32[]{:S(2)}, u32[]{:S(2)}) collective-permute-start(bf16[6,80,128]{2,1,0:T(8,128)(2,1)S(1)} %gather_fusion), channel_id=1, source_target_pairs={{0,64},{32,96},{64,0},{96,32},{128,192},{160,224},{192,128},{224,1... | collective-permute-start | bytes 368648 | tf_op jit(solution)/shard_map/ppermute | solution.py:20
  55.4 22.2 %collective-permute-start.8 = (bf16[6,80,128]{2,1,0:T(8,128)(2,1)S(1)}, bf16[6,80,128]{2,1,0:T(8,128)(2,1)S(1)}, u32[]{:S(2)}, u32[]{:S(2)}) collective-permute-start(bf16[6,80,128]{2,1,0:T(8,128)(2,1)S(1)} %gather_fusion), channel_id=1, source_target_pairs={{0,128},{32,160},{64,192},{96,224},{128,0},{160,32},{192,64},{224,... | collective-permute-start | bytes 368648 | tf_op jit(solution)/shard_map/ppermute | solution.py:20

commit v8 on v4

--- a/solution.py
+++ b/solution.py
@@ -252,7 +252,7 @@
                     put(f, t, it, near + (c + own_terms))
         return carry
 
-    lax.fori_loop(0, tiles // 2, two_tiles, 0)
+    lax.fori_loop(0, tiles // 2, two_tiles, 0, unroll=2)
 
 
 def first_kernel(first, per_dev, ints_ref, vals_ref, u_ref, o_ref, rk_out_ref, sa_ref):
@@ -610,7 +610,7 @@
     arrived, stay, traded_ints, traded_vals = lax.optimization_barrier(
         (arrived, stay, traded_ints, traded_vals)
     )
-    layers = offers(jnp.take(arrived, pick(lookup, 6), axis=0))
+    layers = offers(jnp.take(arrived, pick(lookup, 6), axis=0, mode="clip"))
     result = advance_stay(ints, vals, *stay, arrived, plane, 1, per_dev)
     raws, layers, result = lax.optimization_barrier((raws, layers, result))
     result = advance_traded(traded_ints, traded_vals, raws, layers, result)

time: 86.2 us -> 84 us (0.974)
  Pallas kernels: 41.3 us -> 38.7 us
    pallas_call x1, Pallas kernels: 18.3 us -> 16.9 us  [advance_stay(): pl.pallas_call(functools.partial(stay_kernel, first, per_dev), grid_spec=...]
  transfers between devices with their start and end apart: 10 -> 10, of which waited for: 1 -> 1; matrix products, arithmetic and copies ran while one was open for 6% -> 6% of each run, Pallas kernels for 31% -> 29%
where the time goes in v8:
time: 84 us; the launch traced here: 83.4 us
  Pallas kernels  38.7 us (46%)
  starting transfers between devices  22.3 us (27%)
  waiting for transfers between devices  13.1 us (16%)
  local copies, waits for them, and re-layouts  3.7 us (4%)
  other arithmetic  3.27 us (4%)
  between operations  2.36 us (3%)
    pallas_call x1, Pallas kernels, advance_stay(): pl.pallas_call(functools.partial(stay_kernel, first, per_dev), grid_spec=...  16.9 us
    all_to_all x1, waiting for transfers between devices, local(): lax.all_to_all(outgoing, ('gy', 'gz'), split_axis=0, concat_axis=0, tiled...  13.1 us
    all_to_all x1, starting transfers between devices, local(): lax.all_to_all(outgoing, ('gy', 'gz'), split_axis=0, concat_axis=0, tiled...  11.3 us
    ppermute x9, starting transfers between devices, swapped(): lax.ppermute(x, axis, [(i, i ^ 1 << bit) for i in range(lax.axis_size(axi...  11 us
    pallas_call x1, Pallas kernels, advance_traded(): pl.pallas_call(functools.partial(traded_kernel, choices), grid_spec=pltpu...  8.09 us
    pallas_call x1, Pallas kernels, first_substep(): pl.pallas_call(functools.partial(first_kernel, first, per_dev), grid_spec...  7.66 us
    pallas_call x1, Pallas kernels, pack_faces(): pl.pallas_call(pack_kernel, grid_spec=pltpu.PrefetchScalarGridSpec(num_sc...  6.02 us
  transfers between devices with their start and end apart: 10, of which 1 were waited for; matrix products, arithmetic and copies ran while one was open for 6% of the time, Pallas kernels for 29%

profile of v8, /device:TPU:32, one launch (start us, length us, event | category | flops | bytes accessed | tf_op | source)
XLA Modules:
  0.0 83.4 jit_solution(10402290525863876047)
XLA Ops:
  0.3 0.7 select_reduce_fusion.2
  1.1 0.1 reduce_max.20
  1.4 0.1 reduce_min.20
  1.8 6.0 %pack_faces.1 = bf16[64,80,128]{2,1,0:T(8,128)(2,1)} custom-call(s32[64]{0:T(128)S(1)} %reshape.224.send_ref, bf16[4,10,32,1024]{3,2,1,0:T(8,128)(2,1)} %bitcast.46), custom_call_target="tpu_custom_call" | custom-call | tf_op jit(solution)/shard_map/pack_faces/pallas_call | solution.py:109
  7.8 11.3 %all-to-all-start = ((bf16[64,80,128]{2,1,0:T(8,128)(2,1)}), bf16[64,80,128]{2,1,0:T(8,128)(2,1)S(1)}, u32[]{:S(2)}, u32[]{:S(2)}) async-start(bf16[64,80,128]{2,1,0:T(8,128)(2,1)} %pack_faces.1), calls=%async_computation | async-start | bytes 2621440 | tf_op jit(solution)/shard_map/all_to_all | solution.py:571
  19.2 0.1 copy.22
  20.2 0.7 fusion.21
  21.1 0.2 select_reduce_fusion
  21.3 0.7 select_maximum_fusion
  22.0 3.2 %collective-permute-start = (bf16[16,128]{1,0:T(8,128)(2,1)S(1)}, bf16[16,128]{1,0:T(8,128)(2,1)S(1)}, u32[]{:S(2)}, u32[]{:S(2)}) collective-permute-start(bf16[16,128]{1,0:T(8,128)(2,1)S(1)} %broadcast_in_dim.47), channel_id=1, source_target_pairs={{0,128},{32,160},{64,192},{96,224},{128,0},{160,32},{192,64},{224,... | collective-permute-start | bytes 12296 | tf_op jit(solution)/shard_map/ppermute | solution.py:20
  25.3 0.7 collective-permute-start.1
  26.0 1.1 %dynamic-slice_bitcast_fusion.refs_0_ = bf16[1,10,32,1024]{3,2,1,0:T(8,128)(2,1)S(1)} fusion(bf16[1,4,10,32,1024]{4,3,2,1,0:T(8,128)(2,1)} %param.8, s32[]{:T(128)S(6)} %select_n.137), kind=kLoop, calls=%fused_computation.1 | loop fusion | bytes 1310724 | tf_op jit(solution)/shard_map/dynamic_slice | solution.py:588
  27.1 0.6 collective-permute-start.3
  27.7 1.3 %collective-permute-start.4 = (bf16[1,10,32,1024]{3,2,1,0:T(8,128)(2,1)S(1)}, bf16[1,10,32,1024]{3,2,1,0:T(8,128)(2,1)S(1)}, u32[]{:S(2)}, u32[]{:S(2)}) collective-permute-start(bf16[1,10,32,1024]{3,2,1,0:T(8,128)(2,1)S(1)} %dynamic-slice_bitcast_fusion.refs_0_), channel_id=1, source_target_pairs={{0,64},{32,96},{64,0},{96,32},{128,192},{160,224},{192,128},{224,1... | collective-permute-start | bytes 1966088 | tf_op jit(solution)/shard_map/ppermute | solution.py:20
  29.1 0.2 fusion.1
  30.3 7.7 %first_substep.1 = (f32[3,10,8,32,128]{4,3,2,1,0:T(8,128)}, bf16[3,80,240]{2,1,0:T(8,128)(2,1)S(1)}) custom-call(s32[56]{0:T(128)S(1)} %pad_add_fusion.1.ints_ref, f32[122]{0:T(128)S(1)} %pad_maximum_fusion.vals_ref, bf16[4,10,32,1024]{3,2,1,0:T(8,128)(2,1)} %bitcast.47), custom_call_target="tpu_custom_call" | custom-call | tf_op jit(solution)/shard_map/first_substep/pallas_call | solution.py:299
  37.9 0.5 collective-permute-start.5
  38.4 0.5 slice.21
  39.9 13.1 %all-to-all-done.arr_ref = bf16[64,80,128]{2,1,0:T(8,128)(2,1)S(1)} async-done(((bf16[64,80,128]{2,1,0:T(8,128)(2,1)}), bf16[64,80,128]{2,1,0:T(8,128)(2,1)S(1)}, u32[]{:S(2)}, u32[]{:S(2)}) %all-to-all-start) | async-done | bytes 1310752 | tf_op jit(solution)/shard_map/all_to_all | solution.py:571
  53.0 0.6 gather_fusion
  53.7 1.7 %collective-permute-start.7 = (bf16[6,80,128]{2,1,0:T(8,128)(2,1)S(1)}, bf16[6,80,128]{2,1,0:T(8,128)(2,1)S(1)}, u32[]{:S(2)}, u32[]{:S(2)}) collective-permute-start(bf16[6,80,128]{2,1,0:T(8,128)(2,1)S(1)} %gather_fusion), channel_id=1, source_target_pairs={{0,64},{32,96},{64,0},{96,32},{128,192},{160,224},{192,128},{224,1... | collective-permute-start | bytes 368648 | tf_op jit(solution)/shard_map/ppermute | solution.py:20
  55.3 2.9 %collective-permute-start.8 = (bf16[6,80,128]{2,1,0:T(8,128)(2,1)S(1)}, bf16[6,80,128]{2,1,0:T(8,128)(2,1)S(1)}, u32[]{:S(2)}, u32[]{:S(2)}) collective-permute-start(bf16[6,80,128]{2,1,0:T(8,128)(2,1)S(1)} %gather_fusion), channel_id=1, source_target_pairs={{0,128},{32,160},{64,192},{96,224},{128,0},{160,32},{192,64},{224,... | collective-permute-start | bytes 368648 | tf_op jit(solution)/shard_map/ppermute | solution.py:20
  58.2 16.9 %advance_stay.1.refs_8_ = bf16[4,10,32,1024]{3,2,1,0:T(8,128)(2,1)} custom-call(s32[56]{0:T(128)S(1)} %pad_add_fusion.1.ints_ref, f32[122]{0:T(128)S(1)} %pad_maximum_fusion.vals_ref, f32[3,10,8,32,128]{4,3,2,1,0:T(8,128)} %get-tuple-element.26.s_ref, bf16[3,80,240]{2,1,0:T(8,128)(2,1)S(1)} %get-tuple-element.27.rk_ref, ...), custom_call_target="tpu_custom_call" | custom-call | tf_op jit(solution)/shard_map/advance_stay/pallas_call | solution.py:442
  75.2 8.1 %advance_traded.1 = bf16[4,10,32,1024]{3,2,1,0:T(8,128)(2,1)} custom-call(s32[16]{0:T(128)S(1)} %concatenate.18.ints_ref, f32[113]{0:T(128)S(1)} %pad_maximum_fusion.1.vals_ref, bf16[1,10,32,1024]{3,2,1,0:T(8,128)(2,1)S(1)} %dynamic-slice_bitcast_fusion.refs_0_, ...), custom_call_target="tpu_custom_call", output_to_operand_aliasing={{}: (10, {})} | custom-call | tf_op jit(solution)/shard_map/advance_traded/pallas_call | solution.py:513
  (60 shorter events, 2.1 us)
Async XLA Ops:
  1.7 17.4 %copy-start.4 = (s32[1,128]{1,0:T(1,128)S(1)}, s32[1,128]{1,0:T(1,128)}, u32[]{:S(2)}) copy-start(s32[1,128]{1,0:T(1,128)} %param.9) | copy-start | bytes 1540
  1.7 17.5 %copy-start = (s32[1,128,6]{1,0,2:T(1,128)S(1)}, s32[1,128,6]{1,0,2:T(1,128)}, u32[]{:S(2)}) copy-start(s32[1,128,6]{1,0,2:T(1,128)} %param.13) | copy-start | bytes 9220
  1.7 19.1 %copy-start.3 = (bf16[1,4,3]{2,1,0:T(4,128)(2,1)S(1)}, bf16[1,4,3]{2,1,0:T(4,128)(2,1)}, u32[]{:S(2)}) copy-start(bf16[1,4,3]{2,1,0:T(4,128)(2,1)} %param.10) | copy-start | bytes 76
  7.8 21.3 %copy-start.1 = (f32[10,10]{1,0:T(8,128)S(1)}, f32[10,10]{1,0:T(8,128)}, u32[]{:S(2)}) copy-start(f32[10,10]{1,0:T(8,128)} %param.12) | copy-start | bytes 1204
  7.8 21.7 %copy-start.2 = (f32[10]{0:T(128)S(1)}, f32[10]{0:T(128)}, u32[]{:S(2)}) copy-start(f32[10]{0:T(128)} %param.11) | copy-start | bytes 124
  7.8 45.2 %all-to-all-start = ((bf16[64,80,128]{2,1,0:T(8,128)(2,1)}), bf16[64,80,128]{2,1,0:T(8,128)(2,1)S(1)}, u32[]{:S(2)}, u32[]{:S(2)}) async-start(bf16[64,80,128]{2,1,0:T(8,128)(2,1)} %pack_faces.1), calls=%async_computation | async-start | bytes 2621440 | tf_op jit(solution)/shard_map/all_to_all | solution.py:571
  22.0 15.9 %collective-permute-start = (bf16[16,128]{1,0:T(8,128)(2,1)S(1)}, bf16[16,128]{1,0:T(8,128)(2,1)S(1)}, u32[]{:S(2)}, u32[]{:S(2)}) collective-permute-start(bf16[16,128]{1,0:T(8,128)(2,1)S(1)} %broadcast_in_dim.47), channel_id=1, source_target_pairs={{0,128},{32,160},{64,192},{96,224},{128,0},{160,32},{192,64},{224,... | collective-permute-start | bytes 12296 | tf_op jit(solution)/shard_map/ppermute | solution.py:20
  25.3 13.1 %collective-permute-start.1 = (bf16[16,128]{1,0:T(8,128)(2,1)S(1)}, bf16[16,128]{1,0:T(8,128)(2,1)S(1)}, u32[]{:S(2)}, u32[]{:S(2)}) collective-permute-start(bf16[16,128]{1,0:T(8,128)(2,1)S(1)} %broadcast_in_dim.47), channel_id=1, source_target_pairs={{0,64},{32,96},{64,0},{96,32},{128,192},{160,224},{192,128},{224,1... | collective-permute-start | bytes 12296 | tf_op jit(solution)/shard_map/ppermute | solution.py:20
  25.9 12.5 %collective-permute-start.2 = (bf16[16,128]{1,0:T(8,128)(2,1)S(1)}, bf16[16,128]{1,0:T(8,128)(2,1)S(1)}, u32[]{:S(2)}, u32[]{:S(2)}) collective-permute-start(bf16[16,128]{1,0:T(8,128)(2,1)S(1)} %broadcast_in_dim.47), channel_id=1, source_target_pairs={{0,32},{32,0},{64,96},{96,64},{128,160},{160,128},{192,224},{224,1... | collective-permute-start | bytes 12296 | tf_op jit(solution)/shard_map/ppermute | solution.py:20
  27.1 28.2 %collective-permute-start.3 = (bf16[1,10,32,1024]{3,2,1,0:T(8,128)(2,1)S(1)}, bf16[1,10,32,1024]{3,2,1,0:T(8,128)(2,1)S(1)}, u32[]{:S(2)}, u32[]{:S(2)}) collective-permute-start(bf16[1,10,32,1024]{3,2,1,0:T(8,128)(2,1)S(1)} %dynamic-slice_bitcast_fusion.refs_0_), channel_id=1, source_target_pairs={{0,32},{32,0},{64,96},{96,64},{128,160},{160,128},{192,224},{224,1... | collective-permute-start | bytes 1966088 | tf_op jit(solution)/shard_map/ppermute | solution.py:20
  27.7 47.5 %collective-permute-start.4 = (bf16[1,10,32,1024]{3,2,1,0:T(8,128)(2,1)S(1)}, bf16[1,10,32,1024]{3,2,1,0:T(8,128)(2,1)S(1)}, u32[]{:S(2)}, u32[]{:S(2)}) collective-permute-start(bf16[1,10,32,1024]{3,2,1,0:T(8,128)(2,1)S(1)} %dynamic-slice_bitcast_fusion.refs_0_), channel_id=1, source_target_pairs={{0,64},{32,96},{64,0},{96,32},{128,192},{160,224},{192,128},{224,1... | collective-permute-start | bytes 1966088 | tf_op jit(solution)/shard_map/ppermute | solution.py:20
  37.9 37.2 %collective-permute-start.5 = (bf16[1,10,32,1024]{3,2,1,0:T(8,128)(2,1)S(1)}, bf16[1,10,32,1024]{3,2,1,0:T(8,128)(2,1)}, u32[]{:S(2)}, u32[]{:S(2)}) collective-permute-start(bf16[1,10,32,1024]{3,2,1,0:T(8,128)(2,1)S(1)} %dynamic-slice_bitcast_fusion.refs_0_), channel_id=1, source_target_pairs={{0,128},{32,160},{64,192},{96,224},{128,0},{160,32},{192,64},{224,... | collective-permute-start | bytes 1966088 | tf_op jit(solution)/shard_map/ppermute | solution.py:20
  53.6 21.6 %collective-permute-start.6 = (bf16[6,80,128]{2,1,0:T(8,128)(2,1)S(1)}, bf16[6,80,128]{2,1,0:T(8,128)(2,1)S(1)}, u32[]{:S(2)}, u32[]{:S(2)}) collective-permute-start(bf16[6,80,128]{2,1,0:T(8,128)(2,1)S(1)} %gather_fusion), channel_id=1, source_target_pairs={{0,32},{32,0},{64,96},{96,64},{128,160},{160,128},{192,224},{224,1... | collective-permute-start | bytes 368648 | tf_op jit(solution)/shard_map/ppermute | solution.py:20
  53.7 21.5 %collective-permute-start.7 = (bf16[6,80,128]{2,1,0:T(8,128)(2,1)S(1)}, bf16[6,80,128]{2,1,0:T(8,128)(2,1)S(1)}, u32[]{:S(2)}, u32[]{:S(2)}) collective-permute-start(bf16[6,80,128]{2,1,0:T(8,128)(2,1)S(1)} %gather_fusion), channel_id=1, source_target_pairs={{0,64},{32,96},{64,0},{96,32},{128,192},{160,224},{192,128},{224,1... | collective-permute-start | bytes 368648 | tf_op jit(solution)/shard_map/ppermute | solution.py:20
  55.3 19.8 %collective-permute-start.8 = (bf16[6,80,128]{2,1,0:T(8,128)(2,1)S(1)}, bf16[6,80,128]{2,1,0:T(8,128)(2,1)S(1)}, u32[]{:S(2)}, u32[]{:S(2)}) collective-permute-start(bf16[6,80,128]{2,1,0:T(8,128)(2,1)S(1)} %gather_fusion), channel_id=1, source_target_pairs={{0,128},{32,160},{64,192},{96,224},{128,0},{160,32},{192,64},{224,... | collective-permute-start | bytes 368648 | tf_op jit(solution)/shard_map/ppermute | solution.py:20

commit v9 on v8

--- a/solution.py
+++ b/solution.py
@@ -252,7 +252,7 @@
                     put(f, t, it, near + (c + own_terms))
         return carry
 
-    lax.fori_loop(0, tiles // 2, two_tiles, 0, unroll=2)
+    lax.fori_loop(0, tiles // 2, two_tiles, 0, unroll=4)
 
 
 def first_kernel(first, per_dev, ints_ref, vals_ref, u_ref, o_ref, rk_out_ref, sa_ref):

time: 84 us -> 83.4 us (level)
  no operation moved by 1% of the time
where the time goes in v9:
time: 83.4 us; the launch traced here: 82.9 us
  Pallas kernels  38.2 us (46%)
  starting transfers between devices  22.3 us (27%)
  waiting for transfers between devices  13 us (16%)
  local copies, waits for them, and re-layouts  3.7 us (4%)
  other arithmetic  3.27 us (4%)
  between operations  2.36 us (3%)
    pallas_call x1, Pallas kernels, advance_stay(): pl.pallas_call(functools.partial(stay_kernel, first, per_dev), grid_spec=...  16.6 us
    all_to_all x1, waiting for transfers between devices, local(): lax.all_to_all(outgoing, ('gy', 'gz'), split_axis=0, concat_axis=0, tiled...  13 us
    all_to_all x1, starting transfers between devices, local(): lax.all_to_all(outgoing, ('gy', 'gz'), split_axis=0, concat_axis=0, tiled...  11.3 us
    ppermute x9, starting transfers between devices, swapped(): lax.ppermute(x, axis, [(i, i ^ 1 << bit) for i in range(lax.axis_size(axi...  11 us
    pallas_call x1, Pallas kernels, advance_traded(): pl.pallas_call(functools.partial(traded_kernel, choices), grid_spec=pltpu...  7.85 us
    pallas_call x1, Pallas kernels, first_substep(): pl.pallas_call(functools.partial(first_kernel, first, per_dev), grid_spec...  7.72 us
    pallas_call x1, Pallas kernels, pack_faces(): pl.pallas_call(pack_kernel, grid_spec=pltpu.PrefetchScalarGridSpec(num_sc...  6.02 us
  transfers between devices with their start and end apart: 10, of which 1 were waited for; matrix products, arithmetic and copies ran while one was open for 6% of the time, Pallas kernels for 29%

profile of v9, /device:TPU:32, one launch (start us, length us, event | category | flops | bytes accessed | tf_op | source)
XLA Modules:
  0.0 82.9 jit_solution(1281116282717893799)
XLA Ops:
  0.3 0.7 select_reduce_fusion.2
  1.1 0.1 reduce_max.20
  1.4 0.1 reduce_min.20
  1.8 6.0 %pack_faces.1 = bf16[64,80,128]{2,1,0:T(8,128)(2,1)} custom-call(s32[64]{0:T(128)S(1)} %reshape.224.send_ref, bf16[4,10,32,1024]{3,2,1,0:T(8,128)(2,1)} %bitcast.46), custom_call_target="tpu_custom_call" | custom-call | tf_op jit(solution)/shard_map/pack_faces/pallas_call | solution.py:109
  7.8 11.3 %all-to-all-start = ((bf16[64,80,128]{2,1,0:T(8,128)(2,1)}), bf16[64,80,128]{2,1,0:T(8,128)(2,1)S(1)}, u32[]{:S(2)}, u32[]{:S(2)}) async-start(bf16[64,80,128]{2,1,0:T(8,128)(2,1)} %pack_faces.1), calls=%async_computation | async-start | bytes 2621440 | tf_op jit(solution)/shard_map/all_to_all | solution.py:571
  19.2 0.1 copy.22
  20.2 0.7 fusion.21
  21.1 0.2 select_reduce_fusion
  21.3 0.7 select_maximum_fusion
  22.0 3.2 %collective-permute-start = (bf16[16,128]{1,0:T(8,128)(2,1)S(1)}, bf16[16,128]{1,0:T(8,128)(2,1)S(1)}, u32[]{:S(2)}, u32[]{:S(2)}) collective-permute-start(bf16[16,128]{1,0:T(8,128)(2,1)S(1)} %broadcast_in_dim.47), channel_id=1, source_target_pairs={{0,128},{32,160},{64,192},{96,224},{128,0},{160,32},{192,64},{224,... | collective-permute-start | bytes 12296 | tf_op jit(solution)/shard_map/ppermute | solution.py:20
  25.3 0.7 collective-permute-start.1
  26.0 1.1 %dynamic-slice_bitcast_fusion.refs_0_ = bf16[1,10,32,1024]{3,2,1,0:T(8,128)(2,1)S(1)} fusion(bf16[1,4,10,32,1024]{4,3,2,1,0:T(8,128)(2,1)} %param.8, s32[]{:T(128)S(6)} %select_n.137), kind=kLoop, calls=%fused_computation.1 | loop fusion | bytes 1310724 | tf_op jit(solution)/shard_map/dynamic_slice | solution.py:588
  27.1 0.6 collective-permute-start.3
  27.7 1.3 %collective-permute-start.4 = (bf16[1,10,32,1024]{3,2,1,0:T(8,128)(2,1)S(1)}, bf16[1,10,32,1024]{3,2,1,0:T(8,128)(2,1)S(1)}, u32[]{:S(2)}, u32[]{:S(2)}) collective-permute-start(bf16[1,10,32,1024]{3,2,1,0:T(8,128)(2,1)S(1)} %dynamic-slice_bitcast_fusion.refs_0_), channel_id=1, source_target_pairs={{0,64},{32,96},{64,0},{96,32},{128,192},{160,224},{192,128},{224,1... | collective-permute-start | bytes 1966088 | tf_op jit(solution)/shard_map/ppermute | solution.py:20
  29.1 0.2 fusion.1
  30.3 7.7 %first_substep.1 = (f32[3,10,8,32,128]{4,3,2,1,0:T(8,128)}, bf16[3,80,240]{2,1,0:T(8,128)(2,1)S(1)}) custom-call(s32[56]{0:T(128)S(1)} %pad_add_fusion.1.ints_ref, f32[122]{0:T(128)S(1)} %pad_maximum_fusion.vals_ref, bf16[4,10,32,1024]{3,2,1,0:T(8,128)(2,1)} %bitcast.47), custom_call_target="tpu_custom_call" | custom-call | tf_op jit(solution)/shard_map/first_substep/pallas_call | solution.py:299
  38.0 0.5 collective-permute-start.5
  38.5 0.5 slice.21
  40.0 13.0 %all-to-all-done.arr_ref = bf16[64,80,128]{2,1,0:T(8,128)(2,1)S(1)} async-done(((bf16[64,80,128]{2,1,0:T(8,128)(2,1)}), bf16[64,80,128]{2,1,0:T(8,128)(2,1)S(1)}, u32[]{:S(2)}, u32[]{:S(2)}) %all-to-all-start) | async-done | bytes 1310752 | tf_op jit(solution)/shard_map/all_to_all | solution.py:571
  53.0 0.6 gather_fusion
  53.7 1.7 %collective-permute-start.7 = (bf16[6,80,128]{2,1,0:T(8,128)(2,1)S(1)}, bf16[6,80,128]{2,1,0:T(8,128)(2,1)S(1)}, u32[]{:S(2)}, u32[]{:S(2)}) collective-permute-start(bf16[6,80,128]{2,1,0:T(8,128)(2,1)S(1)} %gather_fusion), channel_id=1, source_target_pairs={{0,64},{32,96},{64,0},{96,32},{128,192},{160,224},{192,128},{224,1... | collective-permute-start | bytes 368648 | tf_op jit(solution)/shard_map/ppermute | solution.py:20
  55.3 2.9 %collective-permute-start.8 = (bf16[6,80,128]{2,1,0:T(8,128)(2,1)S(1)}, bf16[6,80,128]{2,1,0:T(8,128)(2,1)S(1)}, u32[]{:S(2)}, u32[]{:S(2)}) collective-permute-start(bf16[6,80,128]{2,1,0:T(8,128)(2,1)S(1)} %gather_fusion), channel_id=1, source_target_pairs={{0,128},{32,160},{64,192},{96,224},{128,0},{160,32},{192,64},{224,... | collective-permute-start | bytes 368648 | tf_op jit(solution)/shard_map/ppermute | solution.py:20
  58.2 16.6 %advance_stay.1.refs_8_ = bf16[4,10,32,1024]{3,2,1,0:T(8,128)(2,1)} custom-call(s32[56]{0:T(128)S(1)} %pad_add_fusion.1.ints_ref, f32[122]{0:T(128)S(1)} %pad_maximum_fusion.vals_ref, f32[3,10,8,32,128]{4,3,2,1,0:T(8,128)} %get-tuple-element.26.s_ref, bf16[3,80,240]{2,1,0:T(8,128)(2,1)S(1)} %get-tuple-element.27.rk_ref, ...), custom_call_target="tpu_custom_call" | custom-call | tf_op jit(solution)/shard_map/advance_stay/pallas_call | solution.py:442
  74.9 7.9 %advance_traded.1 = bf16[4,10,32,1024]{3,2,1,0:T(8,128)(2,1)} custom-call(s32[16]{0:T(128)S(1)} %concatenate.18.ints_ref, f32[113]{0:T(128)S(1)} %pad_maximum_fusion.1.vals_ref, bf16[1,10,32,1024]{3,2,1,0:T(8,128)(2,1)S(1)} %dynamic-slice_bitcast_fusion.refs_0_, ...), custom_call_target="tpu_custom_call", output_to_operand_aliasing={{}: (10, {})} | custom-call | tf_op jit(solution)/shard_map/advance_traded/pallas_call | solution.py:513
  (60 shorter events, 2.1 us)
Async XLA Ops:
  1.7 17.4 %copy-start.4 = (s32[1,128]{1,0:T(1,128)S(1)}, s32[1,128]{1,0:T(1,128)}, u32[]{:S(2)}) copy-start(s32[1,128]{1,0:T(1,128)} %param.9) | copy-start | bytes 1540
  1.7 17.5 %copy-start = (s32[1,128,6]{1,0,2:T(1,128)S(1)}, s32[1,128,6]{1,0,2:T(1,128)}, u32[]{:S(2)}) copy-start(s32[1,128,6]{1,0,2:T(1,128)} %param.13) | copy-start | bytes 9220
  1.7 19.1 %copy-start.3 = (bf16[1,4,3]{2,1,0:T(4,128)(2,1)S(1)}, bf16[1,4,3]{2,1,0:T(4,128)(2,1)}, u32[]{:S(2)}) copy-start(bf16[1,4,3]{2,1,0:T(4,128)(2,1)} %param.10) | copy-start | bytes 76
  7.8 21.3 %copy-start.1 = (f32[10,10]{1,0:T(8,128)S(1)}, f32[10,10]{1,0:T(8,128)}, u32[]{:S(2)}) copy-start(f32[10,10]{1,0:T(8,128)} %param.12) | copy-start | bytes 1204
  7.8 21.7 %copy-start.2 = (f32[10]{0:T(128)S(1)}, f32[10]{0:T(128)}, u32[]{:S(2)}) copy-start(f32[10]{0:T(128)} %param.11) | copy-start | bytes 124
  7.8 45.2 %all-to-all-start = ((bf16[64,80,128]{2,1,0:T(8,128)(2,1)}), bf16[64,80,128]{2,1,0:T(8,128)(2,1)S(1)}, u32[]{:S(2)}, u32[]{:S(2)}) async-start(bf16[64,80,128]{2,1,0:T(8,128)(2,1)} %pack_faces.1), calls=%async_computation | async-start | bytes 2621440 | tf_op jit(solution)/shard_map/all_to_all | solution.py:571
  22.0 15.9 %collective-permute-start = (bf16[16,128]{1,0:T(8,128)(2,1)S(1)}, bf16[16,128]{1,0:T(8,128)(2,1)S(1)}, u32[]{:S(2)}, u32[]{:S(2)}) collective-permute-start(bf16[16,128]{1,0:T(8,128)(2,1)S(1)} %broadcast_in_dim.47), channel_id=1, source_target_pairs={{0,128},{32,160},{64,192},{96,224},{128,0},{160,32},{192,64},{224,... | collective-permute-start | bytes 12296 | tf_op jit(solution)/shard_map/ppermute | solution.py:20
  25.3 13.2 %collective-permute-start.1 = (bf16[16,128]{1,0:T(8,128)(2,1)S(1)}, bf16[16,128]{1,0:T(8,128)(2,1)S(1)}, u32[]{:S(2)}, u32[]{:S(2)}) collective-permute-start(bf16[16,128]{1,0:T(8,128)(2,1)S(1)} %broadcast_in_dim.47), channel_id=1, source_target_pairs={{0,64},{32,96},{64,0},{96,32},{128,192},{160,224},{192,128},{224,1... | collective-permute-start | bytes 12296 | tf_op jit(solution)/shard_map/ppermute | solution.py:20
  25.9 12.5 %collective-permute-start.2 = (bf16[16,128]{1,0:T(8,128)(2,1)S(1)}, bf16[16,128]{1,0:T(8,128)(2,1)S(1)}, u32[]{:S(2)}, u32[]{:S(2)}) collective-permute-start(bf16[16,128]{1,0:T(8,128)(2,1)S(1)} %broadcast_in_dim.47), channel_id=1, source_target_pairs={{0,32},{32,0},{64,96},{96,64},{128,160},{160,128},{192,224},{224,1... | collective-permute-start | bytes 12296 | tf_op jit(solution)/shard_map/ppermute | solution.py:20
  27.1 28.2 %collective-permute-start.3 = (bf16[1,10,32,1024]{3,2,1,0:T(8,128)(2,1)S(1)}, bf16[1,10,32,1024]{3,2,1,0:T(8,128)(2,1)S(1)}, u32[]{:S(2)}, u32[]{:S(2)}) collective-permute-start(bf16[1,10,32,1024]{3,2,1,0:T(8,128)(2,1)S(1)} %dynamic-slice_bitcast_fusion.refs_0_), channel_id=1, source_target_pairs={{0,32},{32,0},{64,96},{96,64},{128,160},{160,128},{192,224},{224,1... | collective-permute-start | bytes 1966088 | tf_op jit(solution)/shard_map/ppermute | solution.py:20
  27.7 47.2 %collective-permute-start.4 = (bf16[1,10,32,1024]{3,2,1,0:T(8,128)(2,1)S(1)}, bf16[1,10,32,1024]{3,2,1,0:T(8,128)(2,1)S(1)}, u32[]{:S(2)}, u32[]{:S(2)}) collective-permute-start(bf16[1,10,32,1024]{3,2,1,0:T(8,128)(2,1)S(1)} %dynamic-slice_bitcast_fusion.refs_0_), channel_id=1, source_target_pairs={{0,64},{32,96},{64,0},{96,32},{128,192},{160,224},{192,128},{224,1... | collective-permute-start | bytes 1966088 | tf_op jit(solution)/shard_map/ppermute | solution.py:20
  38.0 36.9 %collective-permute-start.5 = (bf16[1,10,32,1024]{3,2,1,0:T(8,128)(2,1)S(1)}, bf16[1,10,32,1024]{3,2,1,0:T(8,128)(2,1)}, u32[]{:S(2)}, u32[]{:S(2)}) collective-permute-start(bf16[1,10,32,1024]{3,2,1,0:T(8,128)(2,1)S(1)} %dynamic-slice_bitcast_fusion.refs_0_), channel_id=1, source_target_pairs={{0,128},{32,160},{64,192},{96,224},{128,0},{160,32},{192,64},{224,... | collective-permute-start | bytes 1966088 | tf_op jit(solution)/shard_map/ppermute | solution.py:20
  53.6 21.3 %collective-permute-start.6 = (bf16[6,80,128]{2,1,0:T(8,128)(2,1)S(1)}, bf16[6,80,128]{2,1,0:T(8,128)(2,1)S(1)}, u32[]{:S(2)}, u32[]{:S(2)}) collective-permute-start(bf16[6,80,128]{2,1,0:T(8,128)(2,1)S(1)} %gather_fusion), channel_id=1, source_target_pairs={{0,32},{32,0},{64,96},{96,64},{128,160},{160,128},{192,224},{224,1... | collective-permute-start | bytes 368648 | tf_op jit(solution)/shard_map/ppermute | solution.py:20
  53.7 21.2 %collective-permute-start.7 = (bf16[6,80,128]{2,1,0:T(8,128)(2,1)S(1)}, bf16[6,80,128]{2,1,0:T(8,128)(2,1)S(1)}, u32[]{:S(2)}, u32[]{:S(2)}) collective-permute-start(bf16[6,80,128]{2,1,0:T(8,128)(2,1)S(1)} %gather_fusion), channel_id=1, source_target_pairs={{0,64},{32,96},{64,0},{96,32},{128,192},{160,224},{192,128},{224,1... | collective-permute-start | bytes 368648 | tf_op jit(solution)/shard_map/ppermute | solution.py:20
  55.3 19.6 %collective-permute-start.8 = (bf16[6,80,128]{2,1,0:T(8,128)(2,1)S(1)}, bf16[6,80,128]{2,1,0:T(8,128)(2,1)S(1)}, u32[]{:S(2)}, u32[]{:S(2)}) collective-permute-start(bf16[6,80,128]{2,1,0:T(8,128)(2,1)S(1)} %gather_fusion), channel_id=1, source_target_pairs={{0,128},{32,160},{64,192},{96,224},{128,0},{160,32},{192,64},{224,... | collective-permute-start | bytes 368648 | tf_op jit(solution)/shard_map/ppermute | solution.py:20
